TPU v7x, 32 devices: a whole 2x2x4 slice. The times are simulated.
32 devices in a mesh: rows: 8 (over z, y), rhs: 4 (over x, core).
Axes of the slice: x: 2, y: 2, z: 4, core: 2. Of those that a mesh axis runs over, the one named last changes fastest.
Arguments:
- right_sides: bfloat16 [65536, 1024], P(None, ('rows', 'rhs')), may hold values from -6 to 6
- col_panels: bfloat16 [2, 65536, 1024], P(None, ('rows', 'rhs')), may hold values from -0.1875 to 0.1875
- diag_inverses: bfloat16 [2, 1024, 1024], replicated, may hold values from -0.1875 to 0.1875
Outputs:
- current: float32 [65536, 1024], P(('rows', 'rhs'))
All inputs are finite; a program needn't handle non-finite values.
Results may differ from a plain program's by a relative error of at most 0.003.
Values may be sent and summed in bfloat16 or wider, within the bound.
No kernel may reach another device: no remote copies, remote signals or barrier semaphores. Data moves between devices by JAX's collectives and lax.ppermute only.
A program may use at most 128 MiB of HBM per device.

v0:
```python
import jax
import jax.numpy as jnp
from jax import lax
from jax.sharding import PartitionSpec as P


def spread(shard, axis, root):
    mine = lax.axis_index(axis) == root
    return lax.psum(jnp.where(mine, shard, jnp.zeros_like(shard)), axis)


def local(right_sides, col_panels, diag_inverses):
    panel_size = diag_inverses.shape[1]
    early_solved = None
    gathered = lax.all_to_all(right_sides, ("rows", "rhs"), split_axis=0, concat_axis=1, tiled=True)
    current = gathered.astype(jnp.float32)
    rows_dev = current.shape[0]
    panel_count = diag_inverses.shape[0]
    devices_all = lax.axis_size("rows") * lax.axis_size("rhs")
    position = lax.axis_index(("rows", "rhs"))
    global_rows = position * rows_dev + jnp.arange(rows_dev, dtype=jnp.int32)
    for panel_id in range(panel_count):
        owner_dev = panel_id * devices_all // panel_count
        first_row = owner_dev * rows_dev
        is_owner = position == owner_dev
        local_panel = current[:panel_size].astype(jnp.bfloat16)
        inverse_now = diag_inverses[panel_id]
        solved_here = lax.cond(
            is_owner,
            lambda: jnp.dot(inverse_now, local_panel, preferred_element_type=jnp.float32).astype(
                jnp.bfloat16
            ),
            lambda: jnp.zeros(local_panel.shape, jnp.bfloat16),
        )
        solved = spread(solved_here, ("rows", "rhs"), owner_dev)
        update_term = jnp.dot(col_panels[panel_id], solved, preferred_element_type=jnp.float32)
        trailing = (global_rows >= first_row + panel_size)[:, None]
        current = jnp.where(trailing, current - update_term, current)
        top_rows = jnp.where(is_owner, solved.astype(jnp.float32), current[:panel_size])
        current = jnp.concatenate([top_rows, current[panel_size:]], axis=0)
    return current


def solution(mesh):
    return jax.shard_map(
        local,
        mesh=mesh,
        in_specs=(P(None, ("rows", "rhs")), P(None, ("rows", "rhs"), None), P()),
        out_specs=P(("rows", "rhs"), None),
        check_vma=False,
    )
```

profile of v0, /device:TPU:21, one launch (start us, length us, event | category | flops | bytes accessed | tf_op | source)
XLA Modules:
  0.0 442.7 jit_solution(2553022597957633385)
XLA Ops:
  6.5 4.8 %copy.27 = bf16[4,32,8,2048]{3,2,0,1:T(8,128)(2,1)} copy(bf16[4,32,8,2048]{3,2,1,0:T(8,128)(2,1)} %bitcast.34) | data formatting | bytes 8388608 | tf_op jit(solution)/shard_map/all_to_all | solution.py:15
  11.3 6.3 %all-to-all-start = ((bf16[32,2048,32]{1,2,0:T(8,128)(2,1)}), bf16[32,2048,32]{1,2,0:T(8,128)(2,1)}, u32[]{:S(2)}, u32[]{:S(2)}) async-start(bf16[32,2048,32]{1,2,0:T(8,128)(2,1)} %bitcast.33), calls=%async_computation | async-start | bytes 8388608 | tf_op jit(solution)/shard_map/all_to_all | solution.py:15
  17.6 0.0 all-reduce.3.cloned.1.call-start
  17.6 90.0 %all-to-all-done = bf16[32,2048,32]{1,2,0:T(8,128)(2,1)} async-done(((bf16[32,2048,32]{1,2,0:T(8,128)(2,1)}), bf16[32,2048,32]{1,2,0:T(8,128)(2,1)}, u32[]{:S(2)}, u32[]{:S(2)}) %all-to-all-start) | async-done | bytes 4194336 | tf_op jit(solution)/shard_map/all_to_all | solution.py:15
  107.7 0.3 conditional.2
  107.7 0.3 broadcast.21.clone
  107.9 1.5 broadcast_select_fusion
  109.4 0.0 all-reduce.3.cloned.1.call-update
  109.4 0.0 all-reduce.5.cloned.1.call-start
  109.5 140.0 %all-reduce.3.cloned.1.call-done = bf16[1024,1024]{0,1:T(8,128)(2,1)} async-done(((bf16[1024,1024]{0,1:T(8,128)(2,1)}), bf16[1024,1024]{0,1:T(8,128)(2,1)}) %all-reduce.3.cloned.1.call-update) | async-done | bytes 2097168 | tf_op jit(solution)/shard_map/psum | solution.py:9
  249.5 0.0 copy-start
  249.5 8.7 %subtract_select_fusion.1 = f32[2048,1024]{0,1:T(8,128)S(1)} fusion(bf16[2048,1024]{0,1:T(8,128)(2,1)} %bitcast.9, bf16[1024,1024]{0,1:T(8,128)(2,1)} %all-reduce.3.cloned.1.call-done, bf16[2,2048,1024]{2,1,0:T(8,128)(2,1)} %param.8, pred[2048]{0:T(1024)(128)(4,1)S(1)} %fusion.17), kind=kOutput, calls=%fused_computation.9 | convolution fusion | flops 4301258752 | bytes 18876416 | tf_op jit(solution)/shard_map/dot_general | solution.py:36
  258.2 0.0 copy-done
  258.2 4.9 %fusion.18 = (bf16[1024,1024]{0,1:T(8,128)(2,1)}, f32[1024,1024]{0,1:T(8,128)}, f32[1024,1024]{0,1:T(8,128)}) fusion(f32[2048,1024]{0,1:T(8,128)S(1)} %subtract_select_fusion.1, bf16[1024,1024]{0,1:T(8,128)(2,1)S(1)} %copy-done, pred[]{:T(512)S(6)} %eq.9), kind=kLoop, calls=%fused_computation.23 | loop fusion | flops 3145728 | bytes 20971520 | tf_op jit(solution)/shard_map/convert_element_type | solution.py:26
  263.1 0.4 conditional.3
  263.1 0.3 broadcast.22.clone
  263.6 1.5 broadcast_select_fusion.1
  265.0 0.0 all-reduce.5.cloned.1.call-update
  265.1 139.7 %all-reduce.5.cloned.1.call-done = bf16[1024,1024]{0,1:T(8,128)(2,1)} async-done(((bf16[1024,1024]{0,1:T(8,128)(2,1)}), bf16[1024,1024]{0,1:T(8,128)(2,1)}) %all-reduce.5.cloned.1.call-update) | async-done | bytes 2097168 | tf_op jit(solution)/shard_map/psum | solution.py:9
  404.7 0.0 copy-start.1
  404.7 13.3 %subtract_select_fusion = f32[2048,1024]{0,1:T(8,128)} fusion(f32[1024,1024]{0,1:T(8,128)} %get-tuple-element.43, f32[1024,1024]{0,1:T(8,128)} %get-tuple-element.40, bf16[1024,1024]{0,1:T(8,128)(2,1)} %all-reduce.5.cloned.1.call-done, bf16[2,2048,1024]{2,1,0:T(8,128)(2,1)} %param.8, pred[2048]{0:T(1024)(128)(4,1)S(1)} %fusion.16), kind=kOutput, calls=%fused_computation.8 | convolution fusion | flops 4301258752 | bytes 23070720 | tf_op jit(solution)/shard_map/dot_general | solution.py:36
  418.0 0.0 copy-done.1
  418.0 4.7 %slice_select_fusion = (f32[1024,1024]{0,1:T(8,128)S(1)}, f32[1024,1024]{0,1:T(8,128)S(1)}) fusion(f32[2048,1024]{0,1:T(8,128)} %subtract_select_fusion, bf16[1024,1024]{0,1:T(8,128)(2,1)S(1)} %copy-done.1, pred[]{:T(512)S(6)} %eq.8), kind=kLoop, calls=%fused_computation.12 | loop fusion | flops 2097152 | bytes 18874368 | tf_op jit(solution)/shard_map/jit(_where)/select_n | solution.py:39
  422.8 3.8 pad_maximum_fusion
  426.6 9.2 %copy.19 = f32[2048,1024]{1,0:T(8,128)} copy(f32[2048,1024]{0,1:T(8,128)} %pad_maximum_fusion) | data formatting | bytes 16777216 | tf_op jit(solution)/shard_map/concatenate | solution.py:40
  (2 shorter events, 0.0 us)
Async XLA Ops:
  11.3 96.3 %all-to-all-start = ((bf16[32,2048,32]{1,2,0:T(8,128)(2,1)}), bf16[32,2048,32]{1,2,0:T(8,128)(2,1)}, u32[]{:S(2)}, u32[]{:S(2)}) async-start(bf16[32,2048,32]{1,2,0:T(8,128)(2,1)} %bitcast.33), calls=%async_computation | async-start | bytes 8388608 | tf_op jit(solution)/shard_map/all_to_all | solution.py:15
  17.6 231.9 %all-reduce.3.cloned.1.call-start = ((), (), s32[]{:S(2)}) async-start(), calls=%async_computation.1 | async-start | bytes 4194304 | tf_op jit(solution)/shard_map/psum | solution.py:9
  109.4 295.3 %all-reduce.5.cloned.1.call-start = ((), (), s32[]{:S(2)}) async-start(), calls=%async_computation.2 | async-start | bytes 4194304 | tf_op jit(solution)/shard_map/psum | solution.py:9
  249.5 8.8 %copy-start = (bf16[1024,1024]{0,1:T(8,128)(2,1)S(1)}, bf16[1024,1024]{0,1:T(8,128)(2,1)}, u32[]{:S(2)}) copy-start(bf16[1024,1024]{0,1:T(8,128)(2,1)} %all-reduce.3.cloned.1.call-done) | copy-start | bytes 6291460
  404.7 13.3 %copy-start.1 = (bf16[1024,1024]{0,1:T(8,128)(2,1)S(1)}, bf16[1024,1024]{0,1:T(8,128)(2,1)}, u32[]{:S(2)}) copy-start(bf16[1024,1024]{0,1:T(8,128)(2,1)} %all-reduce.5.cloned.1.call-done) | copy-start | bytes 6291460
Sparse Core Ops, SparseCore 0:
  109.5 139.9 all-reduce.2
  265.2 139.5 all-reduce.4
where the time goes:
time: 447 us; the launch traced here: 443 us
  waiting for transfers between devices  370 us (83%)
  matrix products  22 us (5%)
  other arithmetic  16.4 us (4%)
  local copies, waits for them, and re-layouts  14.5 us (3%)
  between operations  13.5 us (3%)
  starting transfers between devices  6.34 us (1%)
    psum x2, waiting for transfers between devices, spread(): return lax.psum(jnp.where(mine, shard, jnp.zeros_like(shard)), axis)  280 us
    all_to_all x1, waiting for transfers between devices, local(): lax.all_to_all(right_sides, ('rows', 'rhs'), split_axis=0, concat_axis=1,...  90 us
    dot_general x2, matrix products, local(): jnp.dot(col_panels[panel_id], solved, preferred_element_type=jnp.float32)  22 us
    concatenate x1, local copies, waits for them, and re-layouts, local(): current = jnp.concatenate([top_rows, current[panel_size:]], axis=0)  9.24 us
  transfers between devices with their start and end apart: 3, of which 3 were waited for; matrix products, arithmetic and copies ran while one was open for 0% of the time, Pallas kernels for 0%

commit v1 on v0

v1 whole, which is shorter than its diff:
```python
import jax
import jax.numpy as jnp
from jax import lax
from jax.experimental import pallas as pl
from jax.experimental.pallas import tpu as pltpu
from jax.sharding import PartitionSpec as P

AXES = ("rows", "rhs")
F32 = jnp.float32
BF16 = jnp.bfloat16


def swap(x, mask, n):
    return lax.ppermute(x, AXES, [(i, i ^ mask) for i in range(n)])


def scatter_block(block, owner, n, me):
    half = n // 2
    piece = block.shape[0] // half
    slots = block.reshape(half // 2, 2, piece, block.shape[1])
    odd = lax.ppermute(slots[:, 1], AXES, [(owner, owner + 1)])
    mine = jnp.where(me == owner, slots[:, 0], odd)
    got = mine[0]
    for t in range(1, half // 2):
        pairs = [(owner, owner + 2 * t), (owner + 1, owner + 1 + 2 * t)]
        here = lax.ppermute(mine[t], AXES, pairs)
        got = jnp.where(me // 2 == owner // 2 + t, here, got)
    return got


def update_kernel(pos_ref, a_ref, c_ref, s0_ref, s1_ref, o_ref, *, owner, panel_blocks):
    i = pl.program_id(0)
    pos = pos_ref[0]
    in_panel = i < panel_blocks
    top0 = jnp.logical_and(pos == 0, in_panel)
    top1 = jnp.logical_and(pos == owner, in_panel)
    tm = o_ref.shape[0]

    @pl.when(jnp.logical_not(jnp.logical_or(top0, top1)))
    def _():
        base = a_ref[...].astype(F32).T
        o_ref[...] = base - jnp.dot(c_ref[0], s0_ref[...], preferred_element_type=F32)

        @pl.when(pos >= owner)
        def _():
            o_ref[...] -= jnp.dot(c_ref[1], s1_ref[...], preferred_element_type=F32)

    start = pl.multiple_of(jnp.where(in_panel, i, 0) * tm, tm)

    @pl.when(top0)
    def _():
        o_ref[...] = s0_ref[pl.ds(start, tm), :].astype(F32)

    @pl.when(top1)
    def _():
        o_ref[...] = s1_ref[pl.ds(start, tm), :].astype(F32)


def update(pos, a_t, cols, s0, s1, owner):
    width, rows = a_t.shape
    nb = s0.shape[0]
    tm = 256
    return pl.pallas_call(
        lambda *refs: update_kernel(*refs, owner=owner, panel_blocks=nb // tm),
        out_shape=jax.ShapeDtypeStruct((rows, width), F32),
        grid_spec=pltpu.PrefetchScalarGridSpec(
            num_scalar_prefetch=1,
            grid=(rows // tm,),
            in_specs=[
                pl.BlockSpec((width, tm), lambda i, p: (0, i)),
                pl.BlockSpec((2, tm, nb), lambda i, p: (0, i, 0)),
                pl.BlockSpec((nb, width), lambda i, p: (0, 0)),
                pl.BlockSpec((nb, width), lambda i, p: (0, 0)),
            ],
            out_specs=pl.BlockSpec((tm, width), lambda i, p: (i, 0)),
        ),
        compiler_params=pltpu.CompilerParams(vmem_limit_bytes=60 << 20),
        cost_estimate=pl.CostEstimate(
            flops=4 * rows * width * nb, bytes_accessed=20 << 20, transcendentals=0
        ),
        name="update",
    )(pos, a_t, cols, s0, s1)


def local(right_sides, col_panels, diag_inverses):
    n = lax.axis_size("rows") * lax.axis_size("rhs")
    me = lax.axis_index(AXES)
    nb = diag_inverses.shape[1]
    total_rows, width = right_sides.shape
    half = n // 2
    owner = half
    x_t = right_sides.T
    pan = jnp.stack([x_t[:, :nb], x_t[:, total_rows // 2 : total_rows // 2 + nb]])
    other = swap(pan, half, n)
    low = jnp.where(me < half, pan, other)
    high = jnp.where(me < half, other, pan)
    piece = scatter_block(col_panels[0, :nb], owner, n, me)
    mine = jnp.concatenate([low[0], high[0], low[1], high[1], piece], axis=0)
    groups = [list(range(half)), list(range(half, n))]
    all_in = lax.all_gather(mine, AXES, axis=0, axis_index_groups=groups)

    a_t = lax.all_to_all(right_sides, AXES, split_axis=0, concat_axis=1, tiled=True).T

    def rows_of(at):
        return all_in[:, at : at + width].reshape(half * width, nb)

    rs0_t = jnp.concatenate([rows_of(0), rows_of(width)], axis=0)
    rs1_t = jnp.concatenate([rows_of(2 * width), rows_of(3 * width)], axis=0)
    block = all_in[:, 4 * width :].reshape(nb, nb)
    nt = (((1,), (1,)), ((), ()))
    s0 = lax.dot_general(diag_inverses[0], rs0_t, nt, preferred_element_type=F32).astype(BF16)
    k0 = jnp.dot(block, s0, preferred_element_type=F32)
    panel1 = (rs1_t.T.astype(F32) - k0).astype(BF16)
    s1 = jnp.dot(diag_inverses[1], panel1, preferred_element_type=F32).astype(BF16)
    return update(me.reshape(1).astype(jnp.int32), a_t, col_panels, s0, s1, owner)


def solution(mesh):
    return jax.shard_map(
        local,
        mesh=mesh,
        in_specs=(P(None, AXES), P(None, AXES, None), P()),
        out_specs=P(AXES, None),
        check_vma=False,
    )
```

time: 447 us -> 189 us (0.42)
  waiting for transfers between devices: 370 us -> 103 us
  starting transfers between devices: 6.34 us -> 25.6 us
  Pallas kernels: 0 us -> 16.4 us
  other arithmetic: 16.4 us -> 0.33 us
  matrix products: 22 us -> 12.3 us
    psum x2 -> x0, waiting for transfers between devices: 280 us -> none  [spread(): return lax.psum(jnp.where(mine, shard, jnp.zeros_like(shard)), axis)]
    all_gather x0 -> x1, waiting for transfers between devices: none -> 95.6 us  [local(): all_in = lax.all_gather(mine, AXES, axis=0, axis_index_groups=groups)]
    all_to_all x1, waiting for transfers between devices: 90 us -> 0.01 us  [local(): lax.all_to_all(right_sides, AXES, split_axis=0, concat_axis=1, tiled=True)]
    pallas_call x0 -> x1, Pallas kernels: none -> 16.4 us  [update(): pl.pallas_call(lambda *refs: update_kernel(*refs, owner=owner, panel_bloc...]
    all_to_all x1, starting transfers between devices: 6.26 us -> 19.5 us  [local(): lax.all_to_all(right_sides, AXES, split_axis=0, concat_axis=1, tiled=True)]
    dot_general x2, matrix products: 22 us -> 12.3 us  [the longest x1 8.54 us: local(): jnp.dot(diag_inverses[1], panel1, preferred_element_type=F32).astype(BF16)]
    concatenate x1 -> x0, local copies, waits for them, and re-layouts: 9.24 us -> none  [local(): current = jnp.concatenate([top_rows, current[panel_size:]], axis=0)]
    slice x0 -> x3, local copies, waits for them, and re-layouts: none -> 7.64 us  [the longest x1 4.03 us: rows_of(): return all_in[:, at:at + width].reshape(half * width, nb)]
  transfers between devices with their start and end apart: 3 -> 11, of which waited for: 3 -> 3; matrix products, arithmetic and copies ran while one was open for 0% -> 13% of each run, Pallas kernels for 0% -> 0%
where the time goes in v1:
time: 189 us; the launch traced here: 187 us
  waiting for transfers between devices  103 us (54%)
  starting transfers between devices  25.6 us (14%)
  Pallas kernels  16.4 us (9%)
  local copies, waits for them, and re-layouts  15.2 us (8%)
  between operations  13.6 us (7%)
  matrix products  12.3 us (7%)
    all_gather x1, waiting for transfers between devices, local(): all_in = lax.all_gather(mine, AXES, axis=0, axis_index_groups=groups)  95.6 us
    all_to_all x1, starting transfers between devices, local(): lax.all_to_all(right_sides, AXES, split_axis=0, concat_axis=1, tiled=True)  19.5 us
    pallas_call x1, Pallas kernels, update(): pl.pallas_call(lambda *refs: update_kernel(*refs, owner=owner, panel_bloc...  16.4 us
    dot_general x1, matrix products, local(): jnp.dot(diag_inverses[1], panel1, preferred_element_type=F32).astype(BF16)  8.54 us
    ppermute x7, starting transfers between devices, scatter_block(): here = lax.ppermute(mine[t], AXES, pairs)  5.29 us
    ppermute x1, waiting for transfers between devices, swap(): return lax.ppermute(x, AXES, [(i, i ^ mask) for i in range(n)])  5.21 us
    all_to_all x1, local copies, waits for them, and re-layouts, local(): lax.all_to_all(right_sides, AXES, split_axis=0, concat_axis=1, tiled=True)  4.79 us
    slice x1, local copies, waits for them, and re-layouts, rows_of(): return all_in[:, at:at + width].reshape(half * width, nb)  4.03 us
  transfers between devices with their start and end apart: 11, of which 3 were waited for; matrix products, arithmetic and copies ran while one was open for 13% of the time, Pallas kernels for 0%

profile of v1, /device:TPU:21, one launch (start us, length us, event | category | flops | bytes accessed | tf_op | source)
XLA Modules:
  0.0 186.6 jit_solution(14356861394178609052)
XLA Ops:
  6.5 1.8 slice.78
  8.3 1.1 slice_bitcast_fusion
  9.4 0.7 collective-permute-start.1
  10.1 0.9 slice_bitcast_fusion.15
  11.0 0.1 collective-permute-start
  11.1 5.2 %collective-permute-done = bf16[2,32,1024]{2,1,0:T(8,128)(2,1)S(1)} collective-permute-done((bf16[2,32,1024]{2,1,0:T(8,128)(2,1)S(1)}, bf16[2,32,1024]{2,1,0:T(8,128)(2,1)S(1)}, u32[]{:S(2)}, u32[]{:S(2)}) %collective-permute-start) | collective-permute-done | bytes 131104 | tf_op jit(solution)/shard_map/ppermute | solution.py:14
  16.4 0.1 fusion.25
  16.5 0.1 slice_bitcast_fusion.3
  16.6 0.7 collective-permute-start.8
  17.3 1.3 collective-permute-start.7
  18.6 0.7 collective-permute-start.6
  19.3 0.7 collective-permute-start.5
  20.0 0.7 collective-permute-start.4
  20.6 0.7 collective-permute-start.3
  21.3 2.3 %collective-permute-done.7 = bf16[64,1024]{1,0:T(8,128)(2,1)S(1)} collective-permute-done((bf16[64,1024]{1,0:T(8,128)(2,1)S(1)}, bf16[64,1024]{1,0:T(8,128)(2,1)S(1)}, u32[]{:S(2)}, u32[]{:S(2)}) %collective-permute-start.7) | collective-permute-done | bytes 131104 | tf_op jit(solution)/shard_map/ppermute | solution.py:26
  23.6 0.7 collective-permute-start.2
  24.3 0.0 collective-permute-done.6
  24.3 0.0 collective-permute-done.3
  24.3 0.0 collective-permute-done.2
  24.3 0.2 fusion.33
  24.5 0.7 copy-done
  25.3 0.0 all-gather.3.cloned.1.call-update
  25.3 4.8 %copy.13 = bf16[4,32,8,2048]{3,2,0,1:T(8,128)(2,1)} copy(bf16[4,32,8,2048]{3,2,1,0:T(8,128)(2,1)} %bitcast.106) | data formatting | bytes 8388608 | tf_op jit(solution)/shard_map/all_to_all | solution.py:102
  30.1 19.5 %all-to-all-start = ((bf16[32,2048,32]{1,2,0:T(8,128)(2,1)}), bf16[32,2048,32]{1,2,0:T(8,128)(2,1)}, u32[]{:S(2)}, u32[]{:S(2)}) async-start(bf16[32,2048,32]{1,2,0:T(8,128)(2,1)} %bitcast.100), calls=%async_computation | async-start | bytes 8388608 | tf_op jit(solution)/shard_map/all_to_all | solution.py:102
  49.6 95.6 %all-gather.3.cloned.1.call-done = bf16[3072,1024]{1,0:T(8,128)(2,1)} async-done(((bf16[192,1024]{1,0:T(8,128)(2,1)}), bf16[3072,1024]{1,0:T(8,128)(2,1)}) %all-gather.3.cloned.1.call-update) | async-done | bytes 6291472 | tf_op jit(solution)/shard_map/all_gather | solution.py:100
  145.1 1.9 slice.116
  147.0 0.0 copy-start.1
  147.0 4.0 %fusion.40 = (bf16[16,32,1024]{2,1,0:T(8,128)(2,1)S(1)}, bf16[16,32,1024]{2,1,0:T(8,128)(2,1)}, bf16[16,32,1024]{2,1,0:T(8,128)(2,1)S(1)}, bf16[16,32,1024]{2,1,0:T(8,128)(2,1)S(1)}) fusion(bf16[16,192,1024]{2,1,0:T(8,128)(2,1)} %bitcast.104), kind=kLoop, calls=%fused_computation.52 | loop fusion | bytes 8388608 | tf_op jit(solution)/shard_map/slice | solution.py:105
  151.0 3.7 %fusion.14 = bf16[1024,1024]{0,1:T(8,128)(2,1)} fusion(bf16[2,1024,1024]{2,1,0:T(8,128)(2,1)S(1)} %copy-done.1, bf16[512,1024]{1,0:T(8,128)(2,1)S(1)} %bitcast.110, bf16[512,1024]{1,0:T(8,128)(2,1)S(1)} %bitcast.111), kind=kOutput, calls=%fused_computation.16 | convolution fusion | flops 2152726528 | bytes 6291456 | tf_op jit(solution)/shard_map/dot_general | solution.py:111
  154.7 8.5 %convert_bitcast_fusion.refs_4_ = bf16[1024,1024]{1,0:T(8,128)(2,1)} fusion(bf16[2,1024,1024]{2,1,0:T(8,128)(2,1)} %param.5, bf16[512,1024]{1,0:T(8,128)(2,1)} %bitcast.109, bf16[512,1024]{1,0:T(8,128)(2,1)S(1)} %bitcast.108, bf16[1024,1024]{1,0:T(8,128)(2,1)S(1)} %bitcast.107, bf16[1024,1024]{0,1:T(8,128)(2,1)} %fusion.14), kind=kOutput, calls=%fused_computation.13 | convolution fusion | flops 4302307328 | bytes 10485760 | tf_op jit(solution)/shard_map/dot_general | solution.py:114
  163.3 0.0 all-to-all-done
  163.3 16.4 %update.1 = f32[2048,1024]{1,0:T(8,128)} custom-call(s32[1]{0:T(128)} %bitcast.refs_0_, bf16[1024,2048]{1,0:T(8,128)(2,1)} %bitcast.3.refs_1_, bf16[2,2048,1024]{2,1,0:T(8,128)(2,1)} %refs_2_.1, bf16[1024,1024]{1,0:T(8,128)(2,1)} %bitcast.112, bf16[1024,1024]{1,0:T(8,128)(2,1)} %convert_bitcast_fusion.refs_4_), custom_call_target="tpu_custom_call" | custom-call | flops 8589934592 | bytes 20971520 | tf_op jit(solution)/shard_map/update/pallas_call | solution.py:63
  (13 shorter events, 0.1 us)
Async XLA Ops:
  6.5 138.6 %all-gather.3.cloned.1.call-start = ((), (), s32[]{:S(2)}) async-start(), calls=%async_computation.1 | async-start | bytes 6684672 | tf_op jit(solution)/shard_map/all_gather | solution.py:100
  9.4 7.0 %collective-permute-start.1 = (bf16[8,64,1024]{2,1,0:T(8,128)(2,1)}, bf16[8,64,1024]{2,1,0:T(8,128)(2,1)S(1)}, u32[]{:S(2)}, u32[]{:S(2)}) collective-permute-start(bf16[8,64,1024]{2,1,0:T(8,128)(2,1)} %slice_bitcast_fusion), channel_id=1, source_target_pairs={{16,17}} | collective-permute-start | bytes 3145736 | tf_op jit(solution)/shard_map/ppermute | solution.py:21
  11.0 5.3 %collective-permute-start = (bf16[2,32,1024]{2,1,0:T(8,128)(2,1)S(1)}, bf16[2,32,1024]{2,1,0:T(8,128)(2,1)S(1)}, u32[]{:S(2)}, u32[]{:S(2)}) collective-permute-start(bf16[2,32,1024]{2,1,0:T(8,128)(2,1)S(1)} %pad_maximum_fusion), channel_id=1, source_target_pairs={{0,16},{1,17},{2,18},{3,19},{4,20},{5,21},{6,22},{7,23},{8,24},{9,... | collective-permute-start | bytes 393224 | tf_op jit(solution)/shard_map/ppermute | solution.py:14
  16.6 4.0 %collective-permute-start.8 = (bf16[64,1024]{1,0:T(8,128)(2,1)S(1)}, bf16[64,1024]{1,0:T(8,128)(2,1)S(1)}, u32[]{:S(2)}, u32[]{:S(2)}) collective-permute-start(bf16[64,1024]{1,0:T(8,128)(2,1)S(1)} %get-tuple-element.11), channel_id=1, source_target_pairs={{16,18},{17,19}} | collective-permute-start | bytes 393224 | tf_op jit(solution)/shard_map/ppermute | solution.py:26
  17.3 6.3 %collective-permute-start.7 = (bf16[64,1024]{1,0:T(8,128)(2,1)S(1)}, bf16[64,1024]{1,0:T(8,128)(2,1)S(1)}, u32[]{:S(2)}, u32[]{:S(2)}) collective-permute-start(bf16[64,1024]{1,0:T(8,128)(2,1)S(1)} %get-tuple-element.12), channel_id=1, source_target_pairs={{16,20},{17,21}} | collective-permute-start | bytes 393224 | tf_op jit(solution)/shard_map/ppermute | solution.py:26
  18.6 5.7 %collective-permute-start.6 = (bf16[64,1024]{1,0:T(8,128)(2,1)S(1)}, bf16[64,1024]{1,0:T(8,128)(2,1)S(1)}, u32[]{:S(2)}, u32[]{:S(2)}) collective-permute-start(bf16[64,1024]{1,0:T(8,128)(2,1)S(1)} %get-tuple-element.13), channel_id=1, source_target_pairs={{16,22},{17,23}} | collective-permute-start | bytes 393224 | tf_op jit(solution)/shard_map/ppermute | solution.py:26
  19.3 5.0 %collective-permute-start.5 = (bf16[64,1024]{1,0:T(8,128)(2,1)S(1)}, bf16[64,1024]{1,0:T(8,128)(2,1)S(1)}, u32[]{:S(2)}, u32[]{:S(2)}) collective-permute-start(bf16[64,1024]{1,0:T(8,128)(2,1)S(1)} %get-tuple-element.14), channel_id=1, source_target_pairs={{16,24},{17,25}} | collective-permute-start | bytes 393224 | tf_op jit(solution)/shard_map/ppermute | solution.py:26
  20.0 4.3 %collective-permute-start.4 = (bf16[64,1024]{1,0:T(8,128)(2,1)S(1)}, bf16[64,1024]{1,0:T(8,128)(2,1)S(1)}, u32[]{:S(2)}, u32[]{:S(2)}) collective-permute-start(bf16[64,1024]{1,0:T(8,128)(2,1)S(1)} %get-tuple-element.15), channel_id=1, source_target_pairs={{16,26},{17,27}} | collective-permute-start | bytes 393224 | tf_op jit(solution)/shard_map/ppermute | solution.py:26
  20.6 3.7 %collective-permute-start.3 = (bf16[64,1024]{1,0:T(8,128)(2,1)S(1)}, bf16[64,1024]{1,0:T(8,128)(2,1)S(1)}, u32[]{:S(2)}, u32[]{:S(2)}) collective-permute-start(bf16[64,1024]{1,0:T(8,128)(2,1)S(1)} %get-tuple-element.16), channel_id=1, source_target_pairs={{16,28},{17,29}} | collective-permute-start | bytes 393224 | tf_op jit(solution)/shard_map/ppermute | solution.py:26
  23.6 0.7 collective-permute-start.2
  24.5 0.8 copy-start
  30.1 133.2 %all-to-all-start = ((bf16[32,2048,32]{1,2,0:T(8,128)(2,1)}), bf16[32,2048,32]{1,2,0:T(8,128)(2,1)}, u32[]{:S(2)}, u32[]{:S(2)}) async-start(bf16[32,2048,32]{1,2,0:T(8,128)(2,1)} %bitcast.100), calls=%async_computation | async-start | bytes 8388608 | tf_op jit(solution)/shard_map/all_to_all | solution.py:102
  147.0 4.0 %copy-start.1 = (bf16[2,1024,1024]{2,1,0:T(8,128)(2,1)S(1)}, bf16[2,1024,1024]{2,1,0:T(8,128)(2,1)}, u32[]{:S(2)}) copy-start(bf16[2,1024,1024]{2,1,0:T(8,128)(2,1)} %param.5) | copy-start | bytes 12582916
Sparse Core Ops, SparseCore 0:
  25.4 119.6 all-gather.2

commit v2 on v0

v2 whole, which is shorter than its diff:
```python
import jax
import jax.numpy as jnp
from jax import lax
from jax.experimental import pallas as pl
from jax.experimental.pallas import tpu as pltpu
from jax.sharding import PartitionSpec as P

AXES = ("rows", "rhs")
F32 = jnp.float32
BF16 = jnp.bfloat16
LANES = 128
NT = (((1,), (1,)), ((), ()))
LIMIT = pltpu.CompilerParams(vmem_limit_bytes=58 << 20)
FREE = pl.CostEstimate(flops=0, bytes_accessed=0, transcendentals=0)
ANY = pl.BlockSpec(memory_space=pl.ANY)


def send(x, pairs):
    return lax.ppermute(x, AXES, pairs)


def after(value, *tokens):
    return lax.optimization_barrier((value, *tokens))[0]


def cut(pos, x_t, masks, rows, *tokens):
    width = x_t.shape[0]
    count = len(masks)

    def kernel(pos_ref, *refs):
        for src, dst in zip(refs[:count], refs[-count:]):
            dst[...] = src[...]

    def spec(mask):
        return pl.BlockSpec((width, rows), lambda i, p: (0, p[0] ^ mask))

    whole = pl.BlockSpec((width, rows), lambda i, p: (0, 0))
    return pl.pallas_call(
        kernel,
        out_shape=[jax.ShapeDtypeStruct((width, rows), x_t.dtype)] * count,
        grid_spec=pltpu.PrefetchScalarGridSpec(
            num_scalar_prefetch=1,
            grid=(1,),
            in_specs=[spec(m) for m in masks] + [ANY] * len(tokens),
            out_specs=[whole] * count,
        ),
        compiler_params=LIMIT,
        cost_estimate=FREE,
        name="cut",
    )(pos, *[x_t] * count, *tokens)


def held_rows(tm, pos, i, owner, panel_rows):
    in_panel = i * tm < panel_rows
    return jnp.logical_and(in_panel, jnp.logical_or(pos == 0, pos == owner))


def solve_update(pos, rs0, rs1, block, diag, cols, owner, half, offs0, offs1, offs2):
    rows, nb = cols.shape[1:]
    width = rs0[0].shape[1]
    members = width * len(offs0)
    tm = 256
    wide = BF16 if width % 16 == 0 else F32

    def gather(dst, pair, offs, wrap):
        height = pair[0].shape[1]
        count = pair[0].shape[0]
        for j, off in enumerate(offs):
            ref = pair[j // count]
            at = pl.multiple_of(((wrap ^ off) & (len(offs) - 1)) * height, height)
            dst[pl.ds(at, height), :] = ref[j % count].astype(dst.dtype)

    def dot_nt(a, b):
        return lax.dot_general(a.astype(BF16), b, NT, preferred_element_type=F32)

    def kernel(pos_ref, a0, b0, a1, b1, a2, b2, d_ref, c_ref, o_ref, g0, g1, g2, s0, s1):
        i = pl.program_id(0)
        pos = pos_ref[0]
        upper = pos >= owner
        chunk = 256

        @pl.when(i == 0)
        def _():
            gather(g0, (a0, b0), offs0, pos)

            @pl.loop(0, members // chunk)
            def _(t):
                at = pl.ds(pl.multiple_of(t * chunk, chunk), chunk)
                s0[at, :] = dot_nt(g0[at, :], d_ref[0]).astype(BF16)

            @pl.when(upper)
            def _():
                gather(g1, (a1, b1), offs1, pos)
                gather(g2, (a2, b2), offs2, pos)

                @pl.loop(0, members // chunk)
                def _(t):
                    at = pl.ds(pl.multiple_of(t * chunk, chunk), chunk)
                    panel = g1[at, :].astype(F32) - dot_nt(s0[at, :], g2[...])
                    s1[at, :] = dot_nt(panel, d_ref[1]).astype(BF16)

        held = held_rows(tm, pos, i, owner, nb)
        start = pl.multiple_of(jnp.where(held, i, 0) * tm, tm)

        @pl.when(jnp.logical_not(held))
        def _():
            o_ref[...] = -dot_nt(c_ref[0], s0[...])

            @pl.when(upper)
            def _():
                o_ref[...] -= dot_nt(c_ref[1], s1[...])

        @pl.when(jnp.logical_and(held, pos == 0))
        def _():
            o_ref[...] = s0[:, pl.ds(start, tm)].astype(F32).T

        @pl.when(jnp.logical_and(held, pos == owner))
        def _():
            o_ref[...] = s1[:, pl.ds(start, tm)].astype(F32).T

    def full(x):
        zeros = (0,) * x.ndim
        return pl.BlockSpec(x.shape, lambda i, p: zeros)

    ins = [*rs0, *rs1, *block, diag]
    return pl.pallas_call(
        kernel,
        out_shape=jax.ShapeDtypeStruct((rows, members), F32),
        grid_spec=pltpu.PrefetchScalarGridSpec(
            num_scalar_prefetch=1,
            grid=(rows // tm,),
            in_specs=[full(x) for x in ins] + [pl.BlockSpec((2, tm, nb), lambda i, p: (0, i, 0))],
            out_specs=pl.BlockSpec((tm, members), lambda i, p: (i, 0)),
            scratch_shapes=[
                pltpu.VMEM((members, nb), wide),
                pltpu.VMEM((members, nb), wide),
                pltpu.VMEM((nb, nb), BF16),
                pltpu.VMEM((members, nb), BF16),
                pltpu.VMEM((members, nb), BF16),
            ],
        ),
        compiler_params=LIMIT,
        cost_estimate=FREE,
        name="solve_update",
    )(pos, *ins, cols)


def add_own(pos, v, own, owner, nb, half):
    rows = v.shape[0]
    width = own.shape[1]
    per = LANES // width
    tm = 1024

    def kernel(pos_ref, v_ref, a_ref, o_ref):
        held = held_rows(tm, pos_ref[0], pl.program_id(1), owner, nb)
        turned = a_ref[...].astype(F32).reshape(LANES, tm).T
        o_ref[...] = v_ref[...] + jnp.where(held, 0.0, turned)

    groups = half // per

    def place(j, i, p):
        return (i, jnp.where(p[0] < half, j, j + groups))

    return pl.pallas_call(
        kernel,
        out_shape=jax.ShapeDtypeStruct(v.shape, F32),
        grid_spec=pltpu.PrefetchScalarGridSpec(
            num_scalar_prefetch=1,
            grid=(groups, rows // tm),
            in_specs=[
                pl.BlockSpec((tm, LANES), place),
                pl.BlockSpec((per, width, tm), lambda j, i, p: (j, 0, i)),
            ],
            out_specs=pl.BlockSpec((tm, LANES), place),
        ),
        input_output_aliases={1: 0},
        compiler_params=LIMIT,
        cost_estimate=FREE,
        name="add_own",
    )(pos, v, own)


def add_group(pos, v, parts, masks, owner, nb):
    rows = v.shape[0]
    width = parts[0].shape[0]
    per = len(masks)
    tm = 1024

    def kernel(pos_ref, v_ref, *refs):
        o_ref, turn = refs[per:]
        pos = pos_ref[0]
        held = held_rows(tm, pos, pl.program_id(0), owner, nb)
        for ref, mask in zip(refs[:per], masks):
            at = ((pos ^ mask) & (per - 1)) * width
            turn[pl.ds(pl.multiple_of(at, 8), width), :] = ref[...].astype(F32)
        o_ref[...] = v_ref[...] + jnp.where(held, 0.0, turn[...].T)

    def place(i, p):
        return (i, (p[0] ^ masks[0]) // per)

    return pl.pallas_call(
        kernel,
        out_shape=jax.ShapeDtypeStruct(v.shape, F32),
        grid_spec=pltpu.PrefetchScalarGridSpec(
            num_scalar_prefetch=1,
            grid=(rows // tm,),
            in_specs=[pl.BlockSpec((tm, LANES), place)]
            + [pl.BlockSpec((width, tm), lambda i, p: (0, i))] * per,
            out_specs=pl.BlockSpec((tm, LANES), place),
            scratch_shapes=[pltpu.VMEM((LANES, tm), F32)],
        ),
        input_output_aliases={1: 0},
        compiler_params=LIMIT,
        cost_estimate=FREE,
        name="add_group",
    )(pos, v, *parts)


def local(right_sides, col_panels, diag_inverses):
    n = lax.axis_size("rows") * lax.axis_size("rhs")
    me = lax.axis_index(AXES).astype(jnp.int32)
    pos = me.reshape(1)
    nb = diag_inverses.shape[1]
    total_rows, width = right_sides.shape
    rows = total_rows // n
    half = n // 2
    owner = half
    per = LANES // width
    x_t = right_sides.T

    def every(mask):
        return [(i, i ^ mask) for i in range(n)]

    def upper(mask):
        return [(i, i ^ mask) for i in range(half, n)]

    big = {}

    def launch(masks, *tokens):
        for m, piece in zip(masks, cut(pos, x_t, masks, rows, *tokens)):
            big[m] = send(piece, every(m))
        return [big[m] for m in masks]

    inner = [1 << k for k in range(1, half.bit_length() - 1)][::-1]
    steps = len(inner)
    turn = [inner[t % steps :] + inner[: t % steps] + [1] for t in range(3)]
    todo = list(range(half, n))

    class Chain:
        def __init__(self, cur, offs, pairs, bits):
            self.cur, self.offs, self.pairs, self.bits = cur, offs, pairs, bits
            self.last = []

        def step(self, with_big):
            bit = self.bits.pop(0)
            cur = after(self.cur, *self.last) if self.last else self.cur
            if with_big:
                self.last = launch([todo.pop(0)], *self.last)
            got = send(cur, self.pairs(bit))
            self.offs = self.offs + [o ^ bit for o in self.offs]
            self.pair = (cur, got)
            if self.bits:
                self.cur = jnp.concatenate([cur, got], axis=0)

    own0 = x_t[:, :nb][None]
    own1 = x_t[:, total_rows // 2 : total_rows // 2 + nb][None]
    c0 = Chain(own0, [0], every, [half] + turn[0])
    c1 = Chain(own1, [0], lambda m: upper(m) if m < half else [(i, i + half) for i in range(half)], [half] + turn[1])

    piece = nb // half
    slots = col_panels[0, :nb].reshape(half // 2, 2, piece, nb)
    odd = send(slots[:, 1], [(owner, owner + 1)])
    c0.step(True)
    c1.step(True)
    mine = jnp.where(me == owner, slots[:, 0], odd)
    got = mine[0]
    for t in range(1, half // 2):
        here = send(mine[t], [(owner, owner + 2 * t), (owner + 1, owner + 1 + 2 * t)])
        got = jnp.where(me // 2 == owner // 2 + t, here, got)
    c2 = Chain(got[None], [0], upper, list(turn[2]))
    for step in range(steps + 1):
        c0.step(True)
        c1.step(True)
        c2.step(False)

    ends = [c0.pair[1], c1.pair[1], c2.pair[1]]
    first = jnp.where(after(me, *ends) < half, 0, half * rows)
    own_rows = lax.dynamic_slice_in_dim(right_sides, first, half * rows, 0)
    halves = [list(range(half)), list(range(half, n))]
    own = lax.all_to_all(
        own_rows, AXES, split_axis=0, concat_axis=1, axis_index_groups=halves, tiled=True
    ).T.reshape(half, width, rows)
    tokens = c0.last + c1.last
    while todo:
        now, todo = todo[:3], todo[3:]
        tokens = launch(now, *tokens)

    v = solve_update(
        pos, c0.pair, c1.pair, c2.pair, diag_inverses, col_panels,
        owner, half, c0.offs, c1.offs, c2.offs,
    )
    v = add_own(pos, v, own, owner, nb, half)
    for m in range(half, n, per):
        masks = list(range(m, m + per))
        v = add_group(pos, v, [big[k] for k in masks], masks, owner, nb)
    return v


def solution(mesh):
    return jax.shard_map(
        local,
        mesh=mesh,
        in_specs=(P(None, AXES), P(None, AXES, None), P()),
        out_specs=P(AXES, None),
        check_vma=False,
    )
```

time: 447 us -> 236 us (0.53)
  waiting for transfers between devices: 370 us -> 42.9 us
  starting transfers between devices: 6.34 us -> 111 us
  Pallas kernels: 0 us -> 62.8 us
  matrix products: 22 us -> 0 us
  between operations: 13.5 us -> 0.58 us
  other arithmetic: 16.4 us -> 4.58 us
    psum x2 -> x0, waiting for transfers between devices: 280 us -> none  [spread(): return lax.psum(jnp.where(mine, shard, jnp.zeros_like(shard)), axis)]
    ppermute x0 -> x38, starting transfers between devices: none -> 99.7 us  [send(): return lax.ppermute(x, AXES, pairs)]
    all_to_all x1, waiting for transfers between devices: 90 us -> 0.01 us  [local(): lax.all_to_all(own_rows, AXES, split_axis=0, concat_axis=1, axis_index_gr...]
    pallas_call x0 -> x18, Pallas kernels: none -> 62.8 us  [the longest x1 26.3 us: solve_update(): pl.pallas_call(kernel, out_shape=jax.ShapeDtypeStruct((rows, members), F3...]
    ppermute x0 -> x38, waiting for transfers between devices: none -> 42.9 us  [send(): return lax.ppermute(x, AXES, pairs)]
    dot_general x2 -> x0, matrix products: 22 us -> none  [local(): jnp.dot(col_panels[panel_id], solved, preferred_element_type=jnp.float32)]
    concatenate x1 -> x0, local copies, waits for them, and re-layouts: 9.24 us -> none  [local(): current = jnp.concatenate([top_rows, current[panel_size:]], axis=0)]
    select_n x3 -> x1, other arithmetic: 7.66 us -> 1.34 us  [local(): mine = jnp.where(me == owner, slots[:, 0], odd)]
  transfers between devices with their start and end apart: 3 -> 39, of which waited for: 3 -> 12; matrix products, arithmetic and copies ran while one was open for 0% -> 3% of each run, Pallas kernels for 0% -> 26%
where the time goes in v2:
time: 236 us; the launch traced here: 235 us
  starting transfers between devices  111 us (47%)
  Pallas kernels  62.8 us (27%)
  waiting for transfers between devices  42.9 us (18%)
  local copies, waits for them, and re-layouts  13 us (6%)
  other arithmetic  4.58 us (2%)
    ppermute x38, starting transfers between devices, send(): return lax.ppermute(x, AXES, pairs)  99.7 us
    ppermute x38, waiting for transfers between devices, send(): return lax.ppermute(x, AXES, pairs)  42.9 us
    pallas_call x1, Pallas kernels, solve_update(): pl.pallas_call(kernel, out_shape=jax.ShapeDtypeStruct((rows, members), F3...  26.3 us
    pallas_call x12, Pallas kernels, cut(): pl.pallas_call(kernel, out_shape=[jax.ShapeDtypeStruct((width, rows), x_t...  19.3 us
    all_to_all x1, starting transfers between devices, local(): lax.all_to_all(own_rows, AXES, split_axis=0, concat_axis=1, axis_index_gr...  11 us
    pallas_call x4, Pallas kernels, add_group(): pl.pallas_call(kernel, out_shape=jax.ShapeDtypeStruct(v.shape, F32), grid...  9.88 us
    pallas_call x1, Pallas kernels, add_own(): pl.pallas_call(kernel, out_shape=jax.ShapeDtypeStruct(v.shape, F32), grid...  7.34 us
    unnamed x48, local copies, waits for them, and re-layouts  5.99 us
  transfers between devices with their start and end apart: 39, of which 12 were waited for; matrix products, arithmetic and copies ran while one was open for 3% of the time, Pallas kernels for 26%

profile of v2, /device:TPU:21, one launch (start us, length us, event | category | flops | bytes accessed | tf_op | source)
XLA Modules:
  0.0 234.5 jit_solution(1252248897298848086)
XLA Ops:
  7.9 4.4 %collective-permute-start.10 = (bf16[32,2048]{1,0:T(8,128)(2,1)}, bf16[32,2048]{1,0:T(8,128)(2,1)S(1)}, u32[]{:S(2)}, u32[]{:S(2)}) collective-permute-start(bf16[32,2048]{1,0:T(8,128)(2,1)} %cut.16), channel_id=1, source_target_pairs={{0,17},{1,16},{2,19},{3,18},{4,21},{5,20},{6,23},{7,22},{8,25},{9,... | collective-permute-start | bytes 393224 | tf_op jit(solution)/shard_map/ppermute | solution.py:19
  13.9 2.4 %collective-permute-start = (bf16[1,32,1024]{2,1,0:T(8,128)(2,1)}, bf16[1,32,1024]{2,1,0:T(8,128)(2,1)}, u32[]{:S(2)}, u32[]{:S(2)}) collective-permute-start(bf16[1,32,1024]{2,1,0:T(8,128)(2,1)} %get-tuple-element.36), channel_id=1, source_target_pairs={{0,16},{1,17},{2,18},{3,19},{4,20},{5,21},{6,22},{7,23},{8,24},{9,... | collective-permute-start | bytes 196616 | tf_op jit(solution)/shard_map/ppermute | solution.py:19
  17.1 5.8 %collective-permute-done.10.refs_1_ = bf16[32,2048]{1,0:T(8,128)(2,1)S(1)} collective-permute-done((bf16[32,2048]{1,0:T(8,128)(2,1)}, bf16[32,2048]{1,0:T(8,128)(2,1)S(1)}, u32[]{:S(2)}, u32[]{:S(2)}) %collective-permute-start.10) | collective-permute-done | bytes 131104 | tf_op jit(solution)/shard_map/ppermute | solution.py:19
  23.0 2.8 %collective-permute-start.11 = (bf16[2,32,1024]{2,1,0:T(8,128)(2,1)S(1)}, bf16[2,32,1024]{2,1,0:T(8,128)(2,1)}, u32[]{:S(2)}, u32[]{:S(2)}) collective-permute-start(bf16[2,32,1024]{2,1,0:T(8,128)(2,1)S(1)} %pad_maximum_fusion.10), channel_id=1, source_target_pairs={{16,20},{17,21},{18,22},{19,23},{20,16},{21,17},{22,18},{23,19},{2... | collective-permute-start | bytes 393224 | tf_op jit(solution)/shard_map/ppermute | solution.py:19
  27.3 2.7 %collective-permute-start.12 = (bf16[32,2048]{1,0:T(8,128)(2,1)}, bf16[32,2048]{1,0:T(8,128)(2,1)S(1)}, u32[]{:S(2)}, u32[]{:S(2)}) collective-permute-start(bf16[32,2048]{1,0:T(8,128)(2,1)} %cut.17), channel_id=1, source_target_pairs={{0,19},{1,18},{2,17},{3,16},{4,23},{5,22},{6,21},{7,20},{8,27},{9,... | collective-permute-start | bytes 393224 | tf_op jit(solution)/shard_map/ppermute | solution.py:19
  40.4 7.3 %collective-permute-start.2 = (bf16[2,32,1024]{2,1,0:T(8,128)(2,1)S(1)}, bf16[2,32,1024]{2,1,0:T(8,128)(2,1)S(1)}, u32[]{:S(2)}, u32[]{:S(2)}) collective-permute-start(bf16[2,32,1024]{2,1,0:T(8,128)(2,1)S(1)} %pad_maximum_fusion.9), channel_id=1, source_target_pairs={{0,8},{1,9},{2,10},{3,11},{4,12},{5,13},{6,14},{7,15},{8,0},{9,1},... | collective-permute-start | bytes 393224 | tf_op jit(solution)/shard_map/ppermute | solution.py:19
  49.7 3.4 %collective-permute-start.26 = (bf16[1,64,1024]{2,1,0:T(8,128)(2,1)S(1)}, bf16[1,64,1024]{2,1,0:T(8,128)(2,1)S(1)}, u32[]{:S(2)}, u32[]{:S(2)}) collective-permute-start(bf16[1,64,1024]{2,1,0:T(8,128)(2,1)S(1)} %fusion.8), channel_id=1, source_target_pairs={{16,18},{17,19},{18,16},{19,17},{20,22},{21,23},{22,20},{23,21},{2... | collective-permute-start | bytes 393224 | tf_op jit(solution)/shard_map/ppermute | solution.py:19
  55.3 3.9 %collective-permute-start.14 = (bf16[32,2048]{1,0:T(8,128)(2,1)}, bf16[32,2048]{1,0:T(8,128)(2,1)S(1)}, u32[]{:S(2)}, u32[]{:S(2)}) collective-permute-start(bf16[32,2048]{1,0:T(8,128)(2,1)} %cut.18), channel_id=1, source_target_pairs={{0,21},{1,20},{2,23},{3,22},{4,17},{5,16},{6,19},{7,18},{8,29},{9,... | collective-permute-start | bytes 393224 | tf_op jit(solution)/shard_map/ppermute | solution.py:19
  59.2 3.1 %collective-permute-done.26 = bf16[1,64,1024]{2,1,0:T(8,128)(2,1)S(1)} collective-permute-done((bf16[1,64,1024]{2,1,0:T(8,128)(2,1)S(1)}, bf16[1,64,1024]{2,1,0:T(8,128)(2,1)S(1)}, u32[]{:S(2)}, u32[]{:S(2)}) %collective-permute-start.26) | collective-permute-done | bytes 131104 | tf_op jit(solution)/shard_map/ppermute | solution.py:19
  62.3 2.0 collective-permute-start.27
  65.1 5.2 %collective-permute-start.15 = (bf16[8,32,1024]{2,1,0:T(8,128)(2,1)S(1)}, bf16[8,32,1024]{2,1,0:T(8,128)(2,1)S(1)}, u32[]{:S(2)}, u32[]{:S(2)}) collective-permute-start(bf16[8,32,1024]{2,1,0:T(8,128)(2,1)S(1)} %pad_maximum_fusion.4), channel_id=1, source_target_pairs={{16,24},{17,25},{18,26},{19,27},{20,28},{21,29},{22,30},{23,31},{2... | collective-permute-start | bytes 1572872 | tf_op jit(solution)/shard_map/ppermute | solution.py:19
  72.0 6.3 %collective-permute-done.5.refs_1_.refs_0_ = bf16[32,2048]{1,0:T(8,128)(2,1)S(1)} collective-permute-done((bf16[32,2048]{1,0:T(8,128)(2,1)}, bf16[32,2048]{1,0:T(8,128)(2,1)S(1)}, u32[]{:S(2)}, u32[]{:S(2)}) %collective-permute-start.5) | collective-permute-done | bytes 131104 | tf_op jit(solution)/shard_map/ppermute | solution.py:19
  78.3 1.9 collective-permute-start.28
  85.1 5.3 %collective-permute-start.7 = (bf16[32,2048]{1,0:T(8,128)(2,1)}, bf16[32,2048]{1,0:T(8,128)(2,1)S(1)}, u32[]{:S(2)}, u32[]{:S(2)}) collective-permute-start(bf16[32,2048]{1,0:T(8,128)(2,1)} %cut.15), channel_id=1, source_target_pairs={{0,22},{1,23},{2,20},{3,21},{4,18},{5,19},{6,16},{7,17},{8,30},{9,... | collective-permute-start | bytes 393224 | tf_op jit(solution)/shard_map/ppermute | solution.py:19
  90.5 3.6 %collective-permute-start.17 = (bf16[16,32,1024]{2,1,0:T(8,128)(2,1)S(1)}, bf16[16,32,1024]{2,1,0:T(8,128)(2,1)S(1)}, u32[]{:S(2)}, u32[]{:S(2)}) collective-permute-start(bf16[16,32,1024]{2,1,0:T(8,128)(2,1)S(1)} %pad_maximum_fusion.1.a1), channel_id=1, source_target_pairs={{16,17},{17,16},{18,19},{19,18},{20,21},{21,20},{22,23},{23,22},{2... | collective-permute-start | bytes 3145736 | tf_op jit(solution)/shard_map/ppermute | solution.py:19
  95.7 2.7 %collective-permute-start.8 = (bf16[16,32,1024]{2,1,0:T(8,128)(2,1)S(1)}, bf16[16,32,1024]{2,1,0:T(8,128)(2,1)S(1)}, u32[]{:S(2)}, u32[]{:S(2)}) collective-permute-start(bf16[16,32,1024]{2,1,0:T(8,128)(2,1)S(1)} %pad_maximum_fusion.a0), channel_id=1, source_target_pairs={{0,1},{1,0},{2,3},{3,2},{4,5},{5,4},{6,7},{7,6},{8,9},{9,8},{10,11... | collective-permute-start | bytes 3145736 | tf_op jit(solution)/shard_map/ppermute | solution.py:19
  98.5 3.7 %collective-permute-start.29 = (bf16[8,64,1024]{2,1,0:T(8,128)(2,1)S(1)}, bf16[8,64,1024]{2,1,0:T(8,128)(2,1)S(1)}, u32[]{:S(2)}, u32[]{:S(2)}) collective-permute-start(bf16[8,64,1024]{2,1,0:T(8,128)(2,1)S(1)} %pad_maximum_fusion.2.a2), channel_id=1, source_target_pairs={{16,17},{17,16},{18,19},{19,18},{20,21},{21,20},{22,23},{23,22},{2... | collective-permute-start | bytes 3145736 | tf_op jit(solution)/shard_map/ppermute | solution.py:19
  104.4 2.1 constant_dynamic-slice_fusion
  108.0 11.0 %all-to-all-start = ((bf16[16,2048,32]{1,2,0:T(8,128)(2,1)}), bf16[16,2048,32]{1,2,0:T(8,128)(2,1)S(1)}, u32[]{:S(2)}, u32[]{:S(2)}) async-start(bf16[16,2048,32]{1,2,0:T(8,128)(2,1)} %bitcast.61), calls=%async_computation | async-start | bytes 4194304 | tf_op jit(solution)/shard_map/all_to_all | solution.py:290
  122.2 2.0 collective-permute-start.31
  125.6 3.6 %collective-permute-done.31.refs_4_.refs_1_ = bf16[32,2048]{1,0:T(8,128)(2,1)S(1)} collective-permute-done((bf16[32,2048]{1,0:T(8,128)(2,1)}, bf16[32,2048]{1,0:T(8,128)(2,1)S(1)}, u32[]{:S(2)}, u32[]{:S(2)}) %collective-permute-start.31) | collective-permute-done | bytes 131104 | tf_op jit(solution)/shard_map/ppermute | solution.py:19
  134.5 3.9 %collective-permute-done.32.refs_2_.refs_3_ = bf16[32,2048]{1,0:T(8,128)(2,1)S(1)} collective-permute-done((bf16[32,2048]{1,0:T(8,128)(2,1)}, bf16[32,2048]{1,0:T(8,128)(2,1)S(1)}, u32[]{:S(2)}, u32[]{:S(2)}) %collective-permute-start.32) | collective-permute-done | bytes 131104 | tf_op jit(solution)/shard_map/ppermute | solution.py:19
  138.3 5.4 %collective-permute-done.33.refs_3_.refs_4_ = bf16[32,2048]{1,0:T(8,128)(2,1)S(1)} collective-permute-done((bf16[32,2048]{1,0:T(8,128)(2,1)}, bf16[32,2048]{1,0:T(8,128)(2,1)S(1)}, u32[]{:S(2)}, u32[]{:S(2)}) %collective-permute-start.33) | collective-permute-done | bytes 131104 | tf_op jit(solution)/shard_map/ppermute | solution.py:19
  143.8 10.5 %collective-permute-done.34.refs_5_.refs_0_ = bf16[32,2048]{1,0:T(8,128)(2,1)S(1)} collective-permute-done((bf16[32,2048]{1,0:T(8,128)(2,1)}, bf16[32,2048]{1,0:T(8,128)(2,1)S(1)}, u32[]{:S(2)}, u32[]{:S(2)}) %collective-permute-start.34) | collective-permute-done | bytes 131104 | tf_op jit(solution)/shard_map/ppermute | solution.py:19
  156.7 25.8 %collective-permute-start.36 = (bf16[32,2048]{1,0:T(8,128)(2,1)}, bf16[32,2048]{1,0:T(8,128)(2,1)S(1)}, u32[]{:S(2)}, u32[]{:S(2)}) collective-permute-start(bf16[32,2048]{1,0:T(8,128)(2,1)} %get-tuple-element.33), channel_id=1, source_target_pairs={{0,30},{1,31},{2,28},{3,29},{4,26},{5,27},{6,24},{7,25},{8,22},{9,... | collective-permute-start | bytes 393224 | tf_op jit(solution)/shard_map/ppermute | solution.py:19
  182.6 5.7 %collective-permute-start.37 = (bf16[32,2048]{1,0:T(8,128)(2,1)}, bf16[32,2048]{1,0:T(8,128)(2,1)S(1)}, u32[]{:S(2)}, u32[]{:S(2)}) collective-permute-start(bf16[32,2048]{1,0:T(8,128)(2,1)} %get-tuple-element.34), channel_id=1, source_target_pairs={{0,31},{1,30},{2,29},{3,28},{4,27},{5,26},{6,25},{7,24},{8,23},{9,... | collective-permute-start | bytes 393224 | tf_op jit(solution)/shard_map/ppermute | solution.py:19
  188.3 26.3 %solve_update.1.v_ref = f32[2048,1024]{1,0:T(8,128)} custom-call(s32[1]{0:T(128)} %bitcast.pos_ref, bf16[16,32,1024]{2,1,0:T(8,128)(2,1)} %copy-done.2, bf16[16,32,1024]{2,1,0:T(8,128)(2,1)} %copy-done.5, bf16[16,32,1024]{2,1,0:T(8,128)(2,1)} %copy-done.1, bf16[16,32,1024]{2,1,0:T(8,128)(2,1)} %copy-done.4, bf16[8,64,1024]{2,1,0:T(8,128)(2,1)} %copy-done.3, ...), custom_call_target="tpu_custom_call" | custom-call | tf_op jit(solution)/shard_map/solve_update/pallas_call | solution.py:126
  216.0 7.3 %add_own.1.v_ref = f32[2048,1024]{1,0:T(8,128)} custom-call(s32[1]{0:T(128)} %bitcast.pos_ref, f32[2048,1024]{1,0:T(8,128)} %solve_update.1.v_ref, bf16[16,32,2048]{2,1,0:T(8,128)(2,1)} %bitcast.82), custom_call_target="tpu_custom_call", output_to_operand_aliasing={{}: (1, {})} | custom-call | tf_op jit(solution)/shard_map/add_own/pallas_call | solution.py:164
  223.3 2.5 %add_group.4.v_ref = f32[2048,1024]{1,0:T(8,128)} custom-call(s32[1]{0:T(128)} %bitcast.pos_ref, f32[2048,1024]{1,0:T(8,128)} %add_own.1.v_ref, bf16[32,2048]{1,0:T(8,128)(2,1)} %copy-done.13, bf16[32,2048]{1,0:T(8,128)(2,1)} %copy-done.12, bf16[32,2048]{1,0:T(8,128)(2,1)} %copy-done.15, bf16[32,2048]{1,0:T(8,128)(2,1)} %copy-done.14), custom_call_target="tpu_custom_call", output_to_operand_aliasing={{}: (1, {})} | custom-call | tf_op jit(solution)/shard_map/add_group/pallas_call | solution.py:201
  225.8 2.5 %add_group.5.v_ref = f32[2048,1024]{1,0:T(8,128)} custom-call(s32[1]{0:T(128)} %bitcast.pos_ref, f32[2048,1024]{1,0:T(8,128)} %add_group.4.v_ref, bf16[32,2048]{1,0:T(8,128)(2,1)} %copy-done.17, bf16[32,2048]{1,0:T(8,128)(2,1)} %copy-done.16, bf16[32,2048]{1,0:T(8,128)(2,1)} %copy-done.19, bf16[32,2048]{1,0:T(8,128)(2,1)} %copy-done.18), custom_call_target="tpu_custom_call", output_to_operand_aliasing={{}: (1, {})} | custom-call | tf_op jit(solution)/shard_map/add_group/pallas_call | solution.py:201
  228.2 2.5 %add_group.6.v_ref = f32[2048,1024]{1,0:T(8,128)} custom-call(s32[1]{0:T(128)} %bitcast.pos_ref, f32[2048,1024]{1,0:T(8,128)} %add_group.5.v_ref, bf16[32,2048]{1,0:T(8,128)(2,1)} %copy-done.7, bf16[32,2048]{1,0:T(8,128)(2,1)} %copy-done.8, bf16[32,2048]{1,0:T(8,128)(2,1)} %copy-done.10, bf16[32,2048]{1,0:T(8,128)(2,1)} %copy-done.11), custom_call_target="tpu_custom_call", output_to_operand_aliasing={{}: (1, {})} | custom-call | tf_op jit(solution)/shard_map/add_group/pallas_call | solution.py:201
  232.1 2.5 %add_group.7 = f32[2048,1024]{1,0:T(8,128)} custom-call(s32[1]{0:T(128)} %bitcast.pos_ref, f32[2048,1024]{1,0:T(8,128)} %add_group.6.v_ref, bf16[32,2048]{1,0:T(8,128)(2,1)} %copy-done.9, bf16[32,2048]{1,0:T(8,128)(2,1)} %copy-done.21, bf16[32,2048]{1,0:T(8,128)(2,1)} %copy-done.22, bf16[32,2048]{1,0:T(8,128)(2,1)} %copy-done.23), custom_call_target="tpu_custom_call", output_to_operand_aliasing={{}: (1, {})} | custom-call | tf_op jit(solution)/shard_map/add_group/pallas_call | solution.py:201
  (131 shorter events, 53.8 us)
Async XLA Ops:
  1.8 28.2 %collective-permute-start.18 = (bf16[8,64,1024]{2,1,0:T(8,128)(2,1)S(1)}, bf16[8,64,1024]{2,1,0:T(8,128)(2,1)}, u32[]{:S(2)}, u32[]{:S(2)}) collective-permute-start(bf16[8,64,1024]{2,1,0:T(8,128)(2,1)S(1)} %slice_bitcast_fusion), channel_id=1, source_target_pairs={{16,17}} | collective-permute-start | bytes 3145736 | tf_op jit(solution)/shard_map/ppermute | solution.py:19
  5.0 11.2 %collective-permute-start.9 = (bf16[1,32,1024]{2,1,0:T(8,128)(2,1)S(1)}, bf16[1,32,1024]{2,1,0:T(8,128)(2,1)}, u32[]{:S(2)}, u32[]{:S(2)}) collective-permute-start(bf16[1,32,1024]{2,1,0:T(8,128)(2,1)S(1)} %get-tuple-element.35), channel_id=1, source_target_pairs={{0,16},{1,17},{2,18},{3,19},{4,20},{5,21},{6,22},{7,23},{8,24},{9,... | collective-permute-start | bytes 196616 | tf_op jit(solution)/shard_map/ppermute | solution.py:19
  7.9 15.1 %collective-permute-start.10 = (bf16[32,2048]{1,0:T(8,128)(2,1)}, bf16[32,2048]{1,0:T(8,128)(2,1)S(1)}, u32[]{:S(2)}, u32[]{:S(2)}) collective-permute-start(bf16[32,2048]{1,0:T(8,128)(2,1)} %cut.16), channel_id=1, source_target_pairs={{0,17},{1,16},{2,19},{3,18},{4,21},{5,20},{6,23},{7,22},{8,25},{9,... | collective-permute-start | bytes 393224 | tf_op jit(solution)/shard_map/ppermute | solution.py:19
  13.9 19.0 %collective-permute-start.1 = (bf16[32,2048]{1,0:T(8,128)(2,1)}, bf16[32,2048]{1,0:T(8,128)(2,1)S(1)}, u32[]{:S(2)}, u32[]{:S(2)}) collective-permute-start(bf16[32,2048]{1,0:T(8,128)(2,1)} %cut.12), channel_id=1, source_target_pairs={{0,16},{1,17},{2,18},{3,19},{4,20},{5,21},{6,22},{7,23},{8,24},{9,... | collective-permute-start | bytes 393224 | tf_op jit(solution)/shard_map/ppermute | solution.py:19
  13.9 18.3 %collective-permute-start = (bf16[1,32,1024]{2,1,0:T(8,128)(2,1)}, bf16[1,32,1024]{2,1,0:T(8,128)(2,1)}, u32[]{:S(2)}, u32[]{:S(2)}) collective-permute-start(bf16[1,32,1024]{2,1,0:T(8,128)(2,1)} %get-tuple-element.36), channel_id=1, source_target_pairs={{0,16},{1,17},{2,18},{3,19},{4,20},{5,21},{6,22},{7,23},{8,24},{9,... | collective-permute-start | bytes 196616 | tf_op jit(solution)/shard_map/ppermute | solution.py:19
  23.0 10.6 %collective-permute-start.11 = (bf16[2,32,1024]{2,1,0:T(8,128)(2,1)S(1)}, bf16[2,32,1024]{2,1,0:T(8,128)(2,1)}, u32[]{:S(2)}, u32[]{:S(2)}) collective-permute-start(bf16[2,32,1024]{2,1,0:T(8,128)(2,1)S(1)} %pad_maximum_fusion.10), channel_id=1, source_target_pairs={{16,20},{17,21},{18,22},{19,23},{20,16},{21,17},{22,18},{23,19},{2... | collective-permute-start | bytes 393224 | tf_op jit(solution)/shard_map/ppermute | solution.py:19
  27.3 6.9 %collective-permute-start.12 = (bf16[32,2048]{1,0:T(8,128)(2,1)}, bf16[32,2048]{1,0:T(8,128)(2,1)S(1)}, u32[]{:S(2)}, u32[]{:S(2)}) collective-permute-start(bf16[32,2048]{1,0:T(8,128)(2,1)} %cut.17), channel_id=1, source_target_pairs={{0,19},{1,18},{2,17},{3,16},{4,23},{5,22},{6,21},{7,20},{8,27},{9,... | collective-permute-start | bytes 393224 | tf_op jit(solution)/shard_map/ppermute | solution.py:19
  32.9 7.5 %collective-permute-start.21 = (bf16[64,1024]{1,0:T(8,128)(2,1)S(1)}, bf16[64,1024]{1,0:T(8,128)(2,1)S(1)}, u32[]{:S(2)}, u32[]{:S(2)}) collective-permute-start(bf16[64,1024]{1,0:T(8,128)(2,1)S(1)} %get-tuple-element.41), channel_id=1, source_target_pairs={{16,26},{17,27}} | collective-permute-start | bytes 393224 | tf_op jit(solution)/shard_map/ppermute | solution.py:19
  33.6 14.1 %collective-permute-start.22 = (bf16[64,1024]{1,0:T(8,128)(2,1)S(1)}, bf16[64,1024]{1,0:T(8,128)(2,1)S(1)}, u32[]{:S(2)}, u32[]{:S(2)}) collective-permute-start(bf16[64,1024]{1,0:T(8,128)(2,1)S(1)} %get-tuple-element.40), channel_id=1, source_target_pairs={{16,24},{17,25}} | collective-permute-start | bytes 393224 | tf_op jit(solution)/shard_map/ppermute | solution.py:19
  34.3 13.4 %collective-permute-start.23 = (bf16[64,1024]{1,0:T(8,128)(2,1)S(1)}, bf16[64,1024]{1,0:T(8,128)(2,1)S(1)}, u32[]{:S(2)}, u32[]{:S(2)}) collective-permute-start(bf16[64,1024]{1,0:T(8,128)(2,1)S(1)} %get-tuple-element.39), channel_id=1, source_target_pairs={{16,22},{17,23}} | collective-permute-start | bytes 393224 | tf_op jit(solution)/shard_map/ppermute | solution.py:19
  34.9 14.7 %collective-permute-start.24 = (bf16[64,1024]{1,0:T(8,128)(2,1)S(1)}, bf16[64,1024]{1,0:T(8,128)(2,1)S(1)}, u32[]{:S(2)}, u32[]{:S(2)}) collective-permute-start(bf16[64,1024]{1,0:T(8,128)(2,1)S(1)} %get-tuple-element.38), channel_id=1, source_target_pairs={{16,20},{17,21}} | collective-permute-start | bytes 393224 | tf_op jit(solution)/shard_map/ppermute | solution.py:19
  36.3 13.4 %collective-permute-start.25 = (bf16[64,1024]{1,0:T(8,128)(2,1)S(1)}, bf16[64,1024]{1,0:T(8,128)(2,1)S(1)}, u32[]{:S(2)}, u32[]{:S(2)}) collective-permute-start(bf16[64,1024]{1,0:T(8,128)(2,1)S(1)} %get-tuple-element.37), channel_id=1, source_target_pairs={{16,18},{17,19}} | collective-permute-start | bytes 393224 | tf_op jit(solution)/shard_map/ppermute | solution.py:19
  40.4 12.7 %collective-permute-start.2 = (bf16[2,32,1024]{2,1,0:T(8,128)(2,1)S(1)}, bf16[2,32,1024]{2,1,0:T(8,128)(2,1)S(1)}, u32[]{:S(2)}, u32[]{:S(2)}) collective-permute-start(bf16[2,32,1024]{2,1,0:T(8,128)(2,1)S(1)} %pad_maximum_fusion.9), channel_id=1, source_target_pairs={{0,8},{1,9},{2,10},{3,11},{4,12},{5,13},{6,14},{7,15},{8,0},{9,1},... | collective-permute-start | bytes 393224 | tf_op jit(solution)/shard_map/ppermute | solution.py:19
  47.7 16.7 %collective-permute-start.13 = (bf16[4,32,1024]{2,1,0:T(8,128)(2,1)S(1)}, bf16[4,32,1024]{2,1,0:T(8,128)(2,1)S(1)}, u32[]{:S(2)}, u32[]{:S(2)}) collective-permute-start(bf16[4,32,1024]{2,1,0:T(8,128)(2,1)S(1)} %pad_maximum_fusion.7), channel_id=1, source_target_pairs={{16,18},{17,19},{18,16},{19,17},{20,22},{21,23},{22,20},{23,21},{2... | collective-permute-start | bytes 786440 | tf_op jit(solution)/shard_map/ppermute | solution.py:19
  49.7 12.6 %collective-permute-start.26 = (bf16[1,64,1024]{2,1,0:T(8,128)(2,1)S(1)}, bf16[1,64,1024]{2,1,0:T(8,128)(2,1)S(1)}, u32[]{:S(2)}, u32[]{:S(2)}) collective-permute-start(bf16[1,64,1024]{2,1,0:T(8,128)(2,1)S(1)} %fusion.8), channel_id=1, source_target_pairs={{16,18},{17,19},{18,16},{19,17},{20,22},{21,23},{22,20},{23,21},{2... | collective-permute-start | bytes 393224 | tf_op jit(solution)/shard_map/ppermute | solution.py:19
  53.7 18.2 %collective-permute-start.4 = (bf16[4,32,1024]{2,1,0:T(8,128)(2,1)S(1)}, bf16[4,32,1024]{2,1,0:T(8,128)(2,1)S(1)}, u32[]{:S(2)}, u32[]{:S(2)}) collective-permute-start(bf16[4,32,1024]{2,1,0:T(8,128)(2,1)S(1)} %pad_maximum_fusion.6), channel_id=1, source_target_pairs={{0,4},{1,5},{2,6},{3,7},{4,0},{5,1},{6,2},{7,3},{8,12},{9,13},{10,... | collective-permute-start | bytes 786440 | tf_op jit(solution)/shard_map/ppermute | solution.py:19
  55.3 9.8 %collective-permute-start.14 = (bf16[32,2048]{1,0:T(8,128)(2,1)}, bf16[32,2048]{1,0:T(8,128)(2,1)S(1)}, u32[]{:S(2)}, u32[]{:S(2)}) collective-permute-start(bf16[32,2048]{1,0:T(8,128)(2,1)} %cut.18), channel_id=1, source_target_pairs={{0,21},{1,20},{2,23},{3,22},{4,17},{5,16},{6,19},{7,18},{8,29},{9,... | collective-permute-start | bytes 393224 | tf_op jit(solution)/shard_map/ppermute | solution.py:19
  62.3 15.9 %collective-permute-start.27 = (bf16[2,64,1024]{2,1,0:T(8,128)(2,1)S(1)}, bf16[2,64,1024]{2,1,0:T(8,128)(2,1)S(1)}, u32[]{:S(2)}, u32[]{:S(2)}) collective-permute-start(bf16[2,64,1024]{2,1,0:T(8,128)(2,1)S(1)} %pad_maximum_fusion.8), channel_id=1, source_target_pairs={{16,24},{17,25},{18,26},{19,27},{20,28},{21,29},{22,30},{23,31},{2... | collective-permute-start | bytes 786440 | tf_op jit(solution)/shard_map/ppermute | solution.py:19
  65.1 25.3 %collective-permute-start.15 = (bf16[8,32,1024]{2,1,0:T(8,128)(2,1)S(1)}, bf16[8,32,1024]{2,1,0:T(8,128)(2,1)S(1)}, u32[]{:S(2)}, u32[]{:S(2)}) collective-permute-start(bf16[8,32,1024]{2,1,0:T(8,128)(2,1)S(1)} %pad_maximum_fusion.4), channel_id=1, source_target_pairs={{16,24},{17,25},{18,26},{19,27},{20,28},{21,29},{22,30},{23,31},{2... | collective-permute-start | bytes 1572872 | tf_op jit(solution)/shard_map/ppermute | solution.py:19
  78.2 17.3 %collective-permute-start.6 = (bf16[8,32,1024]{2,1,0:T(8,128)(2,1)S(1)}, bf16[8,32,1024]{2,1,0:T(8,128)(2,1)S(1)}, u32[]{:S(2)}, u32[]{:S(2)}) collective-permute-start(bf16[8,32,1024]{2,1,0:T(8,128)(2,1)S(1)} %pad_maximum_fusion.3), channel_id=1, source_target_pairs={{0,2},{1,3},{2,0},{3,1},{4,6},{5,7},{6,4},{7,5},{8,10},{9,11},{10,... | collective-permute-start | bytes 1572872 | tf_op jit(solution)/shard_map/ppermute | solution.py:19
  78.3 20.1 %collective-permute-start.28 = (bf16[4,64,1024]{2,1,0:T(8,128)(2,1)S(1)}, bf16[4,64,1024]{2,1,0:T(8,128)(2,1)S(1)}, u32[]{:S(2)}, u32[]{:S(2)}) collective-permute-start(bf16[4,64,1024]{2,1,0:T(8,128)(2,1)S(1)} %pad_maximum_fusion.5), channel_id=1, source_target_pairs={{16,20},{17,21},{18,22},{19,23},{20,16},{21,17},{22,18},{23,19},{2... | collective-permute-start | bytes 1572872 | tf_op jit(solution)/shard_map/ppermute | solution.py:19
  81.8 8.7 %collective-permute-start.16 = (bf16[32,2048]{1,0:T(8,128)(2,1)}, bf16[32,2048]{1,0:T(8,128)(2,1)S(1)}, u32[]{:S(2)}, u32[]{:S(2)}) collective-permute-start(bf16[32,2048]{1,0:T(8,128)(2,1)} %cut.19), channel_id=1, source_target_pairs={{0,23},{1,22},{2,21},{3,20},{4,19},{5,18},{6,17},{7,16},{8,31},{9,... | collective-permute-start | bytes 393224 | tf_op jit(solution)/shard_map/ppermute | solution.py:19
  85.1 10.6 %collective-permute-start.7 = (bf16[32,2048]{1,0:T(8,128)(2,1)}, bf16[32,2048]{1,0:T(8,128)(2,1)S(1)}, u32[]{:S(2)}, u32[]{:S(2)}) collective-permute-start(bf16[32,2048]{1,0:T(8,128)(2,1)} %cut.15), channel_id=1, source_target_pairs={{0,22},{1,23},{2,20},{3,21},{4,18},{5,19},{6,16},{7,17},{8,30},{9,... | collective-permute-start | bytes 393224 | tf_op jit(solution)/shard_map/ppermute | solution.py:19
  90.5 11.6 %collective-permute-start.17 = (bf16[16,32,1024]{2,1,0:T(8,128)(2,1)S(1)}, bf16[16,32,1024]{2,1,0:T(8,128)(2,1)S(1)}, u32[]{:S(2)}, u32[]{:S(2)}) collective-permute-start(bf16[16,32,1024]{2,1,0:T(8,128)(2,1)S(1)} %pad_maximum_fusion.1.a1), channel_id=1, source_target_pairs={{16,17},{17,16},{18,19},{19,18},{20,21},{21,20},{22,23},{23,22},{2... | collective-permute-start | bytes 3145736 | tf_op jit(solution)/shard_map/ppermute | solution.py:19
  108.0 106.6 %all-to-all-start = ((bf16[16,2048,32]{1,2,0:T(8,128)(2,1)}), bf16[16,2048,32]{1,2,0:T(8,128)(2,1)S(1)}, u32[]{:S(2)}, u32[]{:S(2)}) async-start(bf16[16,2048,32]{1,2,0:T(8,128)(2,1)} %bitcast.61), calls=%async_computation | async-start | bytes 4194304 | tf_op jit(solution)/shard_map/all_to_all | solution.py:290
  122.2 7.0 %collective-permute-start.31 = (bf16[32,2048]{1,0:T(8,128)(2,1)}, bf16[32,2048]{1,0:T(8,128)(2,1)S(1)}, u32[]{:S(2)}, u32[]{:S(2)}) collective-permute-start(bf16[32,2048]{1,0:T(8,128)(2,1)} %cut.21), channel_id=1, source_target_pairs={{0,25},{1,24},{2,27},{3,26},{4,29},{5,28},{6,31},{7,30},{8,17},{9,... | collective-permute-start | bytes 393224 | tf_op jit(solution)/shard_map/ppermute | solution.py:19
  131.6 6.7 %collective-permute-start.32 = (bf16[32,2048]{1,0:T(8,128)(2,1)}, bf16[32,2048]{1,0:T(8,128)(2,1)S(1)}, u32[]{:S(2)}, u32[]{:S(2)}) collective-permute-start(bf16[32,2048]{1,0:T(8,128)(2,1)} %get-tuple-element.29), channel_id=1, source_target_pairs={{0,26},{1,27},{2,24},{3,25},{4,30},{5,31},{6,28},{7,29},{8,18},{9,... | collective-permute-start | bytes 393224 | tf_op jit(solution)/shard_map/ppermute | solution.py:19
  133.2 10.5 %collective-permute-start.33 = (bf16[32,2048]{1,0:T(8,128)(2,1)}, bf16[32,2048]{1,0:T(8,128)(2,1)S(1)}, u32[]{:S(2)}, u32[]{:S(2)}) collective-permute-start(bf16[32,2048]{1,0:T(8,128)(2,1)} %get-tuple-element.30), channel_id=1, source_target_pairs={{0,27},{1,26},{2,25},{3,24},{4,31},{5,30},{6,29},{7,28},{8,19},{9,... | collective-permute-start | bytes 393224 | tf_op jit(solution)/shard_map/ppermute | solution.py:19
  133.7 20.6 %collective-permute-start.34 = (bf16[32,2048]{1,0:T(8,128)(2,1)}, bf16[32,2048]{1,0:T(8,128)(2,1)S(1)}, u32[]{:S(2)}, u32[]{:S(2)}) collective-permute-start(bf16[32,2048]{1,0:T(8,128)(2,1)} %get-tuple-element.31), channel_id=1, source_target_pairs={{0,28},{1,29},{2,30},{3,31},{4,24},{5,25},{6,26},{7,27},{8,20},{9,... | collective-permute-start | bytes 393224 | tf_op jit(solution)/shard_map/ppermute | solution.py:19
  156.7 74.0 %collective-permute-start.35 = (bf16[32,2048]{1,0:T(8,128)(2,1)}, bf16[32,2048]{1,0:T(8,128)(2,1)S(1)}, u32[]{:S(2)}, u32[]{:S(2)}) collective-permute-start(bf16[32,2048]{1,0:T(8,128)(2,1)} %get-tuple-element.32), channel_id=1, source_target_pairs={{0,29},{1,28},{2,31},{3,30},{4,25},{5,24},{6,27},{7,26},{8,21},{9,... | collective-permute-start | bytes 393224 | tf_op jit(solution)/shard_map/ppermute | solution.py:19
  156.7 74.0 %collective-permute-start.36 = (bf16[32,2048]{1,0:T(8,128)(2,1)}, bf16[32,2048]{1,0:T(8,128)(2,1)S(1)}, u32[]{:S(2)}, u32[]{:S(2)}) collective-permute-start(bf16[32,2048]{1,0:T(8,128)(2,1)} %get-tuple-element.33), channel_id=1, source_target_pairs={{0,30},{1,31},{2,28},{3,29},{4,26},{5,27},{6,24},{7,25},{8,22},{9,... | collective-permute-start | bytes 393224 | tf_op jit(solution)/shard_map/ppermute | solution.py:19
  182.6 48.2 %collective-permute-start.37 = (bf16[32,2048]{1,0:T(8,128)(2,1)}, bf16[32,2048]{1,0:T(8,128)(2,1)S(1)}, u32[]{:S(2)}, u32[]{:S(2)}) collective-permute-start(bf16[32,2048]{1,0:T(8,128)(2,1)} %get-tuple-element.34), channel_id=1, source_target_pairs={{0,31},{1,30},{2,29},{3,28},{4,27},{5,26},{6,25},{7,24},{8,23},{9,... | collective-permute-start | bytes 393224 | tf_op jit(solution)/shard_map/ppermute | solution.py:19
  (31 other events, 205.4 us)

commit v3 on v2

v3 whole, which is shorter than its diff:
```python
import jax
import jax.numpy as jnp
from jax import lax
from jax.experimental import pallas as pl
from jax.experimental.pallas import tpu as pltpu
from jax.sharding import PartitionSpec as P

AXES = ("rows", "rhs")
F32 = jnp.float32
BF16 = jnp.bfloat16
NT = (((1,), (1,)), ((), ()))
LIMIT = pltpu.CompilerParams(vmem_limit_bytes=58 << 20)
FREE = pl.CostEstimate(flops=0, bytes_accessed=0, transcendentals=0)
ANY = pl.BlockSpec(memory_space=pl.ANY)


def send(x, pairs):
    return lax.ppermute(x, AXES, pairs)


def after(value, *tokens):
    return lax.optimization_barrier((value, *tokens))[0]


def held_rows(tm, pos, i, owner, panel_rows):
    in_panel = i * tm < panel_rows
    return jnp.logical_and(in_panel, jnp.logical_or(pos == 0, pos == owner))


def solve_update(pos, rs0, rs1, block, diag, cols, owner, half, offs0, offs1, offs2):
    rows, nb = cols.shape[1:]
    width = rs0[0].shape[1]
    members = width * len(offs0)
    tm = 512
    wide = BF16 if width % 16 == 0 else F32

    def gather(dst, pair, offs, wrap):
        height = pair[0].shape[1]
        count = pair[0].shape[0]
        for j, off in enumerate(offs):
            ref = pair[j // count]
            at = pl.multiple_of(((wrap ^ off) & (len(offs) - 1)) * height, height)
            dst[pl.ds(at, height), :] = ref[j % count].astype(dst.dtype)

    def dot_nt(a, b):
        return lax.dot_general(a.astype(BF16), b, NT, preferred_element_type=F32)

    def kernel(pos_ref, a0, b0, a1, b1, a2, b2, d_ref, c_ref, o_ref, g0, g1, g2, s0, s1):
        i = pl.program_id(0)
        pos = pos_ref[0]
        upper = pos >= owner
        chunk = min(512, members)

        @pl.when(i == 0)
        def _():
            gather(g0, (a0, b0), offs0, pos)

            @pl.loop(0, members // chunk)
            def _(t):
                at = pl.ds(pl.multiple_of(t * chunk, chunk), chunk)
                s0[at, :] = dot_nt(g0[at, :], d_ref[0]).astype(BF16)

            @pl.when(upper)
            def _():
                gather(g1, (a1, b1), offs1, pos)
                @pl.when(pos & 1 == 0)
                def _():
                    gather(g2, (a2,), offs2, pos >> 1)

                @pl.when(pos & 1 == 1)
                def _():
                    gather(g2, (b2,), offs2, pos >> 1)

                @pl.loop(0, members // chunk)
                def _(t):
                    at = pl.ds(pl.multiple_of(t * chunk, chunk), chunk)
                    panel = g1[at, :].astype(F32) - dot_nt(s0[at, :], g2[...])
                    s1[at, :] = dot_nt(panel, d_ref[1]).astype(BF16)

        held = held_rows(tm, pos, i, owner, nb)
        start = pl.multiple_of(jnp.where(held, i, 0) * tm, tm)

        @pl.when(jnp.logical_not(held))
        def _():
            o_ref[...] = -dot_nt(c_ref[0], s0[...])

            @pl.when(upper)
            def _():
                o_ref[...] -= dot_nt(c_ref[1], s1[...])

        @pl.when(jnp.logical_and(held, pos == 0))
        def _():
            o_ref[...] = s0[:, pl.ds(start, tm)].astype(F32).T

        @pl.when(jnp.logical_and(held, pos == owner))
        def _():
            o_ref[...] = s1[:, pl.ds(start, tm)].astype(F32).T

    def full(x):
        zeros = (0,) * x.ndim
        return pl.BlockSpec(x.shape, lambda i, p: zeros)

    ins = [*rs0, *rs1, *block, diag]
    return pl.pallas_call(
        kernel,
        out_shape=jax.ShapeDtypeStruct((rows, members), F32),
        grid_spec=pltpu.PrefetchScalarGridSpec(
            num_scalar_prefetch=1,
            grid=(rows // tm,),
            in_specs=[full(x) for x in ins] + [pl.BlockSpec((2, tm, nb), lambda i, p: (0, i, 0))],
            out_specs=pl.BlockSpec((tm, members), lambda i, p: (i, 0)),
            scratch_shapes=[
                pltpu.VMEM((members, nb), wide),
                pltpu.VMEM((members, nb), wide),
                pltpu.VMEM((nb, nb), BF16),
                pltpu.VMEM((members, nb), BF16),
                pltpu.VMEM((members, nb), BF16),
            ],
        ),
        compiler_params=LIMIT,
        cost_estimate=pl.CostEstimate(
            flops=14 * members * nb * nb, bytes_accessed=24 << 20, transcendentals=0
        ),
        name="solve_update",
    )(pos, *ins, cols)


def finish(pos, v, a_t, owner, nb):
    rows, members = v.shape
    tm = 256

    def kernel(pos_ref, v_ref, a_ref, o_ref):
        held = held_rows(tm, pos_ref[0], pl.program_id(0), owner, nb)
        row = lax.broadcasted_iota(jnp.int32, (tm, tm), 0)
        col = lax.broadcasted_iota(jnp.int32, (tm, tm), 1)
        keep = jnp.logical_and(row == col, jnp.logical_not(held))
        pick = jnp.where(keep, 1.0, 0.0).astype(BF16)
        turned = lax.dot_general(pick, a_ref[...], NT, preferred_element_type=F32)
        o_ref[...] = v_ref[...] + turned

    return pl.pallas_call(
        kernel,
        out_shape=jax.ShapeDtypeStruct(v.shape, F32),
        grid_spec=pltpu.PrefetchScalarGridSpec(
            num_scalar_prefetch=1,
            grid=(rows // tm,),
            in_specs=[
                pl.BlockSpec((tm, members), lambda i, p: (i, 0)),
                pl.BlockSpec((members, tm), lambda i, p: (0, i)),
            ],
            out_specs=pl.BlockSpec((tm, members), lambda i, p: (i, 0)),
        ),
        input_output_aliases={1: 0},
        compiler_params=LIMIT,
        cost_estimate=pl.CostEstimate(flops=0, bytes_accessed=20 << 20, transcendentals=0),
        name="finish",
    )(pos, v, a_t)


def local(right_sides, col_panels, diag_inverses):
    n = lax.axis_size("rows") * lax.axis_size("rhs")
    me = lax.axis_index(AXES).astype(jnp.int32)
    pos = me.reshape(1)
    nb = diag_inverses.shape[1]
    total_rows, width = right_sides.shape
    rows = total_rows // n
    half = n // 2
    owner = half
    x_t = right_sides.T

    def every(mask):
        return [(i, i ^ mask) for i in range(n)]

    def upper(mask):
        return [(i, i ^ mask) for i in range(half, n)]

    def even(mask):
        return [(i, i ^ mask) for i in range(half, n, 2)]

    quarter = half // 2
    both = jnp.stack([x_t[:, :nb], x_t[:, total_rows // 2 : total_rows // 2 + nb]])
    theirs = send(both, every(half))
    cur = [jnp.stack([both[k], theirs[k]]) for k in range(2)]
    offs = [[0, half], [0, half], [0]]

    chips = quarter // 2
    slots = col_panels[0, :nb].reshape(chips, nb // chips, nb)
    got = slots[0]
    for t in range(1, chips):
        here = send(slots[t], [(owner, owner + 2 * t)])
        got = jnp.where(me // 2 == owner // 2 + t, here, got)
    down = send(got, [(i, i + quarter) for i in range(owner, owner + quarter, 2)])
    cur.append(jnp.where(me >= owner + quarter, down, got)[None])

    new = [send(cur[0], every(quarter)), send(cur[1], upper(quarter))]
    for k in range(2):
        cur[k] = jnp.concatenate([cur[k], new[k]], axis=0)
        offs[k] = offs[k] + [o ^ quarter for o in offs[k]]
    cur = list(lax.optimization_barrier(tuple(cur)))

    inner = [1 << k for k in range(1, quarter.bit_length() - 1)][::-1]
    orders = [inner, inner[::-1], inner]
    pairs = [every, upper, even]
    for k in range(len(inner)):
        bits = [order[k] for order in orders]
        new = [send(cur[t], pairs[t](bits[t])) for t in range(3)]
        new = lax.optimization_barrier(tuple(new))
        if k == 0:
            gate = new
        shifts = [bits[0], bits[1], bits[2] >> 1]
        offs = [offs[t] + [o ^ shifts[t] for o in offs[t]] for t in range(3)]
        cur = [jnp.concatenate([cur[t], new[t]], axis=0) for t in range(3)]
    new = [
        send(cur[0], every(1)),
        send(cur[1], upper(1)),
        send(cur[2], [(i, i + 1) for i in range(half, n, 2)]),
    ]
    ends = [(cur[t], new[t]) for t in range(3)]
    offs = [offs[t] + [o ^ 1 for o in offs[t]] for t in range(2)] + [offs[2]]

    tiles = x_t.reshape(width // 8, 8, n, rows).transpose(2, 0, 1, 3)
    packed = tiles.reshape(n, width, rows)
    a_t = lax.all_to_all(after(packed, *gate), AXES, split_axis=0, concat_axis=0, tiled=True)
    a_t = a_t.reshape(n * width, rows)
    v = solve_update(pos, *ends, diag_inverses, col_panels, owner, half, *offs)
    return finish(pos, v, a_t, owner, nb)


def solution(mesh):
    return jax.shard_map(
        local,
        mesh=mesh,
        in_specs=(P(None, AXES), P(None, AXES, None), P()),
        out_specs=P(AXES, None),
        check_vma=False,
    )
```

time: 236 us -> 163 us (0.69)
  starting transfers between devices: 111 us -> 64.8 us
  Pallas kernels: 62.8 us -> 35.5 us
  waiting for transfers between devices: 42.9 us -> 47.7 us
  local copies, waits for them, and re-layouts: 13 us -> 9.77 us
  other arithmetic: 4.58 us -> 1.49 us
    ppermute x38 -> x16, starting transfers between devices: 99.7 us -> 44.9 us  [send(): return lax.ppermute(x, AXES, pairs)]
    pallas_call x17 -> x1, Pallas kernels: 36.5 us -> 10.6 us  [finish(): pl.pallas_call(kernel, out_shape=jax.ShapeDtypeStruct(v.shape, F32), grid...]
    all_to_all x1, starting transfers between devices: 11 us -> 19.8 us  [local(): lax.all_to_all(after(packed, *gate), AXES, split_axis=0, concat_axis=0, t...]
    transpose x0 -> x1, local copies, waits for them, and re-layouts: none -> 4.79 us  [local(): tiles = x_t.reshape(width // 8, 8, n, rows).transpose(2, 0, 1, 3)]
    ppermute x38 -> x16, waiting for transfers between devices: 42.9 us -> 47.7 us  [send(): return lax.ppermute(x, AXES, pairs)]
    unnamed x48 -> x17, local copies, waits for them, and re-layouts: 5.99 us -> 2.47 us
    concatenate x11 -> x5, other arithmetic: 3.19 us -> 0.25 us  [the longest x3 0.2 us: local(): cur = [jnp.concatenate([cur[t], new[t]], axis=0) for t in range(3)]]
  transfers between devices with their start and end apart: 39 -> 17, of which waited for: 12 -> 7; matrix products, arithmetic and copies ran while one was open for 3% -> 5% of each run, Pallas kernels for 26% -> 16%
where the time goes in v3:
time: 163 us; the launch traced here: 159 us
  starting transfers between devices  64.8 us (40%)
  waiting for transfers between devices  47.7 us (29%)
  Pallas kernels  35.5 us (22%)
  local copies, waits for them, and re-layouts  9.77 us (6%)
    ppermute x16, waiting for transfers between devices, send(): return lax.ppermute(x, AXES, pairs)  47.7 us
    ppermute x16, starting transfers between devices, send(): return lax.ppermute(x, AXES, pairs)  44.9 us
    pallas_call x1, Pallas kernels, solve_update(): pl.pallas_call(kernel, out_shape=jax.ShapeDtypeStruct((rows, members), F3...  24.9 us
    all_to_all x1, starting transfers between devices, local(): lax.all_to_all(after(packed, *gate), AXES, split_axis=0, concat_axis=0, t...  19.8 us
    pallas_call x1, Pallas kernels, finish(): pl.pallas_call(kernel, out_shape=jax.ShapeDtypeStruct(v.shape, F32), grid...  10.6 us
    transpose x1, local copies, waits for them, and re-layouts, local(): tiles = x_t.reshape(width // 8, 8, n, rows).transpose(2, 0, 1, 3)  4.79 us
  transfers between devices with their start and end apart: 17, of which 7 were waited for; matrix products, arithmetic and copies ran while one was open for 5% of the time, Pallas kernels for 16%

profile of v3, /device:TPU:21, one launch (start us, length us, event | category | flops | bytes accessed | tf_op | source)
XLA Modules:
  0.0 159.5 jit_solution(5632367765144522560)
XLA Ops:
  0.0 1.5 slice_bitcast_fusion
  1.5 0.7 collective-permute-start.5
  2.2 0.7 collective-permute-start.4
  2.9 0.7 collective-permute-start.3
  3.6 0.9 slice_bitcast_fusion.3
  4.5 0.1 collective-permute-start
  4.6 1.1 fusion.1
  5.8 0.7 collective-permute-start.6
  6.5 3.0 %collective-permute-done = bf16[2,32,1024]{2,1,0:T(8,128)(2,1)S(1)} collective-permute-done((bf16[2,32,1024]{2,1,0:T(8,128)(2,1)S(1)}, bf16[2,32,1024]{2,1,0:T(8,128)(2,1)S(1)}, u32[]{:S(2)}, u32[]{:S(2)}) %collective-permute-start) | collective-permute-done | bytes 131104 | tf_op jit(solution)/shard_map/ppermute | solution.py:18
  9.5 5.5 %collective-permute-start.1 = (bf16[2,32,1024]{2,1,0:T(8,128)(2,1)S(1)}, bf16[2,32,1024]{2,1,0:T(8,128)(2,1)S(1)}, u32[]{:S(2)}, u32[]{:S(2)}) collective-permute-start(bf16[2,32,1024]{2,1,0:T(8,128)(2,1)S(1)} %pad_maximum_fusion.5), channel_id=1, source_target_pairs={{0,8},{1,9},{2,10},{3,11},{4,12},{5,13},{6,14},{7,15},{8,0},{9,1},... | collective-permute-start | bytes 393224 | tf_op jit(solution)/shard_map/ppermute | solution.py:18
  15.0 1.9 %collective-permute-start.2 = (bf16[2,32,1024]{2,1,0:T(8,128)(2,1)S(1)}, bf16[2,32,1024]{2,1,0:T(8,128)(2,1)S(1)}, u32[]{:S(2)}, u32[]{:S(2)}) collective-permute-start(bf16[2,32,1024]{2,1,0:T(8,128)(2,1)S(1)} %pad_maximum_fusion.7), channel_id=1, source_target_pairs={{16,24},{17,25},{18,26},{19,27},{20,28},{21,29},{22,30},{23,31},{2... | collective-permute-start | bytes 393224 | tf_op jit(solution)/shard_map/ppermute | solution.py:18
  16.9 0.4 collective-permute-done.1
  17.4 4.4 %collective-permute-done.2 = bf16[2,32,1024]{2,1,0:T(8,128)(2,1)S(1)} collective-permute-done((bf16[2,32,1024]{2,1,0:T(8,128)(2,1)S(1)}, bf16[2,32,1024]{2,1,0:T(8,128)(2,1)S(1)}, u32[]{:S(2)}, u32[]{:S(2)}) %collective-permute-start.2) | collective-permute-done | bytes 131104 | tf_op jit(solution)/shard_map/ppermute | solution.py:18
  21.9 0.7 collective-permute-start.9
  22.6 3.9 %collective-permute-start.8 = (bf16[4,32,1024]{2,1,0:T(8,128)(2,1)S(1)}, bf16[4,32,1024]{2,1,0:T(8,128)(2,1)S(1)}, u32[]{:S(2)}, u32[]{:S(2)}) collective-permute-start(bf16[4,32,1024]{2,1,0:T(8,128)(2,1)S(1)} %pad_maximum_fusion.4), channel_id=1, source_target_pairs={{16,18},{17,19},{18,16},{19,17},{20,22},{21,23},{22,20},{23,21},{2... | collective-permute-start | bytes 786440 | tf_op jit(solution)/shard_map/ppermute | solution.py:18
  26.6 4.8 %copy.7 = bf16[32,4,8,2048]{3,2,1,0:T(8,128)(2,1)} copy(bf16[32,4,8,2048]{3,2,0,1:T(8,128)(2,1)} %bitcast.30) | data formatting | bytes 8388608 | tf_op jit(solution)/shard_map/transpose | solution.py:221
  31.4 19.8 %all-to-all-start = ((bf16[32,32,2048]{2,1,0:T(8,128)(2,1)}), bf16[32,32,2048]{2,1,0:T(8,128)(2,1)}, u32[]{:S(2)}, u32[]{:S(2)}) async-start(bf16[32,32,2048]{2,1,0:T(8,128)(2,1)} %bitcast.28), calls=%async_computation | async-start | bytes 8388608 | tf_op jit(solution)/shard_map/all_to_all | solution.py:223
  51.2 0.1 pad_maximum_fusion
  51.3 0.7 collective-permute-start.12
  52.2 2.2 %collective-permute-start.11 = (bf16[8,32,1024]{2,1,0:T(8,128)(2,1)S(1)}, bf16[8,32,1024]{2,1,0:T(8,128)(2,1)S(1)}, u32[]{:S(2)}, u32[]{:S(2)}) collective-permute-start(bf16[8,32,1024]{2,1,0:T(8,128)(2,1)S(1)} %pad_maximum_fusion.2), channel_id=1, source_target_pairs={{16,20},{17,21},{18,22},{19,23},{20,16},{21,17},{22,18},{23,19},{2... | collective-permute-start | bytes 1572872 | tf_op jit(solution)/shard_map/ppermute | solution.py:18
  54.4 1.2 collective-permute-start.10
  55.7 35.2 %collective-permute-done.11 = bf16[8,32,1024]{2,1,0:T(8,128)(2,1)S(1)} collective-permute-done((bf16[8,32,1024]{2,1,0:T(8,128)(2,1)S(1)}, bf16[8,32,1024]{2,1,0:T(8,128)(2,1)S(1)}, u32[]{:S(2)}, u32[]{:S(2)}) %collective-permute-start.11) | collective-permute-done | bytes 524320 | tf_op jit(solution)/shard_map/ppermute | solution.py:18
  90.8 0.5 collective-permute-done.10
  91.4 1.3 collective-permute-start.15
  92.9 24.4 %collective-permute-start.14 = (bf16[16,32,1024]{2,1,0:T(8,128)(2,1)S(1)}, bf16[16,32,1024]{2,1,0:T(8,128)(2,1)S(1)}, u32[]{:S(2)}, u32[]{:S(2)}) collective-permute-start(bf16[16,32,1024]{2,1,0:T(8,128)(2,1)S(1)} %constant_dynamic-update-slice_fusion.3.a1), channel_id=1, source_target_pairs={{16,17},{17,16},{18,19},{19,18},{20,21},{21,20},{22,23},{23,22},{2... | collective-permute-start | bytes 3145736 | tf_op jit(solution)/shard_map/ppermute | solution.py:18
  117.3 0.1 collective-permute-start.13
  117.4 2.8 %collective-permute-done.14.b1 = bf16[16,32,1024]{2,1,0:T(8,128)(2,1)S(1)} collective-permute-done((bf16[16,32,1024]{2,1,0:T(8,128)(2,1)S(1)}, bf16[16,32,1024]{2,1,0:T(8,128)(2,1)S(1)}, u32[]{:S(2)}, u32[]{:S(2)}) %collective-permute-start.14) | collective-permute-done | bytes 1048608 | tf_op jit(solution)/shard_map/ppermute | solution.py:18
  120.2 1.5 collective-permute-done.13.b0
  121.7 1.0 copy-done.5
  122.7 1.3 copy-done.3
  124.0 24.9 %solve_update.1.v_ref = f32[2048,1024]{1,0:T(8,128)} custom-call(s32[1]{0:T(128)} %bitcast.pos_ref, bf16[16,32,1024]{2,1,0:T(8,128)(2,1)} %copy-done.2, bf16[16,32,1024]{2,1,0:T(8,128)(2,1)} %copy-done.5, bf16[16,32,1024]{2,1,0:T(8,128)(2,1)} %copy-done.1, bf16[16,32,1024]{2,1,0:T(8,128)(2,1)} %copy-done.4, bf16[4,256,1024]{2,1,0:T(8,128)(2,1)} %copy-done, ...), custom_call_target="tpu_custom_call" | custom-call | flops 15032385536 | bytes 25165824 | tf_op jit(solution)/shard_map/solve_update/pallas_call | solution.py:104
  148.9 10.6 %finish.1 = f32[2048,1024]{1,0:T(8,128)} custom-call(s32[1]{0:T(128)} %bitcast.pos_ref, f32[2048,1024]{1,0:T(8,128)} %solve_update.1.v_ref, bf16[1024,2048]{1,0:T(8,128)(2,1)} %bitcast.12.a_ref), custom_call_target="tpu_custom_call", output_to_operand_aliasing={{}: (1, {})} | custom-call | bytes 20971520 | tf_op jit(solution)/shard_map/finish/pallas_call | solution.py:141
  (38 shorter events, 0.7 us)
Async XLA Ops:
  1.5 3.1 %collective-permute-start.5 = (bf16[256,1024]{1,0:T(8,128)(2,1)S(1)}, bf16[256,1024]{1,0:T(8,128)(2,1)S(1)}, u32[]{:S(2)}, u32[]{:S(2)}) collective-permute-start(bf16[256,1024]{1,0:T(8,128)(2,1)S(1)} %get-tuple-element.25), channel_id=1, source_target_pairs={{16,18}} | collective-permute-start | bytes 1572872 | tf_op jit(solution)/shard_map/ppermute | solution.py:18
  2.2 2.4 %collective-permute-start.4 = (bf16[256,1024]{1,0:T(8,128)(2,1)S(1)}, bf16[256,1024]{1,0:T(8,128)(2,1)S(1)}, u32[]{:S(2)}, u32[]{:S(2)}) collective-permute-start(bf16[256,1024]{1,0:T(8,128)(2,1)S(1)} %get-tuple-element.26), channel_id=1, source_target_pairs={{16,20}} | collective-permute-start | bytes 1572872 | tf_op jit(solution)/shard_map/ppermute | solution.py:18
  2.9 1.7 %collective-permute-start.3 = (bf16[256,1024]{1,0:T(8,128)(2,1)S(1)}, bf16[256,1024]{1,0:T(8,128)(2,1)S(1)}, u32[]{:S(2)}, u32[]{:S(2)}) collective-permute-start(bf16[256,1024]{1,0:T(8,128)(2,1)S(1)} %get-tuple-element.27), channel_id=1, source_target_pairs={{16,22}} | collective-permute-start | bytes 1572872 | tf_op jit(solution)/shard_map/ppermute | solution.py:18
  4.5 4.9 %collective-permute-start = (bf16[2,32,1024]{2,1,0:T(8,128)(2,1)S(1)}, bf16[2,32,1024]{2,1,0:T(8,128)(2,1)S(1)}, u32[]{:S(2)}, u32[]{:S(2)}) collective-permute-start(bf16[2,32,1024]{2,1,0:T(8,128)(2,1)S(1)} %pad_maximum_fusion.6), channel_id=1, source_target_pairs={{0,16},{1,17},{2,18},{3,19},{4,20},{5,21},{6,22},{7,23},{8,24},{9,... | collective-permute-start | bytes 393224 | tf_op jit(solution)/shard_map/ppermute | solution.py:18
  5.8 16.0 %collective-permute-start.6 = (bf16[256,1024]{1,0:T(8,128)(2,1)S(1)}, bf16[256,1024]{1,0:T(8,128)(2,1)S(1)}, u32[]{:S(2)}, u32[]{:S(2)}) collective-permute-start(bf16[256,1024]{1,0:T(8,128)(2,1)S(1)} %fusion.1), channel_id=1, source_target_pairs={{16,24},{18,26},{20,28},{22,30}} | collective-permute-start | bytes 1572872 | tf_op jit(solution)/shard_map/ppermute | solution.py:18
  9.5 7.9 %collective-permute-start.1 = (bf16[2,32,1024]{2,1,0:T(8,128)(2,1)S(1)}, bf16[2,32,1024]{2,1,0:T(8,128)(2,1)S(1)}, u32[]{:S(2)}, u32[]{:S(2)}) collective-permute-start(bf16[2,32,1024]{2,1,0:T(8,128)(2,1)S(1)} %pad_maximum_fusion.5), channel_id=1, source_target_pairs={{0,8},{1,9},{2,10},{3,11},{4,12},{5,13},{6,14},{7,15},{8,0},{9,1},... | collective-permute-start | bytes 393224 | tf_op jit(solution)/shard_map/ppermute | solution.py:18
  15.0 6.8 %collective-permute-start.2 = (bf16[2,32,1024]{2,1,0:T(8,128)(2,1)S(1)}, bf16[2,32,1024]{2,1,0:T(8,128)(2,1)S(1)}, u32[]{:S(2)}, u32[]{:S(2)}) collective-permute-start(bf16[2,32,1024]{2,1,0:T(8,128)(2,1)S(1)} %pad_maximum_fusion.7), channel_id=1, source_target_pairs={{16,24},{17,25},{18,26},{19,27},{20,28},{21,29},{22,30},{23,31},{2... | collective-permute-start | bytes 393224 | tf_op jit(solution)/shard_map/ppermute | solution.py:18
  21.9 9.5 %collective-permute-start.9 = (bf16[1,256,1024]{2,1,0:T(8,128)(2,1)S(1)}, bf16[1,256,1024]{2,1,0:T(8,128)(2,1)S(1)}, u32[]{:S(2)}, u32[]{:S(2)}) collective-permute-start(bf16[1,256,1024]{2,1,0:T(8,128)(2,1)S(1)} %select_bitcast_fusion), channel_id=1, source_target_pairs={{16,20},{18,22},{20,16},{22,18},{24,28},{26,30},{28,24},{30,26}} | collective-permute-start | bytes 1572872 | tf_op jit(solution)/shard_map/ppermute | solution.py:18
  22.6 8.8 %collective-permute-start.7 = (bf16[4,32,1024]{2,1,0:T(8,128)(2,1)S(1)}, bf16[4,32,1024]{2,1,0:T(8,128)(2,1)S(1)}, u32[]{:S(2)}, u32[]{:S(2)}) collective-permute-start(bf16[4,32,1024]{2,1,0:T(8,128)(2,1)S(1)} %pad_maximum_fusion.3), channel_id=1, source_target_pairs={{0,4},{1,5},{2,6},{3,7},{4,0},{5,1},{6,2},{7,3},{8,12},{9,13},{10,... | collective-permute-start | bytes 786440 | tf_op jit(solution)/shard_map/ppermute | solution.py:18
  22.6 8.7 %collective-permute-start.8 = (bf16[4,32,1024]{2,1,0:T(8,128)(2,1)S(1)}, bf16[4,32,1024]{2,1,0:T(8,128)(2,1)S(1)}, u32[]{:S(2)}, u32[]{:S(2)}) collective-permute-start(bf16[4,32,1024]{2,1,0:T(8,128)(2,1)S(1)} %pad_maximum_fusion.4), channel_id=1, source_target_pairs={{16,18},{17,19},{18,16},{19,17},{20,22},{21,23},{22,20},{23,21},{2... | collective-permute-start | bytes 786440 | tf_op jit(solution)/shard_map/ppermute | solution.py:18
  31.4 117.5 %all-to-all-start = ((bf16[32,32,2048]{2,1,0:T(8,128)(2,1)}), bf16[32,32,2048]{2,1,0:T(8,128)(2,1)}, u32[]{:S(2)}, u32[]{:S(2)}) async-start(bf16[32,32,2048]{2,1,0:T(8,128)(2,1)} %bitcast.28), calls=%async_computation | async-start | bytes 8388608 | tf_op jit(solution)/shard_map/all_to_all | solution.py:223
  51.3 40.0 %collective-permute-start.12 = (bf16[2,256,1024]{2,1,0:T(8,128)(2,1)S(1)}, bf16[2,256,1024]{2,1,0:T(8,128)(2,1)S(1)}, u32[]{:S(2)}, u32[]{:S(2)}) collective-permute-start(bf16[2,256,1024]{2,1,0:T(8,128)(2,1)S(1)} %pad_maximum_fusion), channel_id=1, source_target_pairs={{16,18},{18,16},{20,22},{22,20},{24,26},{26,24},{28,30},{30,28}} | collective-permute-start | bytes 3145736 | tf_op jit(solution)/shard_map/ppermute | solution.py:18
  52.2 38.7 %collective-permute-start.11 = (bf16[8,32,1024]{2,1,0:T(8,128)(2,1)S(1)}, bf16[8,32,1024]{2,1,0:T(8,128)(2,1)S(1)}, u32[]{:S(2)}, u32[]{:S(2)}) collective-permute-start(bf16[8,32,1024]{2,1,0:T(8,128)(2,1)S(1)} %pad_maximum_fusion.2), channel_id=1, source_target_pairs={{16,20},{17,21},{18,22},{19,23},{20,16},{21,17},{22,18},{23,19},{2... | collective-permute-start | bytes 1572872 | tf_op jit(solution)/shard_map/ppermute | solution.py:18
  54.4 37.0 %collective-permute-start.10 = (bf16[8,32,1024]{2,1,0:T(8,128)(2,1)S(1)}, bf16[8,32,1024]{2,1,0:T(8,128)(2,1)S(1)}, u32[]{:S(2)}, u32[]{:S(2)}) collective-permute-start(bf16[8,32,1024]{2,1,0:T(8,128)(2,1)S(1)} %pad_maximum_fusion.1), channel_id=1, source_target_pairs={{0,2},{1,3},{2,0},{3,1},{4,6},{5,7},{6,4},{7,5},{8,10},{9,11},{10,... | collective-permute-start | bytes 1572872 | tf_op jit(solution)/shard_map/ppermute | solution.py:18
  91.4 32.6 %copy-start = (bf16[4,256,1024]{2,1,0:T(8,128)(2,1)}, bf16[4,256,1024]{2,1,0:T(8,128)(2,1)S(1)}, u32[]{:S(2)}) copy-start(bf16[4,256,1024]{2,1,0:T(8,128)(2,1)S(1)} %constant_dynamic-update-slice_fusion.6.a2) | copy-start | bytes 6291460
  91.4 30.3 %collective-permute-start.15 = (bf16[4,256,1024]{2,1,0:T(8,128)(2,1)S(1)}, bf16[4,256,1024]{2,1,0:T(8,128)(2,1)S(1)}, u32[]{:S(2)}, u32[]{:S(2)}) collective-permute-start(bf16[4,256,1024]{2,1,0:T(8,128)(2,1)S(1)} %constant_dynamic-update-slice_fusion.6.a2), channel_id=1, source_target_pairs={{16,17},{18,19},{20,21},{22,23},{24,25},{26,27},{28,29},{30,31}} | collective-permute-start | bytes 6291464 | tf_op jit(solution)/shard_map/ppermute | solution.py:18
  92.8 31.2 %copy-start.1 = (bf16[16,32,1024]{2,1,0:T(8,128)(2,1)}, bf16[16,32,1024]{2,1,0:T(8,128)(2,1)S(1)}, u32[]{:S(2)}) copy-start(bf16[16,32,1024]{2,1,0:T(8,128)(2,1)S(1)} %constant_dynamic-update-slice_fusion.3.a1) | copy-start | bytes 3145732
  92.9 27.3 %collective-permute-start.14 = (bf16[16,32,1024]{2,1,0:T(8,128)(2,1)S(1)}, bf16[16,32,1024]{2,1,0:T(8,128)(2,1)S(1)}, u32[]{:S(2)}, u32[]{:S(2)}) collective-permute-start(bf16[16,32,1024]{2,1,0:T(8,128)(2,1)S(1)} %constant_dynamic-update-slice_fusion.3.a1), channel_id=1, source_target_pairs={{16,17},{17,16},{18,19},{19,18},{20,21},{21,20},{22,23},{23,22},{2... | collective-permute-start | bytes 3145736 | tf_op jit(solution)/shard_map/ppermute | solution.py:18
  117.3 6.7 %copy-start.2 = (bf16[16,32,1024]{2,1,0:T(8,128)(2,1)}, bf16[16,32,1024]{2,1,0:T(8,128)(2,1)S(1)}, u32[]{:S(2)}) copy-start(bf16[16,32,1024]{2,1,0:T(8,128)(2,1)S(1)} %constant_dynamic-update-slice_fusion.a0) | copy-start | bytes 3145732
  117.3 4.4 %collective-permute-start.13 = (bf16[16,32,1024]{2,1,0:T(8,128)(2,1)S(1)}, bf16[16,32,1024]{2,1,0:T(8,128)(2,1)S(1)}, u32[]{:S(2)}, u32[]{:S(2)}) collective-permute-start(bf16[16,32,1024]{2,1,0:T(8,128)(2,1)S(1)} %constant_dynamic-update-slice_fusion.a0), channel_id=1, source_target_pairs={{0,1},{1,0},{2,3},{3,2},{4,5},{5,4},{6,7},{7,6},{8,9},{9,8},{10,11... | collective-permute-start | bytes 3145736 | tf_op jit(solution)/shard_map/ppermute | solution.py:18
  120.2 3.8 %copy-start.4 = (bf16[16,32,1024]{2,1,0:T(8,128)(2,1)}, bf16[16,32,1024]{2,1,0:T(8,128)(2,1)S(1)}, u32[]{:S(2)}) copy-start(bf16[16,32,1024]{2,1,0:T(8,128)(2,1)S(1)} %collective-permute-done.14.b1) | copy-start | bytes 3145732
  121.7 1.0 copy-start.5
  122.7 1.3 copy-start.3

commit v4 on v3

v4 whole, which is shorter than its diff:
```python
import jax
import jax.numpy as jnp
from jax import lax
from jax.experimental import pallas as pl
from jax.experimental.pallas import tpu as pltpu
from jax.sharding import PartitionSpec as P

AXES = ("rows", "rhs")
F32 = jnp.float32
BF16 = jnp.bfloat16
NT = (((1,), (1,)), ((), ()))
FREE = pl.CostEstimate(flops=0, bytes_accessed=0, transcendentals=0)
LIMIT = pltpu.CompilerParams(vmem_limit_bytes=58 << 20)


def send(x, pairs):
    return lax.ppermute(x, AXES, pairs)


def after(value, *tokens):
    return lax.optimization_barrier((value, *tokens))[0]


def collect(dst, refs, offs, where):
    height = refs[0].shape[1]
    count = refs[0].shape[0]
    for j, off in enumerate(offs):
        at = pl.multiple_of(((where ^ off) & (len(offs) - 1)) * height, height)
        dst[pl.ds(at, height), :] = refs[j // count][j % count].astype(dst.dtype)


def dot_nt(a, b):
    return lax.dot_general(a.astype(BF16), b.astype(BF16), NT, preferred_element_type=F32)


def full(x):
    zeros = (0,) * x.ndim
    return pl.BlockSpec(x.shape, lambda i, p: zeros)


def lines_of(width):
    return BF16 if width % 16 == 0 else F32


def first_panel(pos, rs0, diag, cols, owner, offs):
    rows, nb = cols.shape[1:]
    width = rs0[0].shape[1]
    members = width * len(offs)
    tm = 512

    def kernel(pos_ref, a0, b0, d_ref, c_ref, s_ref, o_ref, g0):
        i = pl.program_id(0)
        pos = pos_ref[0]
        chunk = min(512, members)

        @pl.when(i == 0)
        def _():
            collect(g0, (a0, b0), offs, pos)

            @pl.loop(0, members // chunk)
            def _(t):
                at = pl.ds(pl.multiple_of(t * chunk, chunk), chunk)
                s_ref[at, :] = dot_nt(g0[at, :], d_ref[0]).astype(BF16)

        held = jnp.logical_and(pos == 0, i * tm < nb)
        start = pl.multiple_of(jnp.where(held, i, 0) * tm, tm)

        @pl.when(held)
        def _():
            o_ref[...] = s_ref[:, pl.ds(start, tm)].astype(F32).T

        @pl.when(jnp.logical_not(held))
        def _():
            o_ref[...] = -dot_nt(c_ref[0], s_ref[...])

    return pl.pallas_call(
        kernel,
        out_shape=[
            jax.ShapeDtypeStruct((members, nb), BF16),
            jax.ShapeDtypeStruct((rows, members), F32),
        ],
        grid_spec=pltpu.PrefetchScalarGridSpec(
            num_scalar_prefetch=1,
            grid=(rows // tm,),
            in_specs=[
                full(rs0[0]),
                full(rs0[1]),
                pl.BlockSpec((1, nb, nb), lambda i, p: (0, 0, 0)),
                pl.BlockSpec((1, tm, nb), lambda i, p: (0, i, 0)),
            ],
            out_specs=[
                pl.BlockSpec((members, nb), lambda i, p: (0, 0)),
                pl.BlockSpec((tm, members), lambda i, p: (i, 0)),
            ],
            scratch_shapes=[pltpu.VMEM((members, nb), lines_of(width))],
        ),
        compiler_params=LIMIT,
        cost_estimate=FREE,
        name="first_panel",
    )(pos, *rs0, diag, cols)


def second_panel(pos, s0, rs1, block, diag, owner, offs1, offs2):
    members, nb = s0.shape
    width = rs1[0].shape[1]

    def kernel(pos_ref, s0_ref, a1, b1, a2, b2, d_ref, s_ref, g1, g2):
        pos = pos_ref[0]
        chunk = min(512, members)

        @pl.when(pos < owner)
        def _():
            s_ref[...] = jnp.zeros(s_ref.shape, BF16)

        @pl.when(pos >= owner)
        def _():
            collect(g1, (a1, b1), offs1, pos)

            @pl.when(pos & 1 == 0)
            def _():
                collect(g2, (a2,), offs2, pos >> 1)

            @pl.when(pos & 1 == 1)
            def _():
                collect(g2, (b2,), offs2, pos >> 1)

            @pl.loop(0, members // chunk)
            def _(t):
                at = pl.ds(pl.multiple_of(t * chunk, chunk), chunk)
                panel = g1[at, :].astype(F32) - dot_nt(s0_ref[at, :], g2[...])
                s_ref[at, :] = dot_nt(panel, d_ref[0]).astype(BF16)

    ins = [s0, *rs1, *block]
    return pl.pallas_call(
        kernel,
        out_shape=jax.ShapeDtypeStruct((members, nb), BF16),
        grid_spec=pltpu.PrefetchScalarGridSpec(
            num_scalar_prefetch=1,
            grid=(1,),
            in_specs=[full(x) for x in ins] + [pl.BlockSpec((1, nb, nb), lambda i, p: (1, 0, 0))],
            out_specs=pl.BlockSpec((members, nb), lambda i, p: (0, 0)),
            scratch_shapes=[
                pltpu.VMEM((members, nb), lines_of(width)),
                pltpu.VMEM((nb, nb), BF16),
            ],
        ),
        compiler_params=LIMIT,
        cost_estimate=pl.CostEstimate(
            flops=4 * members * nb * nb, bytes_accessed=12 << 20, transcendentals=0
        ),
        name="second_panel",
    )(pos, *ins, diag)


def finish(pos, v, a_t, s1, cols, owner):
    rows, members = v.shape
    nb = s1.shape[1]
    tm = 512

    def kernel(pos_ref, v_ref, a_ref, s_ref, c_ref, o_ref):
        i = pl.program_id(0)
        pos = pos_ref[0]
        panel = i * tm < nb
        kept = jnp.logical_and(pos == 0, panel)
        solved = jnp.logical_and(pos == owner, panel)

        @pl.when(kept)
        def _():
            o_ref[...] = v_ref[...]

        @pl.when(solved)
        def _():
            start = pl.multiple_of(jnp.where(solved, i, 0) * tm, tm)
            o_ref[...] = s_ref[:, pl.ds(start, tm)].astype(F32).T

        @pl.when(jnp.logical_not(jnp.logical_or(kept, solved)))
        def _():
            base = v_ref[...] + a_ref[...].T.astype(F32)

            @pl.when(pos < owner)
            def _():
                o_ref[...] = base

            @pl.when(pos >= owner)
            def _():
                o_ref[...] = base - dot_nt(c_ref[0], s_ref[...])

    def part(i, p):
        return (1, jnp.where(p[0] < owner, 0, i), 0)

    return pl.pallas_call(
        kernel,
        out_shape=jax.ShapeDtypeStruct(v.shape, F32),
        grid_spec=pltpu.PrefetchScalarGridSpec(
            num_scalar_prefetch=1,
            grid=(rows // tm,),
            in_specs=[
                pl.BlockSpec((tm, members), lambda i, p: (i, 0)),
                pl.BlockSpec((members, tm), lambda i, p: (0, i)),
                full(s1),
                pl.BlockSpec((1, tm, nb), part),
            ],
            out_specs=pl.BlockSpec((tm, members), lambda i, p: (i, 0)),
        ),
        compiler_params=LIMIT,
        cost_estimate=pl.CostEstimate(
            flops=2 * rows * members * nb, bytes_accessed=26 << 20, transcendentals=0
        ),
        name="finish",
    )(pos, v, a_t, s1, cols)


def local(right_sides, col_panels, diag_inverses):
    n = lax.axis_size("rows") * lax.axis_size("rhs")
    me = lax.axis_index(AXES).astype(jnp.int32)
    pos = me.reshape(1)
    nb = diag_inverses.shape[1]
    total_rows, width = right_sides.shape
    rows = total_rows // n
    half = n // 2
    owner = half
    x_t = right_sides.T

    def every(mask):
        return [(i, i ^ mask) for i in range(n)]

    def upper(mask):
        return [(i, i ^ mask) for i in range(half, n)]

    def even(mask):
        return [(i, i ^ mask) for i in range(half, n, 2)]

    quarter = half // 2
    both = jnp.stack([x_t[:, :nb], x_t[:, total_rows // 2 : total_rows // 2 + nb]])
    theirs = send(both, every(half))
    cur = [jnp.stack([both[k], theirs[k]]) for k in range(2)]
    offs = [[0, half], [0, half], [0]]

    chips = quarter // 2
    slots = after(col_panels[0, :nb], both).reshape(chips, nb // chips, nb)
    got = slots[0]
    for t in range(1, chips):
        here = send(slots[t], [(owner, owner + 2 * t)])
        got = jnp.where(me // 2 == owner // 2 + t, here, got)
    down = send(got, [(i, i + quarter) for i in range(owner, owner + quarter, 2)])
    cur.append(jnp.where(me >= owner + quarter, down, got)[None])

    new = (send(cur[0], every(quarter)), send(cur[1], upper(quarter)))
    new = lax.optimization_barrier(new)
    for k in range(2):
        cur[k] = jnp.concatenate([cur[k], new[k]], axis=0)
        offs[k] = offs[k] + [o ^ quarter for o in offs[k]]

    inner = [1 << k for k in range(1, quarter.bit_length() - 1)][::-1]
    orders = [inner, inner[::-1], inner]

    def phase(t, k, pairs):
        bit = orders[t][k]
        got = send(cur[t], pairs(bit))
        offs[t] = offs[t] + [o ^ (bit >> 1 if t == 2 else bit) for o in offs[t]]
        return got

    def grow(new):
        for t, got in enumerate(new):
            cur[t] = jnp.concatenate([cur[t], got], axis=0)

    new = lax.optimization_barrier((phase(0, 0, every), phase(1, 0, upper)))
    gate = [*new, cur[2]]
    grow(new)
    for k in range(1, len(inner)):
        new = (phase(0, k, every), phase(1, k, upper), phase(2, k - 1, even))
        new = lax.optimization_barrier(new)
        grow(new)
    rs0 = (cur[0], send(cur[0], every(1)))
    offs = [offs[t] + [o ^ 1 for o in offs[t]] for t in range(2)] + offs[2:]
    got = phase(2, len(inner) - 1, even)
    s0, v = first_panel(pos, rs0, diag_inverses, col_panels, owner, offs[0])
    rs1 = (cur[1], send(cur[1], upper(1)))
    last = jnp.concatenate([cur[2], after(got, s0)], axis=0)
    block = (last, send(last, [(i, i + 1) for i in range(half, n, 2)]))

    tiles = x_t.reshape(width // 8, 8, n, rows).transpose(2, 0, 1, 3)
    packed = tiles.reshape(n, width, rows)
    a_t = lax.all_to_all(after(packed, *gate), AXES, split_axis=0, concat_axis=0, tiled=True)
    a_t = a_t.reshape(n * width, rows)
    s1 = second_panel(pos, s0, rs1, block, diag_inverses, owner, offs[1], offs[2])
    return finish(pos, v, a_t, s1, col_panels, owner)


def solution(mesh):
    return jax.shard_map(
        local,
        mesh=mesh,
        in_specs=(P(None, AXES), P(None, AXES, None), P()),
        out_specs=P(AXES, None),
        check_vma=False,
    )
```

time: 163 us -> 150 us (0.920); the launches traced: 159 us -> 148 us
  starting transfers between devices: 64.8 us -> 54.9 us
  waiting for transfers between devices: 47.7 us -> 41.1 us
  local copies, waits for them, and re-layouts: 9.77 us -> 13.6 us
    all_to_all x1, starting transfers between devices: 19.8 us -> 11.2 us  [local(): lax.all_to_all(after(packed, *gate), AXES, split_axis=0, concat_axis=0, t...]
    ppermute x16, waiting for transfers between devices: 47.7 us -> 41.1 us  [send(): return lax.ppermute(x, AXES, pairs)]
    pallas_call x1, Pallas kernels: 10.6 us -> 13.2 us  [finish(): pl.pallas_call(kernel, out_shape=jax.ShapeDtypeStruct(v.shape, F32), grid...]
    unnamed x17 -> x19, local copies, waits for them, and re-layouts: 2.47 us -> 4.94 us
    pallas_call x1 -> x2, Pallas kernels: 24.9 us -> 23.7 us  [the longest x1 13.3 us: first_panel(): pl.pallas_call(kernel, out_shape=[jax.ShapeDtypeStruct((members, nb), BF1...]
  transfers between devices with their start and end apart: 17 -> 17, of which waited for: 7 -> 6; matrix products, arithmetic and copies ran while one was open for 5% -> 8% of each run, Pallas kernels for 16% -> 16%
where the time goes in v4:
time: 150 us; the launch traced here: 148 us
  starting transfers between devices  54.9 us (37%)
  waiting for transfers between devices  41.1 us (27%)
  Pallas kernels  36.9 us (25%)
  local copies, waits for them, and re-layouts  13.6 us (9%)
  other arithmetic  1.72 us (1%)
    ppermute x16, starting transfers between devices, send(): return lax.ppermute(x, AXES, pairs)  43.7 us
    ppermute x16, waiting for transfers between devices, send(): return lax.ppermute(x, AXES, pairs)  41.1 us
    pallas_call x1, Pallas kernels, first_panel(): pl.pallas_call(kernel, out_shape=[jax.ShapeDtypeStruct((members, nb), BF1...  13.3 us
    pallas_call x1, Pallas kernels, finish(): pl.pallas_call(kernel, out_shape=jax.ShapeDtypeStruct(v.shape, F32), grid...  13.2 us
    all_to_all x1, starting transfers between devices, local(): lax.all_to_all(after(packed, *gate), AXES, split_axis=0, concat_axis=0, t...  11.2 us
    pallas_call x1, Pallas kernels, second_panel(): pl.pallas_call(kernel, out_shape=jax.ShapeDtypeStruct((members, nb), BF16...  10.4 us
    unnamed x19, local copies, waits for them, and re-layouts  4.94 us
    transpose x1, local copies, waits for them, and re-layouts, local(): tiles = x_t.reshape(width // 8, 8, n, rows).transpose(2, 0, 1, 3)  4.79 us
  transfers between devices with their start and end apart: 17, of which 6 were waited for; matrix products, arithmetic and copies ran while one was open for 8% of the time, Pallas kernels for 16%

profile of v4, /device:TPU:21, one launch (start us, length us, event | category | flops | bytes accessed | tf_op | source)
XLA Modules:
  0.0 148.5 jit_solution(8763471263236030084)
XLA Ops:
  0.0 0.9 slice_bitcast_fusion.1
  1.0 1.8 %slice_bitcast_fusion = bf16[1024,1024]{1,0:T(8,128)(2,1)S(1)} fusion(bf16[2,2048,1024]{2,1,0:T(8,128)(2,1)} %c_ref.3), kind=kLoop, calls=%fused_computation.2 | loop fusion | bytes 4194304 | tf_op jit(solution)/shard_map/squeeze | solution.py:240
  2.8 1.1 fusion
  3.9 1.5 collective-permute-start.9
  5.4 1.5 collective-permute-start.8
  6.9 1.5 collective-permute-start.7
  8.3 1.5 %constant_dynamic-update-slice_fusion.9 = (bf16[16,32,1024]{2,1,0:T(8,128)(2,1)}, bf16[16,32,1024]{2,1,0:T(8,128)(2,1)}) fusion(bf16[32,65536]{1,0:T(8,128)(2,1)} %bitcast.24), kind=kLoop, calls=%fused_computation.24 | loop fusion | bytes 262144
  9.9 0.7 constant_dynamic-update-slice_fusion.8
  10.6 1.5 collective-permute-start.1
  12.1 2.0 %collective-permute-start.2 = (bf16[2,32,1024]{2,1,0:T(8,128)(2,1)S(1)}, bf16[2,32,1024]{2,1,0:T(8,128)(2,1)S(1)}, u32[]{:S(2)}, u32[]{:S(2)}) collective-permute-start(bf16[2,32,1024]{2,1,0:T(8,128)(2,1)S(1)} %pad_maximum_fusion.8), channel_id=1, source_target_pairs={{16,24},{17,25},{18,26},{19,27},{20,28},{21,29},{22,30},{23,31},{2... | collective-permute-start | bytes 393224 | tf_op jit(solution)/shard_map/ppermute | solution.py:17
  14.1 1.2 select_select_fusion
  15.2 0.7 collective-permute-start.10
  16.0 2.0 %collective-permute-done.2 = bf16[2,32,1024]{2,1,0:T(8,128)(2,1)S(1)} collective-permute-done((bf16[2,32,1024]{2,1,0:T(8,128)(2,1)S(1)}, bf16[2,32,1024]{2,1,0:T(8,128)(2,1)S(1)}, u32[]{:S(2)}, u32[]{:S(2)}) %collective-permute-start.2) | collective-permute-done | bytes 131104 | tf_op jit(solution)/shard_map/ppermute | solution.py:17
  18.0 3.4 %collective-permute-start.4 = (bf16[4,32,1024]{2,1,0:T(8,128)(2,1)S(1)}, bf16[4,32,1024]{2,1,0:T(8,128)(2,1)S(1)}, u32[]{:S(2)}, u32[]{:S(2)}) collective-permute-start(bf16[4,32,1024]{2,1,0:T(8,128)(2,1)S(1)} %pad_maximum_fusion.5), channel_id=1, source_target_pairs={{16,18},{17,19},{18,16},{19,17},{20,22},{21,23},{22,20},{23,21},{2... | collective-permute-start | bytes 786440 | tf_op jit(solution)/shard_map/ppermute | solution.py:17
  21.5 4.8 %copy.6 = bf16[32,4,8,2048]{3,2,1,0:T(8,128)(2,1)} copy(bf16[32,4,8,2048]{3,2,0,1:T(8,128)(2,1)} %bitcast.25) | data formatting | bytes 8388608 | tf_op jit(solution)/shard_map/transpose | solution.py:282
  26.7 11.2 %all-to-all-start = ((bf16[32,32,2048]{2,1,0:T(8,128)(2,1)}), bf16[32,32,2048]{2,1,0:T(8,128)(2,1)}, u32[]{:S(2)}, u32[]{:S(2)}) async-start(bf16[32,32,2048]{2,1,0:T(8,128)(2,1)} %bitcast.22), calls=%async_computation | async-start | bytes 8388608 | tf_op jit(solution)/shard_map/all_to_all | solution.py:284
  38.1 2.3 %collective-permute-start.6 = (bf16[8,32,1024]{2,1,0:T(8,128)(2,1)S(1)}, bf16[8,32,1024]{2,1,0:T(8,128)(2,1)S(1)}, u32[]{:S(2)}, u32[]{:S(2)}) collective-permute-start(bf16[8,32,1024]{2,1,0:T(8,128)(2,1)S(1)} %pad_maximum_fusion.3), channel_id=1, source_target_pairs={{16,20},{17,21},{18,22},{19,23},{20,16},{21,17},{22,18},{23,19},{2... | collective-permute-start | bytes 1572872 | tf_op jit(solution)/shard_map/ppermute | solution.py:17
  40.4 1.2 collective-permute-start.5
  41.6 0.7 collective-permute-start.11
  42.3 0.7 constant_dynamic-update-slice_fusion.2
  43.0 34.5 %collective-permute-done.6 = bf16[8,32,1024]{2,1,0:T(8,128)(2,1)S(1)} collective-permute-done((bf16[8,32,1024]{2,1,0:T(8,128)(2,1)S(1)}, bf16[8,32,1024]{2,1,0:T(8,128)(2,1)S(1)}, u32[]{:S(2)}, u32[]{:S(2)}) %collective-permute-start.6) | collective-permute-done | bytes 524320 | tf_op jit(solution)/shard_map/ppermute | solution.py:17
  78.1 10.2 %collective-permute-start.12 = (bf16[16,32,1024]{2,1,0:T(8,128)(2,1)S(1)}, bf16[16,32,1024]{2,1,0:T(8,128)(2,1)S(1)}, u32[]{:S(2)}, u32[]{:S(2)}) collective-permute-start(bf16[16,32,1024]{2,1,0:T(8,128)(2,1)S(1)} %constant_dynamic-update-slice_fusion.a0), channel_id=1, source_target_pairs={{0,1},{1,0},{2,3},{3,2},{4,5},{5,4},{6,7},{7,6},{8,9},{9,8},{10,11... | collective-permute-start | bytes 3145736 | tf_op jit(solution)/shard_map/ppermute | solution.py:17
  88.4 0.7 collective-permute-start.14
  89.2 1.5 collective-permute-done.12.b0
  90.6 1.0 copy-done.3
  91.6 13.3 %first_panel.1 = (bf16[1024,1024]{1,0:T(8,128)(2,1)}, f32[2048,1024]{1,0:T(8,128)}) custom-call(s32[1]{0:T(128)} %bitcast.pos_ref, bf16[16,32,1024]{2,1,0:T(8,128)(2,1)} %copy-done.2, bf16[16,32,1024]{2,1,0:T(8,128)(2,1)} %copy-done.3, bf16[2,1024,1024]{2,1,0:T(8,128)(2,1)} %d_ref.3, bf16[2,2048,1024]{2,1,0:T(8,128)(2,1)} %c_ref.3), custom_call_target="tpu_custom_call" | custom-call | tf_op jit(solution)/shard_map/first_panel/pallas_call | solution.py:76
  105.1 1.4 collective-permute-start.15
  106.6 14.9 %collective-permute-start.13 = (bf16[16,32,1024]{2,1,0:T(8,128)(2,1)S(1)}, bf16[16,32,1024]{2,1,0:T(8,128)(2,1)S(1)}, u32[]{:S(2)}, u32[]{:S(2)}) collective-permute-start(bf16[16,32,1024]{2,1,0:T(8,128)(2,1)S(1)} %constant_dynamic-update-slice_fusion.5.a1), channel_id=1, source_target_pairs={{16,17},{17,16},{18,19},{19,18},{20,21},{21,20},{22,23},{23,22},{2... | collective-permute-start | bytes 3145736 | tf_op jit(solution)/shard_map/ppermute | solution.py:17
  121.6 2.3 %collective-permute-done.13.b1 = bf16[16,32,1024]{2,1,0:T(8,128)(2,1)S(1)} collective-permute-done((bf16[16,32,1024]{2,1,0:T(8,128)(2,1)S(1)}, bf16[16,32,1024]{2,1,0:T(8,128)(2,1)S(1)}, u32[]{:S(2)}, u32[]{:S(2)}) %collective-permute-start.13) | collective-permute-done | bytes 1048608 | tf_op jit(solution)/shard_map/ppermute | solution.py:17
  123.9 1.0 copy-done.6
  124.8 10.4 %second_panel.1.s_ref = bf16[1024,1024]{1,0:T(8,128)(2,1)} custom-call(s32[1]{0:T(128)} %bitcast.pos_ref, bf16[1024,1024]{1,0:T(8,128)(2,1)} %get-tuple-element.25.s0_ref, bf16[16,32,1024]{2,1,0:T(8,128)(2,1)} %copy-done.5, bf16[16,32,1024]{2,1,0:T(8,128)(2,1)} %copy-done.6, bf16[4,256,1024]{2,1,0:T(8,128)(2,1)} %copy-done, ...), custom_call_target="tpu_custom_call" | custom-call | flops 4294967296 | bytes 12582912 | tf_op jit(solution)/shard_map/second_panel/pallas_call | solution.py:134
  135.3 13.2 %finish.1 = f32[2048,1024]{1,0:T(8,128)} custom-call(s32[1]{0:T(128)} %bitcast.pos_ref, f32[2048,1024]{1,0:T(8,128)} %get-tuple-element.23.v_ref, bf16[1024,2048]{1,0:T(8,128)(2,1)} %bitcast.9.a_ref, bf16[1024,1024]{1,0:T(8,128)(2,1)} %second_panel.1.s_ref, bf16[2,2048,1024]{2,1,0:T(8,128)(2,1)} %c_ref.3), custom_call_target="tpu_custom_call" | custom-call | flops 4294967296 | bytes 27262976 | tf_op jit(solution)/shard_map/finish/pallas_call | solution.py:191
  (41 shorter events, 1.8 us)
Async XLA Ops:
  0.9 9.0 %collective-permute-start = (bf16[2,32,1024]{2,1,0:T(8,128)(2,1)S(1)}, bf16[2,32,1024]{2,1,0:T(8,128)(2,1)S(1)}, u32[]{:S(2)}, u32[]{:S(2)}) collective-permute-start(bf16[2,32,1024]{2,1,0:T(8,128)(2,1)S(1)} %pad_maximum_fusion.7), channel_id=1, source_target_pairs={{0,16},{1,17},{2,18},{3,19},{4,20},{5,21},{6,22},{7,23},{8,24},{9,... | collective-permute-start | bytes 393224 | tf_op jit(solution)/shard_map/ppermute | solution.py:17
  3.9 10.2 %collective-permute-start.9 = (bf16[256,1024]{1,0:T(8,128)(2,1)}, bf16[256,1024]{1,0:T(8,128)(2,1)}, u32[]{:S(2)}, u32[]{:S(2)}) collective-permute-start(bf16[256,1024]{1,0:T(8,128)(2,1)} %get-tuple-element.33), channel_id=1, source_target_pairs={{16,18}} | collective-permute-start | bytes 1572872 | tf_op jit(solution)/shard_map/ppermute | solution.py:17
  5.4 8.7 %collective-permute-start.8 = (bf16[256,1024]{1,0:T(8,128)(2,1)}, bf16[256,1024]{1,0:T(8,128)(2,1)}, u32[]{:S(2)}, u32[]{:S(2)}) collective-permute-start(bf16[256,1024]{1,0:T(8,128)(2,1)} %get-tuple-element.34), channel_id=1, source_target_pairs={{16,20}} | collective-permute-start | bytes 1572872 | tf_op jit(solution)/shard_map/ppermute | solution.py:17
  6.9 7.2 %collective-permute-start.7 = (bf16[256,1024]{1,0:T(8,128)(2,1)S(1)}, bf16[256,1024]{1,0:T(8,128)(2,1)}, u32[]{:S(2)}, u32[]{:S(2)}) collective-permute-start(bf16[256,1024]{1,0:T(8,128)(2,1)S(1)} %get-tuple-element.35), channel_id=1, source_target_pairs={{16,22}} | collective-permute-start | bytes 1572872 | tf_op jit(solution)/shard_map/ppermute | solution.py:17
  10.6 5.4 %collective-permute-start.1 = (bf16[2,32,1024]{2,1,0:T(8,128)(2,1)S(1)}, bf16[2,32,1024]{2,1,0:T(8,128)(2,1)S(1)}, u32[]{:S(2)}, u32[]{:S(2)}) collective-permute-start(bf16[2,32,1024]{2,1,0:T(8,128)(2,1)S(1)} %pad_maximum_fusion.6), channel_id=1, source_target_pairs={{0,8},{1,9},{2,10},{3,11},{4,12},{5,13},{6,14},{7,15},{8,0},{9,1},... | collective-permute-start | bytes 393224 | tf_op jit(solution)/shard_map/ppermute | solution.py:17
  12.1 5.8 %collective-permute-start.2 = (bf16[2,32,1024]{2,1,0:T(8,128)(2,1)S(1)}, bf16[2,32,1024]{2,1,0:T(8,128)(2,1)S(1)}, u32[]{:S(2)}, u32[]{:S(2)}) collective-permute-start(bf16[2,32,1024]{2,1,0:T(8,128)(2,1)S(1)} %pad_maximum_fusion.8), channel_id=1, source_target_pairs={{16,24},{17,25},{18,26},{19,27},{20,28},{21,29},{22,30},{23,31},{2... | collective-permute-start | bytes 393224 | tf_op jit(solution)/shard_map/ppermute | solution.py:17
  15.2 11.4 %collective-permute-start.10 = (bf16[256,1024]{1,0:T(8,128)(2,1)S(1)}, bf16[256,1024]{1,0:T(8,128)(2,1)S(1)}, u32[]{:S(2)}, u32[]{:S(2)}) collective-permute-start(bf16[256,1024]{1,0:T(8,128)(2,1)S(1)} %select_select_fusion), channel_id=1, source_target_pairs={{16,24},{18,26},{20,28},{22,30}} | collective-permute-start | bytes 1572872 | tf_op jit(solution)/shard_map/ppermute | solution.py:17
  18.0 8.3 %collective-permute-start.4 = (bf16[4,32,1024]{2,1,0:T(8,128)(2,1)S(1)}, bf16[4,32,1024]{2,1,0:T(8,128)(2,1)S(1)}, u32[]{:S(2)}, u32[]{:S(2)}) collective-permute-start(bf16[4,32,1024]{2,1,0:T(8,128)(2,1)S(1)} %pad_maximum_fusion.5), channel_id=1, source_target_pairs={{16,18},{17,19},{18,16},{19,17},{20,22},{21,23},{22,20},{23,21},{2... | collective-permute-start | bytes 786440 | tf_op jit(solution)/shard_map/ppermute | solution.py:17
  21.4 5.3 %collective-permute-start.3 = (bf16[4,32,1024]{2,1,0:T(8,128)(2,1)S(1)}, bf16[4,32,1024]{2,1,0:T(8,128)(2,1)S(1)}, u32[]{:S(2)}, u32[]{:S(2)}) collective-permute-start(bf16[4,32,1024]{2,1,0:T(8,128)(2,1)S(1)} %pad_maximum_fusion.4), channel_id=1, source_target_pairs={{0,4},{1,5},{2,6},{3,7},{4,0},{5,1},{6,2},{7,3},{8,12},{9,13},{10,... | collective-permute-start | bytes 786440 | tf_op jit(solution)/shard_map/ppermute | solution.py:17
  26.7 108.5 %all-to-all-start = ((bf16[32,32,2048]{2,1,0:T(8,128)(2,1)}), bf16[32,32,2048]{2,1,0:T(8,128)(2,1)}, u32[]{:S(2)}, u32[]{:S(2)}) async-start(bf16[32,32,2048]{2,1,0:T(8,128)(2,1)} %bitcast.22), calls=%async_computation | async-start | bytes 8388608 | tf_op jit(solution)/shard_map/all_to_all | solution.py:284
  37.9 4.4 %copy-start.1 = (bf16[16,32,1024]{2,1,0:T(8,128)(2,1)S(1)}, bf16[16,32,1024]{2,1,0:T(8,128)(2,1)}, u32[]{:S(2)}) copy-start(bf16[16,32,1024]{2,1,0:T(8,128)(2,1)} %get-tuple-element.37) | copy-start | bytes 3145732
  38.1 39.5 %collective-permute-start.6 = (bf16[8,32,1024]{2,1,0:T(8,128)(2,1)S(1)}, bf16[8,32,1024]{2,1,0:T(8,128)(2,1)S(1)}, u32[]{:S(2)}, u32[]{:S(2)}) collective-permute-start(bf16[8,32,1024]{2,1,0:T(8,128)(2,1)S(1)} %pad_maximum_fusion.3), channel_id=1, source_target_pairs={{16,20},{17,21},{18,22},{19,23},{20,16},{21,17},{22,18},{23,19},{2... | collective-permute-start | bytes 1572872 | tf_op jit(solution)/shard_map/ppermute | solution.py:17
  40.4 37.6 %collective-permute-start.5 = (bf16[8,32,1024]{2,1,0:T(8,128)(2,1)S(1)}, bf16[8,32,1024]{2,1,0:T(8,128)(2,1)S(1)}, u32[]{:S(2)}, u32[]{:S(2)}) collective-permute-start(bf16[8,32,1024]{2,1,0:T(8,128)(2,1)S(1)} %pad_maximum_fusion.2), channel_id=1, source_target_pairs={{0,2},{1,3},{2,0},{3,1},{4,6},{5,7},{6,4},{7,5},{8,10},{9,11},{10,... | collective-permute-start | bytes 1572872 | tf_op jit(solution)/shard_map/ppermute | solution.py:17
  41.6 36.4 %collective-permute-start.11 = (bf16[1,256,1024]{2,1,0:T(8,128)(2,1)S(1)}, bf16[1,256,1024]{2,1,0:T(8,128)(2,1)S(1)}, u32[]{:S(2)}, u32[]{:S(2)}) collective-permute-start(bf16[1,256,1024]{2,1,0:T(8,128)(2,1)S(1)} %select_bitcast_fusion), channel_id=1, source_target_pairs={{16,20},{18,22},{20,16},{22,18},{24,28},{26,30},{28,24},{30,26}} | collective-permute-start | bytes 1572872 | tf_op jit(solution)/shard_map/ppermute | solution.py:17
  78.1 12.5 %copy-start.2 = (bf16[16,32,1024]{2,1,0:T(8,128)(2,1)}, bf16[16,32,1024]{2,1,0:T(8,128)(2,1)S(1)}, u32[]{:S(2)}) copy-start(bf16[16,32,1024]{2,1,0:T(8,128)(2,1)S(1)} %constant_dynamic-update-slice_fusion.a0) | copy-start | bytes 3145732
  78.1 12.5 %collective-permute-start.12 = (bf16[16,32,1024]{2,1,0:T(8,128)(2,1)S(1)}, bf16[16,32,1024]{2,1,0:T(8,128)(2,1)S(1)}, u32[]{:S(2)}, u32[]{:S(2)}) collective-permute-start(bf16[16,32,1024]{2,1,0:T(8,128)(2,1)S(1)} %constant_dynamic-update-slice_fusion.a0), channel_id=1, source_target_pairs={{0,1},{1,0},{2,3},{3,2},{4,5},{5,4},{6,7},{7,6},{8,9},{9,8},{10,11... | collective-permute-start | bytes 3145736 | tf_op jit(solution)/shard_map/ppermute | solution.py:17
  88.4 16.4 %collective-permute-start.14 = (bf16[2,256,1024]{2,1,0:T(8,128)(2,1)S(1)}, bf16[2,256,1024]{2,1,0:T(8,128)(2,1)S(1)}, u32[]{:S(2)}, u32[]{:S(2)}) collective-permute-start(bf16[2,256,1024]{2,1,0:T(8,128)(2,1)S(1)} %pad_maximum_fusion.1), channel_id=1, source_target_pairs={{16,18},{18,16},{20,22},{22,20},{24,26},{26,24},{28,30},{30,28}} | collective-permute-start | bytes 3145736 | tf_op jit(solution)/shard_map/ppermute | solution.py:17
  90.6 1.0 copy-start.3
  104.9 1.7 %copy-start.4 = (bf16[16,32,1024]{2,1,0:T(8,128)(2,1)S(1)}, bf16[16,32,1024]{2,1,0:T(8,128)(2,1)}, u32[]{:S(2)}) copy-start(bf16[16,32,1024]{2,1,0:T(8,128)(2,1)} %get-tuple-element.41) | copy-start | bytes 3145732
  105.1 18.8 %copy-start = (bf16[4,256,1024]{2,1,0:T(8,128)(2,1)}, bf16[4,256,1024]{2,1,0:T(8,128)(2,1)S(1)}, u32[]{:S(2)}) copy-start(bf16[4,256,1024]{2,1,0:T(8,128)(2,1)S(1)} %pad_maximum_fusion.a2) | copy-start | bytes 6291460
  105.1 18.7 %collective-permute-start.15 = (bf16[4,256,1024]{2,1,0:T(8,128)(2,1)S(1)}, bf16[4,256,1024]{2,1,0:T(8,128)(2,1)}, u32[]{:S(2)}, u32[]{:S(2)}) collective-permute-start(bf16[4,256,1024]{2,1,0:T(8,128)(2,1)S(1)} %pad_maximum_fusion.a2), channel_id=1, source_target_pairs={{16,17},{18,19},{20,21},{22,23},{24,25},{26,27},{28,29},{30,31}} | collective-permute-start | bytes 6291464 | tf_op jit(solution)/shard_map/ppermute | solution.py:17
  106.6 17.2 %copy-start.5 = (bf16[16,32,1024]{2,1,0:T(8,128)(2,1)}, bf16[16,32,1024]{2,1,0:T(8,128)(2,1)S(1)}, u32[]{:S(2)}) copy-start(bf16[16,32,1024]{2,1,0:T(8,128)(2,1)S(1)} %constant_dynamic-update-slice_fusion.5.a1) | copy-start | bytes 3145732
  106.6 17.2 %collective-permute-start.13 = (bf16[16,32,1024]{2,1,0:T(8,128)(2,1)S(1)}, bf16[16,32,1024]{2,1,0:T(8,128)(2,1)S(1)}, u32[]{:S(2)}, u32[]{:S(2)}) collective-permute-start(bf16[16,32,1024]{2,1,0:T(8,128)(2,1)S(1)} %constant_dynamic-update-slice_fusion.5.a1), channel_id=1, source_target_pairs={{16,17},{17,16},{18,19},{19,18},{20,21},{21,20},{22,23},{23,22},{2... | collective-permute-start | bytes 3145736 | tf_op jit(solution)/shard_map/ppermute | solution.py:17
  123.9 1.0 copy-start.6

commit v5 on v3

--- a/solution.py
+++ b/solution.py
@@ -127,16 +127,11 @@
 
 def finish(pos, v, a_t, owner, nb):
     rows, members = v.shape
-    tm = 256
+    tm = 512
 
     def kernel(pos_ref, v_ref, a_ref, o_ref):
         held = held_rows(tm, pos_ref[0], pl.program_id(0), owner, nb)
-        row = lax.broadcasted_iota(jnp.int32, (tm, tm), 0)
-        col = lax.broadcasted_iota(jnp.int32, (tm, tm), 1)
-        keep = jnp.logical_and(row == col, jnp.logical_not(held))
-        pick = jnp.where(keep, 1.0, 0.0).astype(BF16)
-        turned = lax.dot_general(pick, a_ref[...], NT, preferred_element_type=F32)
-        o_ref[...] = v_ref[...] + turned
+        o_ref[...] = v_ref[...] + jnp.where(held, 0.0, a_ref[...].T.astype(F32))
 
     return pl.pallas_call(
         kernel,
@@ -184,7 +179,7 @@
     offs = [[0, half], [0, half], [0]]
 
     chips = quarter // 2
-    slots = col_panels[0, :nb].reshape(chips, nb // chips, nb)
+    slots = after(col_panels[0, :nb], both).reshape(chips, nb // chips, nb)
     got = slots[0]
     for t in range(1, chips):
         here = send(slots[t], [(owner, owner + 2 * t)])
@@ -192,37 +187,51 @@
     down = send(got, [(i, i + quarter) for i in range(owner, owner + quarter, 2)])
     cur.append(jnp.where(me >= owner + quarter, down, got)[None])
 
-    new = [send(cur[0], every(quarter)), send(cur[1], upper(quarter))]
+    new = (send(cur[0], every(quarter)), send(cur[1], upper(quarter)))
+    new = lax.optimization_barrier(new)
     for k in range(2):
         cur[k] = jnp.concatenate([cur[k], new[k]], axis=0)
         offs[k] = offs[k] + [o ^ quarter for o in offs[k]]
-    cur = list(lax.optimization_barrier(tuple(cur)))
 
     inner = [1 << k for k in range(1, quarter.bit_length() - 1)][::-1]
-    orders = [inner, inner[::-1], inner]
-    pairs = [every, upper, even]
-    for k in range(len(inner)):
-        bits = [order[k] for order in orders]
-        new = [send(cur[t], pairs[t](bits[t])) for t in range(3)]
-        new = lax.optimization_barrier(tuple(new))
+    orders = [inner, inner[::-1]]
+    pairs = [every, upper]
+
+    def phase(t, k):
+        bit = orders[t][k]
+        offs[t] = offs[t] + [o ^ bit for o in offs[t]]
+        return send(cur[t], pairs[t](bit))
+
+    def grow(new):
+        for t, got in enumerate(new):
+            cur[t] = jnp.concatenate([cur[t], *got], axis=0)
+
+    last = len(inner) - 1
+    for k in range(last):
+        new = [[phase(0, k)], [phase(1, k)]]
+        if k < last - 1:
+            new.append([send(cur[2], even(inner[k]))])
+            offs[2] = offs[2] + [o ^ (inner[k] >> 1) for o in offs[2]]
+        new = lax.optimization_barrier(new)
         if k == 0:
-            gate = new
-        shifts = [bits[0], bits[1], bits[2] >> 1]
-        offs = [offs[t] + [o ^ shifts[t] for o in offs[t]] for t in range(3)]
-        cur = [jnp.concatenate([cur[t], new[t]], axis=0) for t in range(3)]
-    new = [
-        send(cur[0], every(1)),
-        send(cur[1], upper(1)),
-        send(cur[2], [(i, i + 1) for i in range(half, n, 2)]),
-    ]
-    ends = [(cur[t], new[t]) for t in range(3)]
-    offs = [offs[t] + [o ^ 1 for o in offs[t]] for t in range(2)] + [offs[2]]
+            gate = [*new, cur[2]]
+        grow(new)
+    ends = [inner[-1] ^ inner[-2], inner[-1], inner[-2]]
+    new = [[phase(0, last)], [phase(1, last)], [send(cur[2], even(m)) for m in ends]]
+    offs[2] = offs[2] + [o ^ (m >> 1) for m in ends for o in offs[2]]
+    grow(lax.optimization_barrier(new))
+    rs0 = (cur[0], send(cur[0], every(1)))
+    rs1 = (cur[1], send(cur[1], upper(1)))
+    block = (cur[2], send(cur[2], [(i, i + 1) for i in range(half, n, 2)]))
+    offs = [offs[t] + [o ^ 1 for o in offs[t]] for t in range(2)] + offs[2:]
 
     tiles = x_t.reshape(width // 8, 8, n, rows).transpose(2, 0, 1, 3)
     packed = tiles.reshape(n, width, rows)
-    a_t = lax.all_to_all(after(packed, *gate), AXES, split_axis=0, concat_axis=0, tiled=True)
+    a_t = lax.all_to_all(after(packed, gate), AXES, split_axis=0, concat_axis=0, tiled=True)
     a_t = a_t.reshape(n * width, rows)
-    v = solve_update(pos, *ends, diag_inverses, col_panels, owner, half, *offs)
+    v = solve_update(
+        pos, rs0, rs1, block, diag_inverses, col_panels, owner, half, *offs
+    )
     return finish(pos, v, a_t, owner, nb)
 
 

time: 163 us -> 149 us (0.914); the launches traced: 159 us -> 148 us
  waiting for transfers between devices: 47.7 us -> 40.5 us
  starting transfers between devices: 64.8 us -> 58.8 us
  local copies, waits for them, and re-layouts: 9.77 us -> 13.5 us
  Pallas kernels: 35.5 us -> 33.3 us
    all_to_all x1, starting transfers between devices: 19.8 us -> 11.2 us  [local(): lax.all_to_all(after(packed, gate), AXES, split_axis=0, concat_axis=0, ti...]
    ppermute x16 -> x17, waiting for transfers between devices: 47.7 us -> 40.5 us  [send(): return lax.ppermute(x, AXES, pairs)]
    ppermute x16 -> x17, starting transfers between devices: 44.9 us -> 47.6 us  [send(): return lax.ppermute(x, AXES, pairs)]
    unnamed x17 -> x23, local copies, waits for them, and re-layouts: 2.47 us -> 4.75 us
    pallas_call x1, Pallas kernels: 10.6 us -> 8.52 us  [finish(): pl.pallas_call(kernel, out_shape=jax.ShapeDtypeStruct(v.shape, F32), grid...]
  transfers between devices with their start and end apart: 17 -> 18, of which waited for: 7 -> 6; matrix products, arithmetic and copies ran while one was open for 5% -> 8% of each run, Pallas kernels for 16% -> 17%
where the time goes in v5:
time: 149 us; the launch traced here: 148 us
  starting transfers between devices  58.8 us (39%)
  waiting for transfers between devices  40.5 us (27%)
  Pallas kernels  33.3 us (22%)
  local copies, waits for them, and re-layouts  13.5 us (9%)
  other arithmetic  1.67 us (1%)
    ppermute x17, starting transfers between devices, send(): return lax.ppermute(x, AXES, pairs)  47.6 us
    ppermute x17, waiting for transfers between devices, send(): return lax.ppermute(x, AXES, pairs)  40.5 us
    pallas_call x1, Pallas kernels, solve_update(): pl.pallas_call(kernel, out_shape=jax.ShapeDtypeStruct((rows, members), F3...  24.8 us
    all_to_all x1, starting transfers between devices, local(): lax.all_to_all(after(packed, gate), AXES, split_axis=0, concat_axis=0, ti...  11.2 us
    pallas_call x1, Pallas kernels, finish(): pl.pallas_call(kernel, out_shape=jax.ShapeDtypeStruct(v.shape, F32), grid...  8.52 us
    transpose x1, local copies, waits for them, and re-layouts, local(): tiles = x_t.reshape(width // 8, 8, n, rows).transpose(2, 0, 1, 3)  4.79 us
    unnamed x23, local copies, waits for them, and re-layouts  4.75 us
  transfers between devices with their start and end apart: 18, of which 6 were waited for; matrix products, arithmetic and copies ran while one was open for 8% of the time, Pallas kernels for 17%

profile of v5, /device:TPU:21, one launch (start us, length us, event | category | flops | bytes accessed | tf_op | source)
XLA Modules:
  0.0 148.0 jit_solution(5592799526975510098)
XLA Ops:
  0.0 0.9 slice_bitcast_fusion.1
  1.0 1.8 %slice_bitcast_fusion = bf16[1024,1024]{1,0:T(8,128)(2,1)S(1)} fusion(bf16[2,2048,1024]{2,1,0:T(8,128)(2,1)} %c_ref.1), kind=kLoop, calls=%fused_computation.2 | loop fusion | bytes 4194304 | tf_op jit(solution)/shard_map/squeeze | solution.py:182
  2.8 1.2 fusion
  4.0 0.7 collective-permute-start.9
  4.7 1.5 collective-permute-start.8
  6.1 1.5 collective-permute-start.7
  7.6 1.5 %constant_dynamic-update-slice_fusion.9 = (bf16[16,32,1024]{2,1,0:T(8,128)(2,1)}, bf16[16,32,1024]{2,1,0:T(8,128)(2,1)}) fusion(bf16[32,65536]{1,0:T(8,128)(2,1)} %bitcast.24), kind=kLoop, calls=%fused_computation.23 | loop fusion | bytes 262144
  9.1 0.7 constant_dynamic-update-slice_fusion.8
  9.8 2.2 %collective-permute-start.1 = (bf16[2,32,1024]{2,1,0:T(8,128)(2,1)S(1)}, bf16[2,32,1024]{2,1,0:T(8,128)(2,1)S(1)}, u32[]{:S(2)}, u32[]{:S(2)}) collective-permute-start(bf16[2,32,1024]{2,1,0:T(8,128)(2,1)S(1)} %pad_maximum_fusion.5), channel_id=1, source_target_pairs={{0,8},{1,9},{2,10},{3,11},{4,12},{5,13},{6,14},{7,15},{8,0},{9,1},... | collective-permute-start | bytes 393224 | tf_op jit(solution)/shard_map/ppermute | solution.py:18
  12.1 1.9 %collective-permute-start.2 = (bf16[2,32,1024]{2,1,0:T(8,128)(2,1)S(1)}, bf16[2,32,1024]{2,1,0:T(8,128)(2,1)S(1)}, u32[]{:S(2)}, u32[]{:S(2)}) collective-permute-start(bf16[2,32,1024]{2,1,0:T(8,128)(2,1)S(1)} %pad_maximum_fusion.7), channel_id=1, source_target_pairs={{16,24},{17,25},{18,26},{19,27},{20,28},{21,29},{22,30},{23,31},{2... | collective-permute-start | bytes 393224 | tf_op jit(solution)/shard_map/ppermute | solution.py:18
  14.0 0.8 copy-done.1
  14.8 1.1 select_select_fusion
  16.0 0.7 collective-permute-start.10
  16.7 1.5 %collective-permute-done.2 = bf16[2,32,1024]{2,1,0:T(8,128)(2,1)S(1)} collective-permute-done((bf16[2,32,1024]{2,1,0:T(8,128)(2,1)S(1)}, bf16[2,32,1024]{2,1,0:T(8,128)(2,1)S(1)}, u32[]{:S(2)}, u32[]{:S(2)}) %collective-permute-start.2) | collective-permute-done | bytes 131104 | tf_op jit(solution)/shard_map/ppermute | solution.py:18
  18.3 3.2 %collective-permute-start.4 = (bf16[4,32,1024]{2,1,0:T(8,128)(2,1)S(1)}, bf16[4,32,1024]{2,1,0:T(8,128)(2,1)S(1)}, u32[]{:S(2)}, u32[]{:S(2)}) collective-permute-start(bf16[4,32,1024]{2,1,0:T(8,128)(2,1)S(1)} %pad_maximum_fusion.4), channel_id=1, source_target_pairs={{16,18},{17,19},{18,16},{19,17},{20,22},{21,23},{22,20},{23,21},{2... | collective-permute-start | bytes 786440 | tf_op jit(solution)/shard_map/ppermute | solution.py:18
  21.7 4.8 %copy.7 = bf16[32,4,8,2048]{3,2,1,0:T(8,128)(2,1)} copy(bf16[32,4,8,2048]{3,2,0,1:T(8,128)(2,1)} %bitcast.25) | data formatting | bytes 8388608 | tf_op jit(solution)/shard_map/transpose | solution.py:228
  26.5 0.3 collective-permute-done.3
  26.9 11.2 %all-to-all-start = ((bf16[32,32,2048]{2,1,0:T(8,128)(2,1)}), bf16[32,32,2048]{2,1,0:T(8,128)(2,1)}, u32[]{:S(2)}, u32[]{:S(2)}) async-start(bf16[32,32,2048]{2,1,0:T(8,128)(2,1)} %bitcast.22), calls=%async_computation | async-start | bytes 8388608 | tf_op jit(solution)/shard_map/all_to_all | solution.py:230
  38.2 2.3 %collective-permute-start.6 = (bf16[8,32,1024]{2,1,0:T(8,128)(2,1)S(1)}, bf16[8,32,1024]{2,1,0:T(8,128)(2,1)S(1)}, u32[]{:S(2)}, u32[]{:S(2)}) collective-permute-start(bf16[8,32,1024]{2,1,0:T(8,128)(2,1)S(1)} %pad_maximum_fusion.2), channel_id=1, source_target_pairs={{16,20},{17,21},{18,22},{19,23},{20,16},{21,17},{22,18},{23,19},{2... | collective-permute-start | bytes 1572872 | tf_op jit(solution)/shard_map/ppermute | solution.py:18
  40.5 1.2 collective-permute-start.5
  41.7 0.7 collective-permute-start.13
  42.4 0.7 collective-permute-start.12
  43.1 0.7 collective-permute-start.11
  43.8 33.8 %collective-permute-done.6 = bf16[8,32,1024]{2,1,0:T(8,128)(2,1)S(1)} collective-permute-done((bf16[8,32,1024]{2,1,0:T(8,128)(2,1)S(1)}, bf16[8,32,1024]{2,1,0:T(8,128)(2,1)S(1)}, u32[]{:S(2)}, u32[]{:S(2)}) %collective-permute-start.6) | collective-permute-done | bytes 524320 | tf_op jit(solution)/shard_map/ppermute | solution.py:18
  77.7 0.5 collective-permute-done.5
  78.4 1.3 collective-permute-start.16
  79.9 28.7 %collective-permute-start.15 = (bf16[16,32,1024]{2,1,0:T(8,128)(2,1)S(1)}, bf16[16,32,1024]{2,1,0:T(8,128)(2,1)S(1)}, u32[]{:S(2)}, u32[]{:S(2)}) collective-permute-start(bf16[16,32,1024]{2,1,0:T(8,128)(2,1)S(1)} %constant_dynamic-update-slice_fusion.5.a1), channel_id=1, source_target_pairs={{16,17},{17,16},{18,19},{19,18},{20,21},{21,20},{22,23},{23,22},{2... | collective-permute-start | bytes 3145736 | tf_op jit(solution)/shard_map/ppermute | solution.py:18
  108.7 2.8 %collective-permute-done.15.b1 = bf16[16,32,1024]{2,1,0:T(8,128)(2,1)S(1)} collective-permute-done((bf16[16,32,1024]{2,1,0:T(8,128)(2,1)S(1)}, bf16[16,32,1024]{2,1,0:T(8,128)(2,1)S(1)}, u32[]{:S(2)}, u32[]{:S(2)}) %collective-permute-start.15) | collective-permute-done | bytes 1048608 | tf_op jit(solution)/shard_map/ppermute | solution.py:18
  111.5 1.5 %collective-permute-done.14.b0 = bf16[16,32,1024]{2,1,0:T(8,128)(2,1)S(1)} collective-permute-done((bf16[16,32,1024]{2,1,0:T(8,128)(2,1)S(1)}, bf16[16,32,1024]{2,1,0:T(8,128)(2,1)S(1)}, u32[]{:S(2)}, u32[]{:S(2)}) %collective-permute-start.14) | collective-permute-done | bytes 1048608 | tf_op jit(solution)/shard_map/ppermute | solution.py:18
  113.0 1.4 copy-done.6
  114.7 24.8 %solve_update.1.v_ref = f32[2048,1024]{1,0:T(8,128)} custom-call(s32[1]{0:T(128)} %bitcast.pos_ref, bf16[16,32,1024]{2,1,0:T(8,128)(2,1)} %copy-done.5, bf16[16,32,1024]{2,1,0:T(8,128)(2,1)} %copy-done.8, bf16[16,32,1024]{2,1,0:T(8,128)(2,1)} %copy-done.3, bf16[16,32,1024]{2,1,0:T(8,128)(2,1)} %copy-done.7, bf16[4,256,1024]{2,1,0:T(8,128)(2,1)} %copy-done, ...), custom_call_target="tpu_custom_call" | custom-call | flops 15032385536 | bytes 25165824 | tf_op jit(solution)/shard_map/solve_update/pallas_call | solution.py:104
  139.5 8.5 %finish.1 = f32[2048,1024]{1,0:T(8,128)} custom-call(s32[1]{0:T(128)} %bitcast.pos_ref, f32[2048,1024]{1,0:T(8,128)} %solve_update.1.v_ref, bf16[1024,2048]{1,0:T(8,128)(2,1)} %bitcast.9.a_ref), custom_call_target="tpu_custom_call", output_to_operand_aliasing={{}: (1, {})} | custom-call | bytes 20971520 | tf_op jit(solution)/shard_map/finish/pallas_call | solution.py:136
  (45 shorter events, 1.4 us)
Async XLA Ops:
  0.9 8.2 %collective-permute-start = (bf16[2,32,1024]{2,1,0:T(8,128)(2,1)S(1)}, bf16[2,32,1024]{2,1,0:T(8,128)(2,1)S(1)}, u32[]{:S(2)}, u32[]{:S(2)}) collective-permute-start(bf16[2,32,1024]{2,1,0:T(8,128)(2,1)S(1)} %pad_maximum_fusion.6), channel_id=1, source_target_pairs={{0,16},{1,17},{2,18},{3,19},{4,20},{5,21},{6,22},{7,23},{8,24},{9,... | collective-permute-start | bytes 393224 | tf_op jit(solution)/shard_map/ppermute | solution.py:18
  4.0 10.0 %collective-permute-start.9 = (bf16[256,1024]{1,0:T(8,128)(2,1)}, bf16[256,1024]{1,0:T(8,128)(2,1)S(1)}, u32[]{:S(2)}, u32[]{:S(2)}) collective-permute-start(bf16[256,1024]{1,0:T(8,128)(2,1)} %get-tuple-element.31), channel_id=1, source_target_pairs={{16,18}} | collective-permute-start | bytes 1572872 | tf_op jit(solution)/shard_map/ppermute | solution.py:18
  4.7 9.3 %collective-permute-start.8 = (bf16[256,1024]{1,0:T(8,128)(2,1)}, bf16[256,1024]{1,0:T(8,128)(2,1)}, u32[]{:S(2)}, u32[]{:S(2)}) collective-permute-start(bf16[256,1024]{1,0:T(8,128)(2,1)} %get-tuple-element.32), channel_id=1, source_target_pairs={{16,20}} | collective-permute-start | bytes 1572872 | tf_op jit(solution)/shard_map/ppermute | solution.py:18
  6.1 8.7 %collective-permute-start.7 = (bf16[256,1024]{1,0:T(8,128)(2,1)}, bf16[256,1024]{1,0:T(8,128)(2,1)}, u32[]{:S(2)}, u32[]{:S(2)}) collective-permute-start(bf16[256,1024]{1,0:T(8,128)(2,1)} %get-tuple-element.33), channel_id=1, source_target_pairs={{16,22}} | collective-permute-start | bytes 1572872 | tf_op jit(solution)/shard_map/ppermute | solution.py:18
  9.8 6.8 %collective-permute-start.1 = (bf16[2,32,1024]{2,1,0:T(8,128)(2,1)S(1)}, bf16[2,32,1024]{2,1,0:T(8,128)(2,1)S(1)}, u32[]{:S(2)}, u32[]{:S(2)}) collective-permute-start(bf16[2,32,1024]{2,1,0:T(8,128)(2,1)S(1)} %pad_maximum_fusion.5), channel_id=1, source_target_pairs={{0,8},{1,9},{2,10},{3,11},{4,12},{5,13},{6,14},{7,15},{8,0},{9,1},... | collective-permute-start | bytes 393224 | tf_op jit(solution)/shard_map/ppermute | solution.py:18
  12.1 6.1 %collective-permute-start.2 = (bf16[2,32,1024]{2,1,0:T(8,128)(2,1)S(1)}, bf16[2,32,1024]{2,1,0:T(8,128)(2,1)S(1)}, u32[]{:S(2)}, u32[]{:S(2)}) collective-permute-start(bf16[2,32,1024]{2,1,0:T(8,128)(2,1)S(1)} %pad_maximum_fusion.7), channel_id=1, source_target_pairs={{16,24},{17,25},{18,26},{19,27},{20,28},{21,29},{22,30},{23,31},{2... | collective-permute-start | bytes 393224 | tf_op jit(solution)/shard_map/ppermute | solution.py:18
  14.0 0.8 copy-start.1
  16.0 10.8 %collective-permute-start.10 = (bf16[256,1024]{1,0:T(8,128)(2,1)S(1)}, bf16[256,1024]{1,0:T(8,128)(2,1)S(1)}, u32[]{:S(2)}, u32[]{:S(2)}) collective-permute-start(bf16[256,1024]{1,0:T(8,128)(2,1)S(1)} %select_select_fusion), channel_id=1, source_target_pairs={{16,24},{18,26},{20,28},{22,30}} | collective-permute-start | bytes 1572872 | tf_op jit(solution)/shard_map/ppermute | solution.py:18
  18.3 8.2 %collective-permute-start.4 = (bf16[4,32,1024]{2,1,0:T(8,128)(2,1)S(1)}, bf16[4,32,1024]{2,1,0:T(8,128)(2,1)S(1)}, u32[]{:S(2)}, u32[]{:S(2)}) collective-permute-start(bf16[4,32,1024]{2,1,0:T(8,128)(2,1)S(1)} %pad_maximum_fusion.4), channel_id=1, source_target_pairs={{16,18},{17,19},{18,16},{19,17},{20,22},{21,23},{22,20},{23,21},{2... | collective-permute-start | bytes 786440 | tf_op jit(solution)/shard_map/ppermute | solution.py:18
  21.5 5.3 %collective-permute-start.3 = (bf16[4,32,1024]{2,1,0:T(8,128)(2,1)S(1)}, bf16[4,32,1024]{2,1,0:T(8,128)(2,1)S(1)}, u32[]{:S(2)}, u32[]{:S(2)}) collective-permute-start(bf16[4,32,1024]{2,1,0:T(8,128)(2,1)S(1)} %pad_maximum_fusion.3), channel_id=1, source_target_pairs={{0,4},{1,5},{2,6},{3,7},{4,0},{5,1},{6,2},{7,3},{8,12},{9,13},{10,... | collective-permute-start | bytes 786440 | tf_op jit(solution)/shard_map/ppermute | solution.py:18
  26.9 112.7 %all-to-all-start = ((bf16[32,32,2048]{2,1,0:T(8,128)(2,1)}), bf16[32,32,2048]{2,1,0:T(8,128)(2,1)}, u32[]{:S(2)}, u32[]{:S(2)}) async-start(bf16[32,32,2048]{2,1,0:T(8,128)(2,1)} %bitcast.22), calls=%async_computation | async-start | bytes 8388608 | tf_op jit(solution)/shard_map/all_to_all | solution.py:230
  38.1 41.6 %copy-start.2 = (bf16[16,32,1024]{2,1,0:T(8,128)(2,1)S(1)}, bf16[16,32,1024]{2,1,0:T(8,128)(2,1)}, u32[]{:S(2)}) copy-start(bf16[16,32,1024]{2,1,0:T(8,128)(2,1)} %get-tuple-element.34) | copy-start | bytes 3145732
  38.2 41.6 %copy-start.4 = (bf16[16,32,1024]{2,1,0:T(8,128)(2,1)S(1)}, bf16[16,32,1024]{2,1,0:T(8,128)(2,1)}, u32[]{:S(2)}) copy-start(bf16[16,32,1024]{2,1,0:T(8,128)(2,1)} %get-tuple-element.35) | copy-start | bytes 3145732
  38.2 39.5 %collective-permute-start.6 = (bf16[8,32,1024]{2,1,0:T(8,128)(2,1)S(1)}, bf16[8,32,1024]{2,1,0:T(8,128)(2,1)S(1)}, u32[]{:S(2)}, u32[]{:S(2)}) collective-permute-start(bf16[8,32,1024]{2,1,0:T(8,128)(2,1)S(1)} %pad_maximum_fusion.2), channel_id=1, source_target_pairs={{16,20},{17,21},{18,22},{19,23},{20,16},{21,17},{22,18},{23,19},{2... | collective-permute-start | bytes 1572872 | tf_op jit(solution)/shard_map/ppermute | solution.py:18
  40.5 37.6 %collective-permute-start.5 = (bf16[8,32,1024]{2,1,0:T(8,128)(2,1)S(1)}, bf16[8,32,1024]{2,1,0:T(8,128)(2,1)S(1)}, u32[]{:S(2)}, u32[]{:S(2)}) collective-permute-start(bf16[8,32,1024]{2,1,0:T(8,128)(2,1)S(1)} %pad_maximum_fusion.1), channel_id=1, source_target_pairs={{0,2},{1,3},{2,0},{3,1},{4,6},{5,7},{6,4},{7,5},{8,10},{9,11},{10,... | collective-permute-start | bytes 1572872 | tf_op jit(solution)/shard_map/ppermute | solution.py:18
  41.7 36.4 %collective-permute-start.13 = (bf16[1,256,1024]{2,1,0:T(8,128)(2,1)S(1)}, bf16[1,256,1024]{2,1,0:T(8,128)(2,1)S(1)}, u32[]{:S(2)}, u32[]{:S(2)}) collective-permute-start(bf16[1,256,1024]{2,1,0:T(8,128)(2,1)S(1)} %select_bitcast_fusion), channel_id=1, source_target_pairs={{16,20},{18,22},{20,16},{22,18},{24,28},{26,30},{28,24},{30,26}} | collective-permute-start | bytes 1572872 | tf_op jit(solution)/shard_map/ppermute | solution.py:18
  42.4 35.7 %collective-permute-start.12 = (bf16[1,256,1024]{2,1,0:T(8,128)(2,1)S(1)}, bf16[1,256,1024]{2,1,0:T(8,128)(2,1)S(1)}, u32[]{:S(2)}, u32[]{:S(2)}) collective-permute-start(bf16[1,256,1024]{2,1,0:T(8,128)(2,1)S(1)} %select_bitcast_fusion), channel_id=1, source_target_pairs={{16,18},{18,16},{20,22},{22,20},{24,26},{26,24},{28,30},{30,28}} | collective-permute-start | bytes 1572872 | tf_op jit(solution)/shard_map/ppermute | solution.py:18
  43.1 35.0 %collective-permute-start.11 = (bf16[1,256,1024]{2,1,0:T(8,128)(2,1)S(1)}, bf16[1,256,1024]{2,1,0:T(8,128)(2,1)S(1)}, u32[]{:S(2)}, u32[]{:S(2)}) collective-permute-start(bf16[1,256,1024]{2,1,0:T(8,128)(2,1)S(1)} %select_bitcast_fusion), channel_id=1, source_target_pairs={{16,22},{18,20},{20,18},{22,16},{24,30},{26,28},{28,26},{30,24}} | collective-permute-start | bytes 1572872 | tf_op jit(solution)/shard_map/ppermute | solution.py:18
  78.4 36.0 %copy-start = (bf16[4,256,1024]{2,1,0:T(8,128)(2,1)}, bf16[4,256,1024]{2,1,0:T(8,128)(2,1)S(1)}, u32[]{:S(2)}) copy-start(bf16[4,256,1024]{2,1,0:T(8,128)(2,1)S(1)} %pad_maximum_fusion.a2) | copy-start | bytes 6291460
  78.4 34.6 %collective-permute-start.16 = (bf16[4,256,1024]{2,1,0:T(8,128)(2,1)S(1)}, bf16[4,256,1024]{2,1,0:T(8,128)(2,1)S(1)}, u32[]{:S(2)}, u32[]{:S(2)}) collective-permute-start(bf16[4,256,1024]{2,1,0:T(8,128)(2,1)S(1)} %pad_maximum_fusion.a2), channel_id=1, source_target_pairs={{16,17},{18,19},{20,21},{22,23},{24,25},{26,27},{28,29},{30,31}} | collective-permute-start | bytes 6291464 | tf_op jit(solution)/shard_map/ppermute | solution.py:18
  79.9 33.1 %copy-start.3 = (bf16[16,32,1024]{2,1,0:T(8,128)(2,1)}, bf16[16,32,1024]{2,1,0:T(8,128)(2,1)S(1)}, u32[]{:S(2)}) copy-start(bf16[16,32,1024]{2,1,0:T(8,128)(2,1)S(1)} %constant_dynamic-update-slice_fusion.5.a1) | copy-start | bytes 3145732
  79.9 31.6 %collective-permute-start.15 = (bf16[16,32,1024]{2,1,0:T(8,128)(2,1)S(1)}, bf16[16,32,1024]{2,1,0:T(8,128)(2,1)S(1)}, u32[]{:S(2)}, u32[]{:S(2)}) collective-permute-start(bf16[16,32,1024]{2,1,0:T(8,128)(2,1)S(1)} %constant_dynamic-update-slice_fusion.5.a1), channel_id=1, source_target_pairs={{16,17},{17,16},{18,19},{19,18},{20,21},{21,20},{22,23},{23,22},{2... | collective-permute-start | bytes 3145736 | tf_op jit(solution)/shard_map/ppermute | solution.py:18
  108.6 4.4 %copy-start.5 = (bf16[16,32,1024]{2,1,0:T(8,128)(2,1)}, bf16[16,32,1024]{2,1,0:T(8,128)(2,1)S(1)}, u32[]{:S(2)}) copy-start(bf16[16,32,1024]{2,1,0:T(8,128)(2,1)S(1)} %constant_dynamic-update-slice_fusion.a0) | copy-start | bytes 3145732
  108.6 4.4 %collective-permute-start.14 = (bf16[16,32,1024]{2,1,0:T(8,128)(2,1)S(1)}, bf16[16,32,1024]{2,1,0:T(8,128)(2,1)S(1)}, u32[]{:S(2)}, u32[]{:S(2)}) collective-permute-start(bf16[16,32,1024]{2,1,0:T(8,128)(2,1)S(1)} %constant_dynamic-update-slice_fusion.a0), channel_id=1, source_target_pairs={{0,1},{1,0},{2,3},{3,2},{4,5},{5,4},{6,7},{7,6},{8,9},{9,8},{10,11... | collective-permute-start | bytes 3145736 | tf_op jit(solution)/shard_map/ppermute | solution.py:18
  111.5 2.9 %copy-start.7 = (bf16[16,32,1024]{2,1,0:T(8,128)(2,1)}, bf16[16,32,1024]{2,1,0:T(8,128)(2,1)S(1)}, u32[]{:S(2)}) copy-start(bf16[16,32,1024]{2,1,0:T(8,128)(2,1)S(1)} %collective-permute-done.15.b1) | copy-start | bytes 3145732
  113.0 1.7 %copy-start.8 = (bf16[16,32,1024]{2,1,0:T(8,128)(2,1)}, bf16[16,32,1024]{2,1,0:T(8,128)(2,1)S(1)}, u32[]{:S(2)}) copy-start(bf16[16,32,1024]{2,1,0:T(8,128)(2,1)S(1)} %collective-permute-done.14.b0) | copy-start | bytes 3145732
  113.0 1.4 copy-start.6

commit v6 on v5

--- a/solution.py
+++ b/solution.py
@@ -9,7 +9,7 @@
 F32 = jnp.float32
 BF16 = jnp.bfloat16
 NT = (((1,), (1,)), ((), ()))
-LIMIT = pltpu.CompilerParams(vmem_limit_bytes=58 << 20)
+LIMIT = pltpu.CompilerParams(vmem_limit_bytes=34 << 20)
 FREE = pl.CostEstimate(flops=0, bytes_accessed=0, transcendentals=0)
 ANY = pl.BlockSpec(memory_space=pl.ANY)
 

time: 149 us -> 147 us (0.987)
  Pallas kernels: 33.3 us -> 29.6 us
  other arithmetic: 1.67 us -> 4.93 us
  local copies, waits for them, and re-layouts: 13.5 us -> 10.5 us
  starting transfers between devices: 58.8 us -> 61.8 us
    pallas_call x1, Pallas kernels: 24.8 us -> 21.1 us  [solve_update(): pl.pallas_call(kernel, out_shape=jax.ShapeDtypeStruct((rows, members), F3...]
    unnamed x23 -> x21, local copies, waits for them, and re-layouts: 4.75 us -> 1.85 us
    concatenate x3, other arithmetic: 0.38 us -> 2.05 us  [grow(): cur[t] = jnp.concatenate([cur[t], *got], axis=0)]
    all_to_all x1, starting transfers between devices: 11.2 us -> 12.6 us  [local(): lax.all_to_all(after(packed, gate), AXES, split_axis=0, concat_axis=0, ti...]
  transfers between devices with their start and end apart: 18 -> 18, of which waited for: 6 -> 6; matrix products, arithmetic and copies ran while one was open for 8% -> 9% of each run, Pallas kernels for 17% -> 14%
where the time goes in v6:
time: 147 us; the launch traced here: 146 us
  starting transfers between devices  61.8 us (42%)
  waiting for transfers between devices  39.1 us (27%)
  Pallas kernels  29.6 us (20%)
  local copies, waits for them, and re-layouts  10.5 us (7%)
  other arithmetic  4.93 us (3%)
    ppermute x17, starting transfers between devices, send(): return lax.ppermute(x, AXES, pairs)  49.1 us
    ppermute x17, waiting for transfers between devices, send(): return lax.ppermute(x, AXES, pairs)  39.1 us
    pallas_call x1, Pallas kernels, solve_update(): pl.pallas_call(kernel, out_shape=jax.ShapeDtypeStruct((rows, members), F3...  21.1 us
    all_to_all x1, starting transfers between devices, local(): lax.all_to_all(after(packed, gate), AXES, split_axis=0, concat_axis=0, ti...  12.6 us
    pallas_call x1, Pallas kernels, finish(): pl.pallas_call(kernel, out_shape=jax.ShapeDtypeStruct(v.shape, F32), grid...  8.52 us
    transpose x1, local copies, waits for them, and re-layouts, local(): tiles = x_t.reshape(width // 8, 8, n, rows).transpose(2, 0, 1, 3)  4.74 us
  transfers between devices with their start and end apart: 18, of which 6 were waited for; matrix products, arithmetic and copies ran while one was open for 9% of the time, Pallas kernels for 14%

profile of v6, /device:TPU:21, one launch (start us, length us, event | category | flops | bytes accessed | tf_op | source)
XLA Modules:
  0.0 146.2 jit_solution(1518902468880156282)
XLA Ops:
  0.0 0.9 slice_bitcast_fusion.1
  1.0 1.8 %slice_bitcast_fusion = bf16[1024,1024]{1,0:T(8,128)(2,1)S(1)} fusion(bf16[2,2048,1024]{2,1,0:T(8,128)(2,1)} %c_ref.1), kind=kLoop, calls=%fused_computation.2 | loop fusion | bytes 4194304 | tf_op jit(solution)/shard_map/squeeze | solution.py:182
  2.8 1.2 fusion
  4.0 0.7 collective-permute-start.9
  4.7 1.5 %collective-permute-start.8 = (bf16[256,1024]{1,0:T(8,128)(2,1)}, bf16[256,1024]{1,0:T(8,128)(2,1)}, u32[]{:S(2)}, u32[]{:S(2)}) collective-permute-start(bf16[256,1024]{1,0:T(8,128)(2,1)} %get-tuple-element.32), channel_id=1, source_target_pairs={{16,20}} | collective-permute-start | bytes 1572872 | tf_op jit(solution)/shard_map/ppermute | solution.py:18
  6.2 1.5 %collective-permute-start.7 = (bf16[256,1024]{1,0:T(8,128)(2,1)S(1)}, bf16[256,1024]{1,0:T(8,128)(2,1)}, u32[]{:S(2)}, u32[]{:S(2)}) collective-permute-start(bf16[256,1024]{1,0:T(8,128)(2,1)S(1)} %get-tuple-element.33), channel_id=1, source_target_pairs={{16,22}} | collective-permute-start | bytes 1572872 | tf_op jit(solution)/shard_map/ppermute | solution.py:18
  7.6 0.9 constant_dynamic-update-slice_fusion.9
  8.6 2.8 %collective-permute-start.1 = (bf16[2,32,1024]{2,1,0:T(8,128)(2,1)S(1)}, bf16[2,32,1024]{2,1,0:T(8,128)(2,1)S(1)}, u32[]{:S(2)}, u32[]{:S(2)}) collective-permute-start(bf16[2,32,1024]{2,1,0:T(8,128)(2,1)S(1)} %pad_maximum_fusion.5), channel_id=1, source_target_pairs={{0,8},{1,9},{2,10},{3,11},{4,12},{5,13},{6,14},{7,15},{8,0},{9,1},... | collective-permute-start | bytes 393224 | tf_op jit(solution)/shard_map/ppermute | solution.py:18
  11.4 1.9 %collective-permute-start.2 = (bf16[2,32,1024]{2,1,0:T(8,128)(2,1)S(1)}, bf16[2,32,1024]{2,1,0:T(8,128)(2,1)S(1)}, u32[]{:S(2)}, u32[]{:S(2)}) collective-permute-start(bf16[2,32,1024]{2,1,0:T(8,128)(2,1)S(1)} %pad_maximum_fusion.7), channel_id=1, source_target_pairs={{16,24},{17,25},{18,26},{19,27},{20,28},{21,29},{22,30},{23,31},{2... | collective-permute-start | bytes 393224 | tf_op jit(solution)/shard_map/ppermute | solution.py:18
  13.4 1.3 select_select_fusion
  14.7 1.5 %collective-permute-start.10 = (bf16[256,1024]{1,0:T(8,128)(2,1)S(1)}, bf16[256,1024]{1,0:T(8,128)(2,1)}, u32[]{:S(2)}, u32[]{:S(2)}) collective-permute-start(bf16[256,1024]{1,0:T(8,128)(2,1)S(1)} %select_select_fusion), channel_id=1, source_target_pairs={{16,24},{18,26},{20,28},{22,30}} | collective-permute-start | bytes 1572872 | tf_op jit(solution)/shard_map/ppermute | solution.py:18
  16.2 1.4 collective-permute-done.2
  17.6 0.7 pad_maximum_fusion.3
  18.3 0.7 pad_maximum_fusion.4
  19.0 3.2 %collective-permute-start.4 = (bf16[4,32,1024]{2,1,0:T(8,128)(2,1)}, bf16[4,32,1024]{2,1,0:T(8,128)(2,1)S(1)}, u32[]{:S(2)}, u32[]{:S(2)}) collective-permute-start(bf16[4,32,1024]{2,1,0:T(8,128)(2,1)} %pad_maximum_fusion.4), channel_id=1, source_target_pairs={{16,18},{17,19},{18,16},{19,17},{20,22},{21,23},{22,20},{23,21},{2... | collective-permute-start | bytes 786440 | tf_op jit(solution)/shard_map/ppermute | solution.py:18
  22.5 4.7 %copy.7 = bf16[32,4,8,2048]{3,2,1,0:T(8,128)(2,1)} copy(bf16[32,4,8,2048]{3,2,0,1:T(8,128)(2,1)} %bitcast.25) | data formatting | bytes 8388608 | tf_op jit(solution)/shard_map/transpose | solution.py:228
  27.9 0.7 copy-done.4
  28.7 12.6 %all-to-all-start = ((bf16[32,32,2048]{2,1,0:T(8,128)(2,1)}), bf16[32,32,2048]{2,1,0:T(8,128)(2,1)}, u32[]{:S(2)}, u32[]{:S(2)}) async-start(bf16[32,32,2048]{2,1,0:T(8,128)(2,1)} %bitcast.22), calls=%async_computation | async-start | bytes 8388608 | tf_op jit(solution)/shard_map/all_to_all | solution.py:230
  41.4 0.9 pad_maximum_fusion.1
  42.3 0.9 pad_maximum_fusion.2
  43.2 2.2 %collective-permute-start.6 = (bf16[8,32,1024]{2,1,0:T(8,128)(2,1)S(1)}, bf16[8,32,1024]{2,1,0:T(8,128)(2,1)S(1)}, u32[]{:S(2)}, u32[]{:S(2)}) collective-permute-start(bf16[8,32,1024]{2,1,0:T(8,128)(2,1)S(1)} %pad_maximum_fusion.2), channel_id=1, source_target_pairs={{16,20},{17,21},{18,22},{19,23},{20,16},{21,17},{22,18},{23,19},{2... | collective-permute-start | bytes 1572872 | tf_op jit(solution)/shard_map/ppermute | solution.py:18
  45.4 1.2 collective-permute-start.5
  46.6 0.7 collective-permute-start.13
  47.3 0.7 collective-permute-start.12
  48.0 0.7 collective-permute-start.11
  48.7 32.3 %collective-permute-done.6 = bf16[8,32,1024]{2,1,0:T(8,128)(2,1)S(1)} collective-permute-done((bf16[8,32,1024]{2,1,0:T(8,128)(2,1)S(1)}, bf16[8,32,1024]{2,1,0:T(8,128)(2,1)S(1)}, u32[]{:S(2)}, u32[]{:S(2)}) %collective-permute-start.6) | collective-permute-done | bytes 524320 | tf_op jit(solution)/shard_map/ppermute | solution.py:18
  81.8 1.6 %collective-permute-start.16 = (bf16[4,256,1024]{2,1,0:T(8,128)(2,1)S(1)}, bf16[4,256,1024]{2,1,0:T(8,128)(2,1)S(1)}, u32[]{:S(2)}, u32[]{:S(2)}) collective-permute-start(bf16[4,256,1024]{2,1,0:T(8,128)(2,1)S(1)} %pad_maximum_fusion.a2), channel_id=1, source_target_pairs={{16,17},{18,19},{20,21},{22,23},{24,25},{26,27},{28,29},{30,31}} | collective-permute-start | bytes 6291464 | tf_op jit(solution)/shard_map/ppermute | solution.py:18
  83.5 28.7 %collective-permute-start.15 = (bf16[16,32,1024]{2,1,0:T(8,128)(2,1)S(1)}, bf16[16,32,1024]{2,1,0:T(8,128)(2,1)S(1)}, u32[]{:S(2)}, u32[]{:S(2)}) collective-permute-start(bf16[16,32,1024]{2,1,0:T(8,128)(2,1)S(1)} %constant_dynamic-update-slice_fusion.5.a1), channel_id=1, source_target_pairs={{16,17},{17,16},{18,19},{19,18},{20,21},{21,20},{22,23},{23,22},{2... | collective-permute-start | bytes 3145736 | tf_op jit(solution)/shard_map/ppermute | solution.py:18
  112.3 2.8 %collective-permute-done.15.b1 = bf16[16,32,1024]{2,1,0:T(8,128)(2,1)S(1)} collective-permute-done((bf16[16,32,1024]{2,1,0:T(8,128)(2,1)S(1)}, bf16[16,32,1024]{2,1,0:T(8,128)(2,1)S(1)}, u32[]{:S(2)}, u32[]{:S(2)}) %collective-permute-start.15) | collective-permute-done | bytes 1048608 | tf_op jit(solution)/shard_map/ppermute | solution.py:18
  115.1 1.5 %collective-permute-done.14.b0 = bf16[16,32,1024]{2,1,0:T(8,128)(2,1)S(1)} collective-permute-done((bf16[16,32,1024]{2,1,0:T(8,128)(2,1)S(1)}, bf16[16,32,1024]{2,1,0:T(8,128)(2,1)S(1)}, u32[]{:S(2)}, u32[]{:S(2)}) %collective-permute-start.14) | collective-permute-done | bytes 1048608 | tf_op jit(solution)/shard_map/ppermute | solution.py:18
  116.6 21.1 %solve_update.1.v_ref = f32[2048,1024]{1,0:T(8,128)} custom-call(s32[1]{0:T(128)} %bitcast.pos_ref, bf16[16,32,1024]{2,1,0:T(8,128)(2,1)S(1)} %constant_dynamic-update-slice_fusion.a0, bf16[16,32,1024]{2,1,0:T(8,128)(2,1)S(1)} %collective-permute-done.14.b0, bf16[16,32,1024]{2,1,0:T(8,128)(2,1)S(1)} %constant_dynamic-update-slice_fusion.5.a1, ...), custom_call_target="tpu_custom_call" | custom-call | flops 15032385536 | bytes 25165824 | tf_op jit(solution)/shard_map/solve_update/pallas_call | solution.py:104
  137.7 8.5 %finish.1 = f32[2048,1024]{1,0:T(8,128)} custom-call(s32[1]{0:T(128)} %bitcast.pos_ref, f32[2048,1024]{1,0:T(8,128)} %solve_update.1.v_ref, bf16[1024,2048]{1,0:T(8,128)(2,1)} %bitcast.9.a_ref), custom_call_target="tpu_custom_call", output_to_operand_aliasing={{}: (1, {})} | custom-call | bytes 20971520 | tf_op jit(solution)/shard_map/finish/pallas_call | solution.py:136
  (43 shorter events, 2.2 us)
Async XLA Ops:
  0.9 7.6 %collective-permute-start = (bf16[2,32,1024]{2,1,0:T(8,128)(2,1)S(1)}, bf16[2,32,1024]{2,1,0:T(8,128)(2,1)S(1)}, u32[]{:S(2)}, u32[]{:S(2)}) collective-permute-start(bf16[2,32,1024]{2,1,0:T(8,128)(2,1)S(1)} %pad_maximum_fusion.6), channel_id=1, source_target_pairs={{0,16},{1,17},{2,18},{3,19},{4,20},{5,21},{6,22},{7,23},{8,24},{9,... | collective-permute-start | bytes 393224 | tf_op jit(solution)/shard_map/ppermute | solution.py:18
  2.8 3.4 %copy-start.1 = (bf16[1024,1024]{1,0:T(8,128)(2,1)}, bf16[1024,1024]{1,0:T(8,128)(2,1)S(1)}, u32[]{:S(2)}) copy-start(bf16[1024,1024]{1,0:T(8,128)(2,1)S(1)} %slice_bitcast_fusion) | copy-start | bytes 6291460
  4.0 9.4 %collective-permute-start.9 = (bf16[256,1024]{1,0:T(8,128)(2,1)}, bf16[256,1024]{1,0:T(8,128)(2,1)S(1)}, u32[]{:S(2)}, u32[]{:S(2)}) collective-permute-start(bf16[256,1024]{1,0:T(8,128)(2,1)} %get-tuple-element.31), channel_id=1, source_target_pairs={{16,18}} | collective-permute-start | bytes 1572872 | tf_op jit(solution)/shard_map/ppermute | solution.py:18
  4.7 8.7 %collective-permute-start.8 = (bf16[256,1024]{1,0:T(8,128)(2,1)}, bf16[256,1024]{1,0:T(8,128)(2,1)}, u32[]{:S(2)}, u32[]{:S(2)}) collective-permute-start(bf16[256,1024]{1,0:T(8,128)(2,1)} %get-tuple-element.32), channel_id=1, source_target_pairs={{16,20}} | collective-permute-start | bytes 1572872 | tf_op jit(solution)/shard_map/ppermute | solution.py:18
  6.2 7.2 %collective-permute-start.7 = (bf16[256,1024]{1,0:T(8,128)(2,1)S(1)}, bf16[256,1024]{1,0:T(8,128)(2,1)}, u32[]{:S(2)}, u32[]{:S(2)}) collective-permute-start(bf16[256,1024]{1,0:T(8,128)(2,1)S(1)} %get-tuple-element.33), channel_id=1, source_target_pairs={{16,22}} | collective-permute-start | bytes 1572872 | tf_op jit(solution)/shard_map/ppermute | solution.py:18
  8.6 10.5 %copy-start.6 = (bf16[1,32,1024]{2,1,0:T(8,128)(2,1)}, bf16[1,32,1024]{2,1,0:T(8,128)(2,1)S(1)}, u32[]{:S(2)}) copy-start(bf16[1,32,1024]{2,1,0:T(8,128)(2,1)S(1)} %get-tuple-element.36) | copy-start | bytes 196612
  8.6 10.4 %copy-start.7 = (bf16[1,32,1024]{2,1,0:T(8,128)(2,1)}, bf16[1,32,1024]{2,1,0:T(8,128)(2,1)S(1)}, u32[]{:S(2)}) copy-start(bf16[1,32,1024]{2,1,0:T(8,128)(2,1)S(1)} %get-tuple-element.37) | copy-start | bytes 196612
  8.6 7.6 %collective-permute-start.1 = (bf16[2,32,1024]{2,1,0:T(8,128)(2,1)S(1)}, bf16[2,32,1024]{2,1,0:T(8,128)(2,1)S(1)}, u32[]{:S(2)}, u32[]{:S(2)}) collective-permute-start(bf16[2,32,1024]{2,1,0:T(8,128)(2,1)S(1)} %pad_maximum_fusion.5), channel_id=1, source_target_pairs={{0,8},{1,9},{2,10},{3,11},{4,12},{5,13},{6,14},{7,15},{8,0},{9,1},... | collective-permute-start | bytes 393224 | tf_op jit(solution)/shard_map/ppermute | solution.py:18
  11.4 6.1 %collective-permute-start.2 = (bf16[2,32,1024]{2,1,0:T(8,128)(2,1)S(1)}, bf16[2,32,1024]{2,1,0:T(8,128)(2,1)S(1)}, u32[]{:S(2)}, u32[]{:S(2)}) collective-permute-start(bf16[2,32,1024]{2,1,0:T(8,128)(2,1)S(1)} %pad_maximum_fusion.7), channel_id=1, source_target_pairs={{16,24},{17,25},{18,26},{19,27},{20,28},{21,29},{22,30},{23,31},{2... | collective-permute-start | bytes 393224 | tf_op jit(solution)/shard_map/ppermute | solution.py:18
  14.7 13.9 %collective-permute-start.10 = (bf16[256,1024]{1,0:T(8,128)(2,1)S(1)}, bf16[256,1024]{1,0:T(8,128)(2,1)}, u32[]{:S(2)}, u32[]{:S(2)}) collective-permute-start(bf16[256,1024]{1,0:T(8,128)(2,1)S(1)} %select_select_fusion), channel_id=1, source_target_pairs={{16,24},{18,26},{20,28},{22,30}} | collective-permute-start | bytes 1572872 | tf_op jit(solution)/shard_map/ppermute | solution.py:18
  19.0 8.2 %collective-permute-start.4 = (bf16[4,32,1024]{2,1,0:T(8,128)(2,1)}, bf16[4,32,1024]{2,1,0:T(8,128)(2,1)S(1)}, u32[]{:S(2)}, u32[]{:S(2)}) collective-permute-start(bf16[4,32,1024]{2,1,0:T(8,128)(2,1)} %pad_maximum_fusion.4), channel_id=1, source_target_pairs={{16,18},{17,19},{18,16},{19,17},{20,22},{21,23},{22,20},{23,21},{2... | collective-permute-start | bytes 786440 | tf_op jit(solution)/shard_map/ppermute | solution.py:18
  22.3 5.5 %collective-permute-start.3 = (bf16[4,32,1024]{2,1,0:T(8,128)(2,1)}, bf16[4,32,1024]{2,1,0:T(8,128)(2,1)S(1)}, u32[]{:S(2)}, u32[]{:S(2)}) collective-permute-start(bf16[4,32,1024]{2,1,0:T(8,128)(2,1)} %pad_maximum_fusion.3), channel_id=1, source_target_pairs={{0,4},{1,5},{2,6},{3,7},{4,0},{5,1},{6,2},{7,3},{8,12},{9,13},{10,... | collective-permute-start | bytes 786440 | tf_op jit(solution)/shard_map/ppermute | solution.py:18
  27.2 0.7 copy-start.2
  27.9 0.7 copy-start.4
  28.7 12.7 %copy-start.5 = (bf16[4,32,1024]{2,1,0:T(8,128)(2,1)S(1)}, bf16[4,32,1024]{2,1,0:T(8,128)(2,1)}, u32[]{:S(2)}) copy-start(bf16[4,32,1024]{2,1,0:T(8,128)(2,1)} %copy-done.4) | copy-start | bytes 786436
  28.7 13.6 %copy-start.3 = (bf16[4,32,1024]{2,1,0:T(8,128)(2,1)S(1)}, bf16[4,32,1024]{2,1,0:T(8,128)(2,1)}, u32[]{:S(2)}) copy-start(bf16[4,32,1024]{2,1,0:T(8,128)(2,1)} %copy-done.2) | copy-start | bytes 786436
  28.7 109.0 %all-to-all-start = ((bf16[32,32,2048]{2,1,0:T(8,128)(2,1)}), bf16[32,32,2048]{2,1,0:T(8,128)(2,1)}, u32[]{:S(2)}, u32[]{:S(2)}) async-start(bf16[32,32,2048]{2,1,0:T(8,128)(2,1)} %bitcast.22), calls=%async_computation | async-start | bytes 8388608 | tf_op jit(solution)/shard_map/all_to_all | solution.py:230
  43.2 37.8 %collective-permute-start.6 = (bf16[8,32,1024]{2,1,0:T(8,128)(2,1)S(1)}, bf16[8,32,1024]{2,1,0:T(8,128)(2,1)S(1)}, u32[]{:S(2)}, u32[]{:S(2)}) collective-permute-start(bf16[8,32,1024]{2,1,0:T(8,128)(2,1)S(1)} %pad_maximum_fusion.2), channel_id=1, source_target_pairs={{16,20},{17,21},{18,22},{19,23},{20,16},{21,17},{22,18},{23,19},{2... | collective-permute-start | bytes 1572872 | tf_op jit(solution)/shard_map/ppermute | solution.py:18
  45.4 36.1 %collective-permute-start.5 = (bf16[8,32,1024]{2,1,0:T(8,128)(2,1)S(1)}, bf16[8,32,1024]{2,1,0:T(8,128)(2,1)S(1)}, u32[]{:S(2)}, u32[]{:S(2)}) collective-permute-start(bf16[8,32,1024]{2,1,0:T(8,128)(2,1)S(1)} %pad_maximum_fusion.1), channel_id=1, source_target_pairs={{0,2},{1,3},{2,0},{3,1},{4,6},{5,7},{6,4},{7,5},{8,10},{9,11},{10,... | collective-permute-start | bytes 1572872 | tf_op jit(solution)/shard_map/ppermute | solution.py:18
  46.6 34.9 %collective-permute-start.13 = (bf16[1,256,1024]{2,1,0:T(8,128)(2,1)S(1)}, bf16[1,256,1024]{2,1,0:T(8,128)(2,1)S(1)}, u32[]{:S(2)}, u32[]{:S(2)}) collective-permute-start(bf16[1,256,1024]{2,1,0:T(8,128)(2,1)S(1)} %select_bitcast_fusion), channel_id=1, source_target_pairs={{16,20},{18,22},{20,16},{22,18},{24,28},{26,30},{28,24},{30,26}} | collective-permute-start | bytes 1572872 | tf_op jit(solution)/shard_map/ppermute | solution.py:18
  47.3 34.2 %collective-permute-start.12 = (bf16[1,256,1024]{2,1,0:T(8,128)(2,1)S(1)}, bf16[1,256,1024]{2,1,0:T(8,128)(2,1)S(1)}, u32[]{:S(2)}, u32[]{:S(2)}) collective-permute-start(bf16[1,256,1024]{2,1,0:T(8,128)(2,1)S(1)} %select_bitcast_fusion), channel_id=1, source_target_pairs={{16,18},{18,16},{20,22},{22,20},{24,26},{26,24},{28,30},{30,28}} | collective-permute-start | bytes 1572872 | tf_op jit(solution)/shard_map/ppermute | solution.py:18
  48.0 33.5 %collective-permute-start.11 = (bf16[1,256,1024]{2,1,0:T(8,128)(2,1)S(1)}, bf16[1,256,1024]{2,1,0:T(8,128)(2,1)S(1)}, u32[]{:S(2)}, u32[]{:S(2)}) collective-permute-start(bf16[1,256,1024]{2,1,0:T(8,128)(2,1)S(1)} %select_bitcast_fusion), channel_id=1, source_target_pairs={{16,22},{18,20},{20,18},{22,16},{24,30},{26,28},{28,26},{30,24}} | collective-permute-start | bytes 1572872 | tf_op jit(solution)/shard_map/ppermute | solution.py:18
  81.5 35.1 %copy-start = (bf16[2,1024,1024]{2,1,0:T(8,128)(2,1)S(1)}, bf16[2,1024,1024]{2,1,0:T(8,128)(2,1)}, u32[]{:S(2)}) copy-start(bf16[2,1024,1024]{2,1,0:T(8,128)(2,1)} %d_ref.1) | copy-start | bytes 12582916
  81.8 34.8 %collective-permute-start.16 = (bf16[4,256,1024]{2,1,0:T(8,128)(2,1)S(1)}, bf16[4,256,1024]{2,1,0:T(8,128)(2,1)S(1)}, u32[]{:S(2)}, u32[]{:S(2)}) collective-permute-start(bf16[4,256,1024]{2,1,0:T(8,128)(2,1)S(1)} %pad_maximum_fusion.a2), channel_id=1, source_target_pairs={{16,17},{18,19},{20,21},{22,23},{24,25},{26,27},{28,29},{30,31}} | collective-permute-start | bytes 6291464 | tf_op jit(solution)/shard_map/ppermute | solution.py:18
  83.5 31.6 %collective-permute-start.15 = (bf16[16,32,1024]{2,1,0:T(8,128)(2,1)S(1)}, bf16[16,32,1024]{2,1,0:T(8,128)(2,1)S(1)}, u32[]{:S(2)}, u32[]{:S(2)}) collective-permute-start(bf16[16,32,1024]{2,1,0:T(8,128)(2,1)S(1)} %constant_dynamic-update-slice_fusion.5.a1), channel_id=1, source_target_pairs={{16,17},{17,16},{18,19},{19,18},{20,21},{21,20},{22,23},{23,22},{2... | collective-permute-start | bytes 3145736 | tf_op jit(solution)/shard_map/ppermute | solution.py:18
  112.2 4.4 %collective-permute-start.14 = (bf16[16,32,1024]{2,1,0:T(8,128)(2,1)S(1)}, bf16[16,32,1024]{2,1,0:T(8,128)(2,1)S(1)}, u32[]{:S(2)}, u32[]{:S(2)}) collective-permute-start(bf16[16,32,1024]{2,1,0:T(8,128)(2,1)S(1)} %constant_dynamic-update-slice_fusion.a0), channel_id=1, source_target_pairs={{0,1},{1,0},{2,3},{3,2},{4,5},{5,4},{6,7},{7,6},{8,9},{9,8},{10,11... | collective-permute-start | bytes 3145736 | tf_op jit(solution)/shard_map/ppermute | solution.py:18

commit v7 on v6

--- a/solution.py
+++ b/solution.py
@@ -179,10 +179,15 @@
     offs = [[0, half], [0, half], [0]]
 
     chips = quarter // 2
-    slots = after(col_panels[0, :nb], both).reshape(chips, nb // chips, nb)
-    got = slots[0]
+    piece = nb // chips
+    zero = after(jnp.int32(0), both)
+
+    def slot(t):
+        return lax.dynamic_slice(col_panels, (zero, t * piece, 0), (1, piece, nb))[0]
+
+    got = slot(0)
     for t in range(1, chips):
-        here = send(slots[t], [(owner, owner + 2 * t)])
+        here = send(slot(t), [(owner, owner + 2 * t)])
         got = jnp.where(me // 2 == owner // 2 + t, here, got)
     down = send(got, [(i, i + quarter) for i in range(owner, owner + quarter, 2)])
     cur.append(jnp.where(me >= owner + quarter, down, got)[None])

time: 147 us -> 146 us (level)
  transfers between devices with their start and end apart: 18 -> 18, of which waited for: 6 -> 6; matrix products, arithmetic and copies ran while one was open for 9% -> 9% of each run, Pallas kernels for 14% -> 15%
where the time goes in v7:
time: 146 us; the launch traced here: 145 us
  starting transfers between devices  61.8 us (42%)
  waiting for transfers between devices  38.8 us (27%)
  Pallas kernels  29.6 us (20%)
  local copies, waits for them, and re-layouts  9.98 us (7%)
  other arithmetic  4.93 us (3%)
    ppermute x17, starting transfers between devices, send(): return lax.ppermute(x, AXES, pairs)  49.7 us
    ppermute x17, waiting for transfers between devices, send(): return lax.ppermute(x, AXES, pairs)  38.8 us
    pallas_call x1, Pallas kernels, solve_update(): pl.pallas_call(kernel, out_shape=jax.ShapeDtypeStruct((rows, members), F3...  21.1 us
    all_to_all x1, starting transfers between devices, local(): lax.all_to_all(after(packed, gate), AXES, split_axis=0, concat_axis=0, ti...  12.1 us
    pallas_call x1, Pallas kernels, finish(): pl.pallas_call(kernel, out_shape=jax.ShapeDtypeStruct(v.shape, F32), grid...  8.52 us
    transpose x1, local copies, waits for them, and re-layouts, local(): tiles = x_t.reshape(width // 8, 8, n, rows).transpose(2, 0, 1, 3)  4.73 us
  transfers between devices with their start and end apart: 18, of which 6 were waited for; matrix products, arithmetic and copies ran while one was open for 9% of the time, Pallas kernels for 15%

profile of v7, /device:TPU:21, one launch (start us, length us, event | category | flops | bytes accessed | tf_op | source)
XLA Modules:
  0.0 145.4 jit_solution(15099952500003267742)
XLA Ops:
  0.0 0.9 slice_bitcast_fusion
  1.0 2.5 %dynamic-slice_bitcast_fusion = (bf16[256,1024]{1,0:T(8,128)(2,1)}, bf16[256,1024]{1,0:T(8,128)(2,1)}, bf16[256,1024]{1,0:T(8,128)(2,1)S(1)}) fusion(bf16[2,2048,1024]{2,1,0:T(8,128)(2,1)} %c_ref.1, s32[]{:T(128)S(6)} %select_n.42), kind=kLoop, calls=%fused_computation.8 | loop fusion | bytes 3145732 | tf_op jit(solution)/shard_map/squeeze | solution.py:186
  3.5 0.7 collective-permute-start.9
  4.2 1.5 %collective-permute-start.8 = (bf16[256,1024]{1,0:T(8,128)(2,1)}, bf16[256,1024]{1,0:T(8,128)(2,1)}, u32[]{:S(2)}, u32[]{:S(2)}) collective-permute-start(bf16[256,1024]{1,0:T(8,128)(2,1)} %get-tuple-element.28), channel_id=1, source_target_pairs={{16,20}} | collective-permute-start | bytes 1572872 | tf_op jit(solution)/shard_map/ppermute | solution.py:18
  5.7 1.5 %collective-permute-start.7 = (bf16[256,1024]{1,0:T(8,128)(2,1)S(1)}, bf16[256,1024]{1,0:T(8,128)(2,1)}, u32[]{:S(2)}, u32[]{:S(2)}) collective-permute-start(bf16[256,1024]{1,0:T(8,128)(2,1)S(1)} %get-tuple-element.29), channel_id=1, source_target_pairs={{16,22}} | collective-permute-start | bytes 1572872 | tf_op jit(solution)/shard_map/ppermute | solution.py:18
  7.1 0.9 constant_dynamic-update-slice_fusion.9
  8.1 3.3 %collective-permute-start.1 = (bf16[2,32,1024]{2,1,0:T(8,128)(2,1)S(1)}, bf16[2,32,1024]{2,1,0:T(8,128)(2,1)S(1)}, u32[]{:S(2)}, u32[]{:S(2)}) collective-permute-start(bf16[2,32,1024]{2,1,0:T(8,128)(2,1)S(1)} %pad_maximum_fusion.5), channel_id=1, source_target_pairs={{0,8},{1,9},{2,10},{3,11},{4,12},{5,13},{6,14},{7,15},{8,0},{9,1},... | collective-permute-start | bytes 393224 | tf_op jit(solution)/shard_map/ppermute | solution.py:18
  11.4 1.9 %collective-permute-start.2 = (bf16[2,32,1024]{2,1,0:T(8,128)(2,1)S(1)}, bf16[2,32,1024]{2,1,0:T(8,128)(2,1)S(1)}, u32[]{:S(2)}, u32[]{:S(2)}) collective-permute-start(bf16[2,32,1024]{2,1,0:T(8,128)(2,1)S(1)} %pad_maximum_fusion.7), channel_id=1, source_target_pairs={{16,24},{17,25},{18,26},{19,27},{20,28},{21,29},{22,30},{23,31},{2... | collective-permute-start | bytes 393224 | tf_op jit(solution)/shard_map/ppermute | solution.py:18
  13.4 1.3 fusion.1
  14.7 1.5 %collective-permute-start.10 = (bf16[256,1024]{1,0:T(8,128)(2,1)S(1)}, bf16[256,1024]{1,0:T(8,128)(2,1)}, u32[]{:S(2)}, u32[]{:S(2)}) collective-permute-start(bf16[256,1024]{1,0:T(8,128)(2,1)S(1)} %fusion.1), channel_id=1, source_target_pairs={{16,24},{18,26},{20,28},{22,30}} | collective-permute-start | bytes 1572872 | tf_op jit(solution)/shard_map/ppermute | solution.py:18
  16.2 1.4 collective-permute-done.2
  17.6 0.7 pad_maximum_fusion.3
  18.3 0.7 pad_maximum_fusion.4
  19.0 3.2 %collective-permute-start.4 = (bf16[4,32,1024]{2,1,0:T(8,128)(2,1)}, bf16[4,32,1024]{2,1,0:T(8,128)(2,1)S(1)}, u32[]{:S(2)}, u32[]{:S(2)}) collective-permute-start(bf16[4,32,1024]{2,1,0:T(8,128)(2,1)} %pad_maximum_fusion.4), channel_id=1, source_target_pairs={{16,18},{17,19},{18,16},{19,17},{20,22},{21,23},{22,20},{23,21},{2... | collective-permute-start | bytes 786440 | tf_op jit(solution)/shard_map/ppermute | solution.py:18
  22.5 4.7 %copy.7 = bf16[32,4,8,2048]{3,2,1,0:T(8,128)(2,1)} copy(bf16[32,4,8,2048]{3,2,0,1:T(8,128)(2,1)} %bitcast.35) | data formatting | bytes 8388608 | tf_op jit(solution)/shard_map/transpose | solution.py:233
  27.2 0.6 collective-permute-done.3
  27.9 0.7 copy-done.3
  28.7 12.1 %all-to-all-start = ((bf16[32,32,2048]{2,1,0:T(8,128)(2,1)}), bf16[32,32,2048]{2,1,0:T(8,128)(2,1)}, u32[]{:S(2)}, u32[]{:S(2)}) async-start(bf16[32,32,2048]{2,1,0:T(8,128)(2,1)} %bitcast.32), calls=%async_computation | async-start | bytes 8388608 | tf_op jit(solution)/shard_map/all_to_all | solution.py:235
  40.9 0.9 pad_maximum_fusion.1
  41.8 0.9 pad_maximum_fusion.2
  42.7 2.4 %collective-permute-start.6 = (bf16[8,32,1024]{2,1,0:T(8,128)(2,1)S(1)}, bf16[8,32,1024]{2,1,0:T(8,128)(2,1)S(1)}, u32[]{:S(2)}, u32[]{:S(2)}) collective-permute-start(bf16[8,32,1024]{2,1,0:T(8,128)(2,1)S(1)} %pad_maximum_fusion.2), channel_id=1, source_target_pairs={{16,20},{17,21},{18,22},{19,23},{20,16},{21,17},{22,18},{23,19},{2... | collective-permute-start | bytes 1572872 | tf_op jit(solution)/shard_map/ppermute | solution.py:18
  45.1 1.2 collective-permute-start.5
  46.4 0.7 collective-permute-start.13
  47.1 0.7 collective-permute-start.12
  47.8 0.7 collective-permute-start.11
  48.5 32.0 %collective-permute-done.6 = bf16[8,32,1024]{2,1,0:T(8,128)(2,1)S(1)} collective-permute-done((bf16[8,32,1024]{2,1,0:T(8,128)(2,1)S(1)}, bf16[8,32,1024]{2,1,0:T(8,128)(2,1)S(1)}, u32[]{:S(2)}, u32[]{:S(2)}) %collective-permute-start.6) | collective-permute-done | bytes 524320 | tf_op jit(solution)/shard_map/ppermute | solution.py:18
  81.2 1.3 collective-permute-start.16
  82.7 28.7 %collective-permute-start.15 = (bf16[16,32,1024]{2,1,0:T(8,128)(2,1)S(1)}, bf16[16,32,1024]{2,1,0:T(8,128)(2,1)S(1)}, u32[]{:S(2)}, u32[]{:S(2)}) collective-permute-start(bf16[16,32,1024]{2,1,0:T(8,128)(2,1)S(1)} %constant_dynamic-update-slice_fusion.5.a1), channel_id=1, source_target_pairs={{16,17},{17,16},{18,19},{19,18},{20,21},{21,20},{22,23},{23,22},{2... | collective-permute-start | bytes 3145736 | tf_op jit(solution)/shard_map/ppermute | solution.py:18
  111.5 2.8 %collective-permute-done.15.b1 = bf16[16,32,1024]{2,1,0:T(8,128)(2,1)S(1)} collective-permute-done((bf16[16,32,1024]{2,1,0:T(8,128)(2,1)S(1)}, bf16[16,32,1024]{2,1,0:T(8,128)(2,1)S(1)}, u32[]{:S(2)}, u32[]{:S(2)}) %collective-permute-start.15) | collective-permute-done | bytes 1048608 | tf_op jit(solution)/shard_map/ppermute | solution.py:18
  114.3 1.5 %collective-permute-done.14.b0 = bf16[16,32,1024]{2,1,0:T(8,128)(2,1)S(1)} collective-permute-done((bf16[16,32,1024]{2,1,0:T(8,128)(2,1)S(1)}, bf16[16,32,1024]{2,1,0:T(8,128)(2,1)S(1)}, u32[]{:S(2)}, u32[]{:S(2)}) %collective-permute-start.14) | collective-permute-done | bytes 1048608 | tf_op jit(solution)/shard_map/ppermute | solution.py:18
  115.8 21.1 %solve_update.1.v_ref = f32[2048,1024]{1,0:T(8,128)} custom-call(s32[1]{0:T(128)} %bitcast.pos_ref, bf16[16,32,1024]{2,1,0:T(8,128)(2,1)S(1)} %constant_dynamic-update-slice_fusion.a0, bf16[16,32,1024]{2,1,0:T(8,128)(2,1)S(1)} %collective-permute-done.14.b0, bf16[16,32,1024]{2,1,0:T(8,128)(2,1)S(1)} %constant_dynamic-update-slice_fusion.5.a1, ...), custom_call_target="tpu_custom_call" | custom-call | flops 15032385536 | bytes 25165824 | tf_op jit(solution)/shard_map/solve_update/pallas_call | solution.py:104
  136.9 8.5 %finish.1 = f32[2048,1024]{1,0:T(8,128)} custom-call(s32[1]{0:T(128)} %bitcast.pos_ref, f32[2048,1024]{1,0:T(8,128)} %solve_update.1.v_ref, bf16[1024,2048]{1,0:T(8,128)(2,1)} %bitcast.12.a_ref), custom_call_target="tpu_custom_call", output_to_operand_aliasing={{}: (1, {})} | custom-call | bytes 20971520 | tf_op jit(solution)/shard_map/finish/pallas_call | solution.py:136
  (40 shorter events, 1.6 us)
Async XLA Ops:
  0.9 7.1 %collective-permute-start = (bf16[2,32,1024]{2,1,0:T(8,128)(2,1)S(1)}, bf16[2,32,1024]{2,1,0:T(8,128)(2,1)S(1)}, u32[]{:S(2)}, u32[]{:S(2)}) collective-permute-start(bf16[2,32,1024]{2,1,0:T(8,128)(2,1)S(1)} %pad_maximum_fusion.6), channel_id=1, source_target_pairs={{0,16},{1,17},{2,18},{3,19},{4,20},{5,21},{6,22},{7,23},{8,24},{9,... | collective-permute-start | bytes 393224 | tf_op jit(solution)/shard_map/ppermute | solution.py:18
  3.5 9.9 %collective-permute-start.9 = (bf16[256,1024]{1,0:T(8,128)(2,1)}, bf16[256,1024]{1,0:T(8,128)(2,1)S(1)}, u32[]{:S(2)}, u32[]{:S(2)}) collective-permute-start(bf16[256,1024]{1,0:T(8,128)(2,1)} %get-tuple-element.27), channel_id=1, source_target_pairs={{16,18}} | collective-permute-start | bytes 1572872 | tf_op jit(solution)/shard_map/ppermute | solution.py:18
  4.2 9.2 %collective-permute-start.8 = (bf16[256,1024]{1,0:T(8,128)(2,1)}, bf16[256,1024]{1,0:T(8,128)(2,1)}, u32[]{:S(2)}, u32[]{:S(2)}) collective-permute-start(bf16[256,1024]{1,0:T(8,128)(2,1)} %get-tuple-element.28), channel_id=1, source_target_pairs={{16,20}} | collective-permute-start | bytes 1572872 | tf_op jit(solution)/shard_map/ppermute | solution.py:18
  5.7 7.7 %collective-permute-start.7 = (bf16[256,1024]{1,0:T(8,128)(2,1)S(1)}, bf16[256,1024]{1,0:T(8,128)(2,1)}, u32[]{:S(2)}, u32[]{:S(2)}) collective-permute-start(bf16[256,1024]{1,0:T(8,128)(2,1)S(1)} %get-tuple-element.29), channel_id=1, source_target_pairs={{16,22}} | collective-permute-start | bytes 1572872 | tf_op jit(solution)/shard_map/ppermute | solution.py:18
  8.1 11.0 %copy-start.5 = (bf16[1,32,1024]{2,1,0:T(8,128)(2,1)}, bf16[1,32,1024]{2,1,0:T(8,128)(2,1)S(1)}, u32[]{:S(2)}) copy-start(bf16[1,32,1024]{2,1,0:T(8,128)(2,1)S(1)} %get-tuple-element.36) | copy-start | bytes 196612
  8.1 14.2 %copy-start.6 = (bf16[1,32,1024]{2,1,0:T(8,128)(2,1)}, bf16[1,32,1024]{2,1,0:T(8,128)(2,1)S(1)}, u32[]{:S(2)}) copy-start(bf16[1,32,1024]{2,1,0:T(8,128)(2,1)S(1)} %get-tuple-element.37) | copy-start | bytes 196612
  8.1 8.1 %collective-permute-start.1 = (bf16[2,32,1024]{2,1,0:T(8,128)(2,1)S(1)}, bf16[2,32,1024]{2,1,0:T(8,128)(2,1)S(1)}, u32[]{:S(2)}, u32[]{:S(2)}) collective-permute-start(bf16[2,32,1024]{2,1,0:T(8,128)(2,1)S(1)} %pad_maximum_fusion.5), channel_id=1, source_target_pairs={{0,8},{1,9},{2,10},{3,11},{4,12},{5,13},{6,14},{7,15},{8,0},{9,1},... | collective-permute-start | bytes 393224 | tf_op jit(solution)/shard_map/ppermute | solution.py:18
  11.4 6.1 %collective-permute-start.2 = (bf16[2,32,1024]{2,1,0:T(8,128)(2,1)S(1)}, bf16[2,32,1024]{2,1,0:T(8,128)(2,1)S(1)}, u32[]{:S(2)}, u32[]{:S(2)}) collective-permute-start(bf16[2,32,1024]{2,1,0:T(8,128)(2,1)S(1)} %pad_maximum_fusion.7), channel_id=1, source_target_pairs={{16,24},{17,25},{18,26},{19,27},{20,28},{21,29},{22,30},{23,31},{2... | collective-permute-start | bytes 393224 | tf_op jit(solution)/shard_map/ppermute | solution.py:18
  14.7 13.9 %collective-permute-start.10 = (bf16[256,1024]{1,0:T(8,128)(2,1)S(1)}, bf16[256,1024]{1,0:T(8,128)(2,1)}, u32[]{:S(2)}, u32[]{:S(2)}) collective-permute-start(bf16[256,1024]{1,0:T(8,128)(2,1)S(1)} %fusion.1), channel_id=1, source_target_pairs={{16,24},{18,26},{20,28},{22,30}} | collective-permute-start | bytes 1572872 | tf_op jit(solution)/shard_map/ppermute | solution.py:18
  19.0 8.1 %collective-permute-start.4 = (bf16[4,32,1024]{2,1,0:T(8,128)(2,1)}, bf16[4,32,1024]{2,1,0:T(8,128)(2,1)S(1)}, u32[]{:S(2)}, u32[]{:S(2)}) collective-permute-start(bf16[4,32,1024]{2,1,0:T(8,128)(2,1)} %pad_maximum_fusion.4), channel_id=1, source_target_pairs={{16,18},{17,19},{18,16},{19,17},{20,22},{21,23},{22,20},{23,21},{2... | collective-permute-start | bytes 786440 | tf_op jit(solution)/shard_map/ppermute | solution.py:18
  22.3 5.5 %collective-permute-start.3 = (bf16[4,32,1024]{2,1,0:T(8,128)(2,1)}, bf16[4,32,1024]{2,1,0:T(8,128)(2,1)S(1)}, u32[]{:S(2)}, u32[]{:S(2)}) collective-permute-start(bf16[4,32,1024]{2,1,0:T(8,128)(2,1)} %pad_maximum_fusion.3), channel_id=1, source_target_pairs={{0,4},{1,5},{2,6},{3,7},{4,0},{5,1},{6,2},{7,3},{8,12},{9,13},{10,... | collective-permute-start | bytes 786440 | tf_op jit(solution)/shard_map/ppermute | solution.py:18
  27.2 0.7 copy-start.1
  27.9 0.7 copy-start.3
  28.7 12.2 %copy-start.4 = (bf16[4,32,1024]{2,1,0:T(8,128)(2,1)S(1)}, bf16[4,32,1024]{2,1,0:T(8,128)(2,1)}, u32[]{:S(2)}) copy-start(bf16[4,32,1024]{2,1,0:T(8,128)(2,1)} %copy-done.3) | copy-start | bytes 786436
  28.7 13.1 %copy-start.2 = (bf16[4,32,1024]{2,1,0:T(8,128)(2,1)S(1)}, bf16[4,32,1024]{2,1,0:T(8,128)(2,1)}, u32[]{:S(2)}) copy-start(bf16[4,32,1024]{2,1,0:T(8,128)(2,1)} %copy-done.1) | copy-start | bytes 786436
  28.7 108.2 %all-to-all-start = ((bf16[32,32,2048]{2,1,0:T(8,128)(2,1)}), bf16[32,32,2048]{2,1,0:T(8,128)(2,1)}, u32[]{:S(2)}, u32[]{:S(2)}) async-start(bf16[32,32,2048]{2,1,0:T(8,128)(2,1)} %bitcast.32), calls=%async_computation | async-start | bytes 8388608 | tf_op jit(solution)/shard_map/all_to_all | solution.py:235
  42.7 73.1 %copy-start = (bf16[2,1024,1024]{2,1,0:T(8,128)(2,1)S(1)}, bf16[2,1024,1024]{2,1,0:T(8,128)(2,1)}, u32[]{:S(2)}) copy-start(bf16[2,1024,1024]{2,1,0:T(8,128)(2,1)} %d_ref.1) | copy-start | bytes 12582916
  42.7 37.8 %collective-permute-start.6 = (bf16[8,32,1024]{2,1,0:T(8,128)(2,1)S(1)}, bf16[8,32,1024]{2,1,0:T(8,128)(2,1)S(1)}, u32[]{:S(2)}, u32[]{:S(2)}) collective-permute-start(bf16[8,32,1024]{2,1,0:T(8,128)(2,1)S(1)} %pad_maximum_fusion.2), channel_id=1, source_target_pairs={{16,20},{17,21},{18,22},{19,23},{20,16},{21,17},{22,18},{23,19},{2... | collective-permute-start | bytes 1572872 | tf_op jit(solution)/shard_map/ppermute | solution.py:18
  45.1 35.8 %collective-permute-start.5 = (bf16[8,32,1024]{2,1,0:T(8,128)(2,1)S(1)}, bf16[8,32,1024]{2,1,0:T(8,128)(2,1)S(1)}, u32[]{:S(2)}, u32[]{:S(2)}) collective-permute-start(bf16[8,32,1024]{2,1,0:T(8,128)(2,1)S(1)} %pad_maximum_fusion.1), channel_id=1, source_target_pairs={{0,2},{1,3},{2,0},{3,1},{4,6},{5,7},{6,4},{7,5},{8,10},{9,11},{10,... | collective-permute-start | bytes 1572872 | tf_op jit(solution)/shard_map/ppermute | solution.py:18
  46.4 34.6 %collective-permute-start.13 = (bf16[1,256,1024]{2,1,0:T(8,128)(2,1)S(1)}, bf16[1,256,1024]{2,1,0:T(8,128)(2,1)S(1)}, u32[]{:S(2)}, u32[]{:S(2)}) collective-permute-start(bf16[1,256,1024]{2,1,0:T(8,128)(2,1)S(1)} %select_bitcast_fusion), channel_id=1, source_target_pairs={{16,20},{18,22},{20,16},{22,18},{24,28},{26,30},{28,24},{30,26}} | collective-permute-start | bytes 1572872 | tf_op jit(solution)/shard_map/ppermute | solution.py:18
  47.1 33.9 %collective-permute-start.12 = (bf16[1,256,1024]{2,1,0:T(8,128)(2,1)S(1)}, bf16[1,256,1024]{2,1,0:T(8,128)(2,1)S(1)}, u32[]{:S(2)}, u32[]{:S(2)}) collective-permute-start(bf16[1,256,1024]{2,1,0:T(8,128)(2,1)S(1)} %select_bitcast_fusion), channel_id=1, source_target_pairs={{16,18},{18,16},{20,22},{22,20},{24,26},{26,24},{28,30},{30,28}} | collective-permute-start | bytes 1572872 | tf_op jit(solution)/shard_map/ppermute | solution.py:18
  47.8 33.2 %collective-permute-start.11 = (bf16[1,256,1024]{2,1,0:T(8,128)(2,1)S(1)}, bf16[1,256,1024]{2,1,0:T(8,128)(2,1)S(1)}, u32[]{:S(2)}, u32[]{:S(2)}) collective-permute-start(bf16[1,256,1024]{2,1,0:T(8,128)(2,1)S(1)} %select_bitcast_fusion), channel_id=1, source_target_pairs={{16,22},{18,20},{20,18},{22,16},{24,30},{26,28},{28,26},{30,24}} | collective-permute-start | bytes 1572872 | tf_op jit(solution)/shard_map/ppermute | solution.py:18
  81.2 34.6 %collective-permute-start.16 = (bf16[4,256,1024]{2,1,0:T(8,128)(2,1)S(1)}, bf16[4,256,1024]{2,1,0:T(8,128)(2,1)S(1)}, u32[]{:S(2)}, u32[]{:S(2)}) collective-permute-start(bf16[4,256,1024]{2,1,0:T(8,128)(2,1)S(1)} %pad_maximum_fusion.a2), channel_id=1, source_target_pairs={{16,17},{18,19},{20,21},{22,23},{24,25},{26,27},{28,29},{30,31}} | collective-permute-start | bytes 6291464 | tf_op jit(solution)/shard_map/ppermute | solution.py:18
  82.7 31.6 %collective-permute-start.15 = (bf16[16,32,1024]{2,1,0:T(8,128)(2,1)S(1)}, bf16[16,32,1024]{2,1,0:T(8,128)(2,1)S(1)}, u32[]{:S(2)}, u32[]{:S(2)}) collective-permute-start(bf16[16,32,1024]{2,1,0:T(8,128)(2,1)S(1)} %constant_dynamic-update-slice_fusion.5.a1), channel_id=1, source_target_pairs={{16,17},{17,16},{18,19},{19,18},{20,21},{21,20},{22,23},{23,22},{2... | collective-permute-start | bytes 3145736 | tf_op jit(solution)/shard_map/ppermute | solution.py:18
  111.4 4.4 %collective-permute-start.14 = (bf16[16,32,1024]{2,1,0:T(8,128)(2,1)S(1)}, bf16[16,32,1024]{2,1,0:T(8,128)(2,1)S(1)}, u32[]{:S(2)}, u32[]{:S(2)}) collective-permute-start(bf16[16,32,1024]{2,1,0:T(8,128)(2,1)S(1)} %constant_dynamic-update-slice_fusion.a0), channel_id=1, source_target_pairs={{0,1},{1,0},{2,3},{3,2},{4,5},{5,4},{6,7},{7,6},{8,9},{9,8},{10,11... | collective-permute-start | bytes 3145736 | tf_op jit(solution)/shard_map/ppermute | solution.py:18
